TPU v7x, 256 devices: a whole 4x4x8 slice. The times are simulated.
256 devices in a mesh: rows: 4 (over y), half: 2 (over core), obs: 32 (over z, x).
Axes of the slice: x: 4, y: 4, z: 8, core: 2. Of those that a mesh axis runs over, the one named last changes fastest.
Arguments:
- ens_state: bfloat16 [2, 8192, 256], P('half', ('rows', 'obs')), may hold values from -6 to 6
- state_pos: bfloat16 [8192], P(('rows', 'obs')), may hold values from 0 to 1
- obs_ens: bfloat16 [2, 2, 65536, 256], P(None, 'half', ('rows', 'obs')), may hold values from -6 to 6
- obs_pos: bfloat16 [2, 65536], P(None, ('rows', 'obs')), may hold values from 0 to 1
- innov_weight: bfloat16 [2, 2, 65536, 256], P(None, 'half', ('rows', 'obs')), may hold values from -0.875 to 0.875
- block_rows: int32 [2, 512, 16], replicated, may hold values from 0 to 63, as said below
Outputs:
- increment: float32 [2, 8192, 256], P('half', ('rows', 'obs'))
Inputs may be any that keep to these rules, and one draw needn't show every extreme that they name: `block_rows`: each row lists 16 different state blocks. Counting state blocks in aligned ranges of 16, an observation block names at most 8 blocks of one range, and in every aligned group of 16 observation blocks some range is named exactly 8 times by each block of the group.
All inputs are finite; a program needn't handle non-finite values.
Results may differ from a plain program's by a relative error of at most 0.0029.
Values may be sent and summed in bfloat16 or wider, within the bound.
No kernel may reach another device: no remote copies, remote signals or barrier semaphores. Data moves between devices by JAX's collectives and lax.ppermute only.
A program may use at most 64 MiB of HBM per device.

v0:
```python
import functools
import math

import jax
import jax.numpy as jnp
from jax import lax
from jax.experimental import pallas as pl
from jax.experimental.pallas import tpu as pltpu
from jax.sharding import PartitionSpec as P


BATCHES = 2
ROWS, HALVES, OBS = 4, 2, 32
NX, NZ = 4, 8
EDGE = 128
SHARD = 64
MEMBERS = 256
RANGE_BLOCKS = 16
SPAN = 4
NAMED = 16
OBS_ROWS = SPAN * EDGE
PAD = 16
Z_ORDER = (0, 4, 2, 6, 1, 5, 3, 7)

GROUP = 8
SOURCES = ((0, 2, 0), (3, 2, 0), (1, 2, 0), (2, 1, 0), (2, 1, 1))
PICKS = 8 * GROUP + NAMED
VISITS = 8
BLOCKS = len(SOURCES) * PICKS
TOTALS = BLOCKS + len(SOURCES) * VISITS + 8
LIVE = math.log2(1.0 / (MEMBERS - 1))
STRETCH = 2.0 * math.sqrt(math.log2(math.e))

VMEM = pl.BlockSpec(memory_space=pltpu.VMEM)
SMEM = pl.BlockSpec(memory_space=pltpu.SMEM)


def flip(value):
    return lax.ppermute(value, "half", [(0, 1), (1, 0)])


def along_rows(value, step):
    return lax.ppermute(value, "rows", [(s, (s + step) % ROWS) for s in range(ROWS)])


def along_rows_flip(value, step):
    pairs = [
        (r * HALVES + h, ((r + step) % ROWS) * HALVES + 1 - h)
        for r in range(ROWS)
        for h in range(HALVES)
    ]
    return lax.ppermute(value, ("rows", "half"), pairs)


def swap_z(value, mask):
    pairs = [(z * NX + x, (z ^ mask) * NX + x) for z in range(NZ) for x in range(NX)]
    return lax.ppermute(value, "obs", pairs)


def swap_z_flip(value, mask):
    pairs = [
        (h * OBS + z * NX + x, (1 - h) * OBS + (z ^ mask) * NX + x)
        for h in range(HALVES)
        for z in range(NZ)
        for x in range(NX)
    ]
    return lax.ppermute(value, ("half", "obs"), pairs)


def along_x(value, step):
    pairs = [(z * NX + x, z * NX + (x + step) % NX) for z in range(NZ) for x in range(NX)]
    return lax.ppermute(value, "obs", pairs)


def lists_kernel(named_ref, lists):
    row, column = lax.axis_index("rows"), lax.axis_index("obs")
    first = row * RANGE_BLOCKS
    for s, (turn, batches, batch) in enumerate(SOURCES):
        owner = jnp.bitwise_and(row + turn, ROWS - 1) * OBS + column

        def fill(i, visits, s=s, batch=batch, owner=owner):
            t = batch + lax.shift_right_logical(i, 2)
            place = owner * SPAN + jnp.bitwise_and(i, SPAN - 1)
            start = s * PICKS + visits * GROUP
            for k in range(GROUP):
                lists[start + k] = RANGE_BLOCKS
            write = start
            for e in range(NAMED):
                relative = named_ref[t, e, place] - first
                inside = jnp.bitwise_and(relative, -RANGE_BLOCKS) == 0
                lists[write] = jnp.where(inside, relative, RANGE_BLOCKS)
                write = write + inside.astype(jnp.int32)
            lists[BLOCKS + s * VISITS + visits] = i
            return visits + (write > start).astype(jnp.int32)

        lists[TOTALS + s] = lax.fori_loop(0, batches * SPAN, fill, jnp.int32(0))


def make_lists(named):
    return pl.pallas_call(
        lists_kernel,
        out_shape=jax.ShapeDtypeStruct((TOTALS + 8,), jnp.int32),
        in_specs=[SMEM],
        out_specs=SMEM,
        compiler_params=pltpu.CompilerParams(vmem_limit_bytes=1 << 20),
        cost_estimate=pl.CostEstimate(flops=4_000_000, transcendentals=0, bytes_accessed=4_000_000),
        name="lists",
    )(named)


def visit(s, obs, weights, places, state, spot, acc, tiles, lists):
    total = lists[TOTALS + s]

    def make_tiles(g):
        i = lists[BLOCKS + s * VISITS + g]
        here = obs(i)
        place = places[pl.ds(i, 1), :]
        chosen = [lists[s * PICKS + g * GROUP + k] for k in range(GROUP)]
        gathered = jnp.concatenate(
            [state[pl.ds(2 * b, 2)].reshape(EDGE, MEMBERS) for b in chosen], axis=0
        )
        products = lax.dot_general(
            gathered, here, (((1,), (1,)), ((), ())), preferred_element_type=jnp.float32
        )
        for k, b in enumerate(chosen):
            d = spot[pl.ds(2 * b, 2)].reshape(EDGE, EDGE) - place
            damped = products[k * EDGE : (k + 1) * EDGE] * jnp.exp2(LIVE - d * d)
            tiles[k * EDGE : (k + 1) * EDGE] = damped.astype(jnp.bfloat16)

    def add_tiles(g):
        weight = weights(lists[BLOCKS + s * VISITS + g])
        chosen = [lists[s * PICKS + g * GROUP + k] for k in range(GROUP)]
        added = jnp.dot(tiles[...], weight, preferred_element_type=jnp.float32)
        for k, b in enumerate(chosen):
            acc[b] += added[k * EDGE : (k + 1) * EDGE]

    @pl.when(total > 0)
    def _():
        make_tiles(0)

        def step(g, carry):
            add_tiles(g - 1)
            make_tiles(g)
            return carry

        lax.fori_loop(1, total, step, 0)
        add_tiles(total - 1)


def split(ref):
    def part(i):
        t, r = lax.shift_right_logical(i, 2), jnp.bitwise_and(i, SPAN - 1)
        return ref[t, pl.ds(pl.multiple_of(r * EDGE, EDGE), EDGE), :]

    return part


def flat(ref, start):
    def part(i):
        return ref[pl.ds(pl.multiple_of(start + i * EDGE, PAD), EDGE), :]

    return part


def spread_places(held, places, start):
    places[start : start + SPAN] = held.astype(jnp.float32)[:SPAN] * STRETCH


def near_kernel(
    lists, s0, s1, s2, s3, oo, wo, ol, wl, orr, wr, state, spot, acc, places, tiles,
):
    column = lax.axis_index("obs")
    my_z = lax.shift_right_logical(column, 2)
    my_x = jnp.bitwise_and(column, NX - 1)
    lanes = lax.broadcasted_iota(jnp.int32, (SHARD, EDGE), 1)
    sublanes = lax.broadcasted_iota(jnp.int32, (SHARD, EDGE), 0)
    same = lanes == sublanes
    ones = jnp.ones((EDGE, EDGE), jnp.bfloat16)
    for k, piece in enumerate((s0, s1, s2, s3)):
        src_x = jnp.bitwise_and(my_x + (NX - k), NX - 1)
        held = piece[NZ * SHARD : NZ * SHARD + PAD, :EDGE].astype(jnp.float32)
        spread = jnp.concatenate(
            [jnp.where(same, held[p : p + 1], 0.0) for p in range(NZ)], axis=0
        ).astype(jnp.bfloat16)
        columns = jnp.dot(spread, ones, preferred_element_type=jnp.float32) * STRETCH
        for p, mask in enumerate(Z_ORDER):
            src = (my_z ^ mask) * NX + src_x
            state[src] = piece[p * SHARD : (p + 1) * SHARD, :]
            spot[src] = columns[p * SHARD : (p + 1) * SHARD]
    state[OBS:] = jnp.zeros((2, SHARD, MEMBERS), jnp.bfloat16)
    spot[OBS:] = jnp.zeros((2, SHARD, EDGE), jnp.float32)
    acc[...] = jnp.zeros_like(acc)
    for s, (o, w) in enumerate(((oo, wo), (ol, wl), (orr, wr))):
        for t in range(BATCHES):
            spread_places(o[t, OBS_ROWS : OBS_ROWS + PAD, :EDGE], places, t * SPAN)
        visit(s, split(o), split(w), places, state, spot, acc, tiles, lists)


def near(lists, arrays):
    return pl.pallas_call(
        near_kernel,
        out_shape=(
            jax.ShapeDtypeStruct((OBS + 2, SHARD, MEMBERS), jnp.bfloat16),
            jax.ShapeDtypeStruct((OBS + 2, SHARD, EDGE), jnp.float32),
            jax.ShapeDtypeStruct((RANGE_BLOCKS + 1, EDGE, MEMBERS), jnp.float32),
        ),
        in_specs=[SMEM] + [VMEM] * 10,
        out_specs=(VMEM,) * 3,
        scratch_shapes=[
            pltpu.VMEM((8, EDGE), jnp.float32),
            pltpu.VMEM((GROUP * EDGE, EDGE), jnp.bfloat16),
        ],
        compiler_params=pltpu.CompilerParams(vmem_limit_bytes=24 << 20),
        cost_estimate=pl.CostEstimate(
            flops=4_000_000_000, transcendentals=4_000_000, bytes_accessed=8_000_000
        ),
        name="near",
    )(lists, *arrays)


def far_kernel(lists, state, spot, near_acc, left, right, out, places, tiles, acc):
    acc[...] = near_acc[...]
    for s, both in ((3, left), (4, right)):
        spread_places(both[OBS_ROWS : OBS_ROWS + PAD, :EDGE], places, 0)
        visit(
            s, flat(both, 0), flat(both, OBS_ROWS + PAD), places, state, spot, acc, tiles, lists
        )
    out[...] = acc[:RANGE_BLOCKS].reshape(RANGE_BLOCKS * EDGE, MEMBERS).astype(jnp.bfloat16)


def far(lists, state, spot, acc, arrays):
    return pl.pallas_call(
        far_kernel,
        out_shape=jax.ShapeDtypeStruct((RANGE_BLOCKS * EDGE, MEMBERS), jnp.bfloat16),
        in_specs=[SMEM] + [VMEM] * 5,
        out_specs=VMEM,
        scratch_shapes=[
            pltpu.VMEM((8, EDGE), jnp.float32),
            pltpu.VMEM((GROUP * EDGE, EDGE), jnp.bfloat16),
            pltpu.VMEM((RANGE_BLOCKS + 1, EDGE, MEMBERS), jnp.float32),
        ],
        compiler_params=pltpu.CompilerParams(vmem_limit_bytes=24 << 20),
        cost_estimate=pl.CostEstimate(
            flops=1_000_000_000, transcendentals=1_000_000, bytes_accessed=8_000_000
        ),
        name="far",
    )(lists, state, spot, acc, *arrays)


def pack_kernel(a, b, out):
    held = SHARD + PAD
    places = []
    for p in range(NZ):
        ref, q = (a, p) if p < NZ // 2 else (b, p - NZ // 2)
        out[p * SHARD : (p + 1) * SHARD] = ref[q * held : q * held + SHARD]
        places.append(ref[q * held + SHARD : (q + 1) * held].astype(jnp.float32)[:1])
    places.append(jnp.zeros((PAD - NZ, MEMBERS), jnp.float32))
    out[NZ * SHARD :] = jnp.concatenate(places, axis=0).astype(jnp.bfloat16)


def pack(a, b):
    return pl.pallas_call(
        pack_kernel,
        out_shape=jax.ShapeDtypeStruct((NZ * SHARD + PAD, MEMBERS), jnp.bfloat16),
        in_specs=[VMEM, VMEM],
        out_specs=VMEM,
        compiler_params=pltpu.CompilerParams(vmem_limit_bytes=4 << 20),
        name="pack",
    )(a, b)


def join_kernel(*refs):
    out = refs[-1]
    start = 0
    for ref in refs[:-1]:
        out[start : start + ref.shape[0]] = ref[...]
        start += ref.shape[0]


def join(*parts):
    rows = sum(part.shape[0] for part in parts)
    return pl.pallas_call(
        join_kernel,
        out_shape=jax.ShapeDtypeStruct((rows, MEMBERS), jnp.bfloat16),
        in_specs=[VMEM] * len(parts),
        out_specs=VMEM,
        compiler_params=pltpu.CompilerParams(vmem_limit_bytes=4 << 20),
        name="join",
    )(*parts)


def load_kernel(obs, places, out):
    for t in range(BATCHES):
        out[t, :OBS_ROWS] = obs[t]
        held = places[t : t + 1].astype(jnp.float32)
        rows = [held[:, r * EDGE : (r + 1) * EDGE] for r in range(SPAN)]
        rows.append(jnp.zeros((PAD - SPAN, EDGE), jnp.float32))
        out[t, OBS_ROWS:, :EDGE] = jnp.concatenate(rows, axis=0).astype(jnp.bfloat16)
        out[t, OBS_ROWS:, EDGE:] = jnp.zeros((PAD, MEMBERS - EDGE), jnp.bfloat16)


def load(obs, places):
    return pl.pallas_call(
        load_kernel,
        out_shape=jax.ShapeDtypeStruct((BATCHES, OBS_ROWS + PAD, MEMBERS), jnp.bfloat16),
        in_specs=[VMEM, VMEM],
        out_specs=VMEM,
        compiler_params=pltpu.CompilerParams(vmem_limit_bytes=8 << 20),
        name="load",
    )(obs, places)


def relay_kernel(batch, obs, weights, out):
    out[: OBS_ROWS + PAD] = obs[batch]
    out[OBS_ROWS + PAD :] = weights[batch]


def relay(batch, obs, weights):
    return pl.pallas_call(
        functools.partial(relay_kernel, batch),
        out_shape=jax.ShapeDtypeStruct((2 * OBS_ROWS + PAD, MEMBERS), jnp.bfloat16),
        in_specs=[VMEM, VMEM],
        out_specs=VMEM,
        compiler_params=pltpu.CompilerParams(vmem_limit_bytes=8 << 20),
        name="relay",
    )(obs, weights)


def local(ens_state, state_pos, obs_ens, obs_pos, innov_weight, block_rows):
    state = jnp.concatenate(
        [ens_state[0], jnp.pad(state_pos[None, :], ((0, PAD - 1), (0, MEMBERS - SHARD)))], axis=0
    )
    mine = flip(state)
    other = swap_z_flip(state, 4)
    state = join(mine, other)
    other = swap_z(state, 2)
    state = join(state, other)
    other = swap_z(state, 1)
    state = pack(state, other)
    pieces = [state]
    for k in range(1, NX):
        pieces.append(along_x(state, k))

    weight = innov_weight[:, 0]
    weight_left = along_rows(weight, 1)
    weight_right = along_rows(weight, ROWS - 1)
    obs = load(obs_ens[:, 0], obs_pos)
    obs_left = along_rows_flip(obs, 1)
    obs_right = along_rows_flip(obs, ROWS - 1)
    obs_own = flip(obs)
    far0 = relay(0, obs_left, weight_left)
    far0 = along_rows(far0, 1)
    far1 = relay(1, obs_right, weight_right)
    far1 = along_rows(far1, ROWS - 1)

    lists = make_lists(jnp.transpose(block_rows, (0, 2, 1)))
    held = near(lists, (*pieces, obs_own, weight, obs_left, weight_left, obs_right, weight_right))
    partial = far(lists, *held, (far0, far1))
    shares = lax.all_to_all(partial, "obs", 0, 0, tiled=True)
    shares = shares.reshape(OBS, SHARD, MEMBERS).astype(jnp.float32)
    return jnp.sum(shares, axis=0)[None]


def solution(mesh):
    in_specs = (
        P("half", ("rows", "obs"), None),
        P(("rows", "obs")),
        P(None, "half", ("rows", "obs"), None),
        P(None, ("rows", "obs")),
        P(None, "half", ("rows", "obs"), None),
        P(),
    )
    out_specs = P("half", ("rows", "obs"), None)
    return jax.shard_map(local, mesh=mesh, in_specs=in_specs, out_specs=out_specs, check_vma=False)
```

profile of v0, /device:TPU:1, one launch (start us, length us, event | category | flops | bytes accessed | tf_op | source)
XLA Modules:
  0.0 115.2 jit_solution(17668778868915188274)
XLA Ops:
  0.0 0.8 fusion.1
  0.8 3.2 %collective-permute-start = (bf16[80,256]{1,0:T(8,128)(2,1)S(1)}, bf16[80,256]{1,0:T(8,128)(2,1)S(1)}, u32[]{:S(2)}, u32[]{:S(2)}) collective-permute-start(bf16[80,256]{1,0:T(8,128)(2,1)S(1)} %fusion.1), channel_id=1, source_target_pairs={{0,32},{32,0},{1,33},{33,1},{2,34},{34,2},{3,35},{35,3},{4,36},{36... | collective-permute-start | bytes 122888 | tf_op jit(solution)/shard_map/ppermute | solution.py:39
  4.0 5.2 %collective-permute-start.1 = (bf16[80,256]{1,0:T(8,128)(2,1)S(1)}, bf16[80,256]{1,0:T(8,128)(2,1)S(1)}, u32[]{:S(2)}, u32[]{:S(2)}) collective-permute-start(bf16[80,256]{1,0:T(8,128)(2,1)S(1)} %fusion.1), channel_id=1, source_target_pairs={{0,48},{1,49},{2,50},{3,51},{4,52},{5,53},{6,54},{7,55},{8,56},{9,... | collective-permute-start | bytes 122888 | tf_op jit(solution)/shard_map/ppermute | solution.py:67
  9.2 0.0 collective-permute-done.refs_0_
  9.2 2.2 %collective-permute-done.1.refs_1_ = bf16[80,256]{1,0:T(8,128)(2,1)S(1)} collective-permute-done((bf16[80,256]{1,0:T(8,128)(2,1)S(1)}, bf16[80,256]{1,0:T(8,128)(2,1)S(1)}, u32[]{:S(2)}, u32[]{:S(2)}) %collective-permute-start.1) | collective-permute-done | bytes 40992 | tf_op jit(solution)/shard_map/ppermute | solution.py:67
  11.3 2.2 %collective-permute-start.2 = (bf16[160,256]{1,0:T(8,128)(2,1)S(1)}, bf16[160,256]{1,0:T(8,128)(2,1)S(1)}, u32[]{:S(2)}, u32[]{:S(2)}) collective-permute-start(bf16[160,256]{1,0:T(8,128)(2,1)S(1)} %join.2.refs_0_), channel_id=1, source_target_pairs={{0,8},{1,9},{2,10},{3,11},{4,12},{5,13},{6,14},{7,15},{8,0},{9,1},... | collective-permute-start | bytes 245768 | tf_op jit(solution)/shard_map/ppermute | solution.py:57
  13.5 4.6 %collective-permute-done.2.refs_1_ = bf16[160,256]{1,0:T(8,128)(2,1)S(1)} collective-permute-done((bf16[160,256]{1,0:T(8,128)(2,1)S(1)}, bf16[160,256]{1,0:T(8,128)(2,1)S(1)}, u32[]{:S(2)}, u32[]{:S(2)}) %collective-permute-start.2) | collective-permute-done | bytes 81952 | tf_op jit(solution)/shard_map/ppermute | solution.py:57
  18.1 0.1 collective-permute-start.3
  18.2 0.0 copy-start
  18.2 1.0 copy-done
  19.2 0.0 copy-start.2
  19.2 0.7 copy-done.2
  20.0 0.0 copy-start.1
  20.0 0.0 copy-start.3
  20.0 2.1 %collective-permute-start.8 = (bf16[2,528,256]{2,1,0:T(8,128)(2,1)S(1)}, bf16[2,528,256]{2,1,0:T(8,128)(2,1)S(1)}, u32[]{:S(2)}, u32[]{:S(2)}) collective-permute-start(bf16[2,528,256]{2,1,0:T(8,128)(2,1)S(1)} %load.1), channel_id=1, source_target_pairs={{0,96},{32,64},{64,160},{96,128},{128,224},{160,192},{192,32},{224... | collective-permute-start | bytes 1622024 | tf_op jit(solution)/shard_map/ppermute | solution.py:52
  22.1 1.4 %collective-permute-start.11 = (bf16[2,512,256]{2,1,0:T(8,128)(2,1)}, bf16[2,512,256]{2,1,0:T(8,128)(2,1)S(1)}, u32[]{:S(2)}, u32[]{:S(2)}) collective-permute-start(bf16[2,512,256]{2,1,0:T(8,128)(2,1)} %bitcast.10), channel_id=1, source_target_pairs={{0,192},{64,0},{128,64},{192,128},{1,193},{65,1},{129,65},{193,129... | collective-permute-start | bytes 1572872 | tf_op jit(solution)/shard_map/ppermute | solution.py:43
  23.5 0.1 collective-permute-start.9
  23.6 3.3 %collective-permute-start.10 = (bf16[2,528,256]{2,1,0:T(8,128)(2,1)S(1)}, bf16[2,528,256]{2,1,0:T(8,128)(2,1)S(1)}, u32[]{:S(2)}, u32[]{:S(2)}) collective-permute-start(bf16[2,528,256]{2,1,0:T(8,128)(2,1)S(1)} %load.1), channel_id=1, source_target_pairs={{0,224},{32,192},{64,32},{96,0},{128,96},{160,64},{192,160},{224,1... | collective-permute-start | bytes 1622024 | tf_op jit(solution)/shard_map/ppermute | solution.py:52
  26.9 0.0 collective-permute-done.3.b
  26.9 0.0 collective-permute-start.7
  26.9 9.3 %collective-permute-done.11.wr.weights = bf16[2,512,256]{2,1,0:T(8,128)(2,1)S(1)} collective-permute-done((bf16[2,512,256]{2,1,0:T(8,128)(2,1)}, bf16[2,512,256]{2,1,0:T(8,128)(2,1)S(1)}, u32[]{:S(2)}, u32[]{:S(2)}) %collective-permute-start.11) | collective-permute-done | bytes 524320 | tf_op jit(solution)/shard_map/ppermute | solution.py:43
  36.1 1.2 %collective-permute-start.4 = (bf16[528,256]{1,0:T(8,128)(2,1)S(1)}, bf16[528,256]{1,0:T(8,128)(2,1)S(1)}, u32[]{:S(2)}, u32[]{:S(2)}) collective-permute-start(bf16[528,256]{1,0:T(8,128)(2,1)S(1)} %pack.1.s0), channel_id=1, source_target_pairs={{0,1},{1,2},{2,3},{3,0},{4,5},{5,6},{6,7},{7,4},{8,9},{9,10},{10,1... | collective-permute-start | bytes 811016 | tf_op jit(solution)/shard_map/ppermute | solution.py:72
  37.4 9.8 %collective-permute-done.9.wl.weights = bf16[2,512,256]{2,1,0:T(8,128)(2,1)S(1)} collective-permute-done((bf16[2,512,256]{2,1,0:T(8,128)(2,1)}, bf16[2,512,256]{2,1,0:T(8,128)(2,1)S(1)}, u32[]{:S(2)}, u32[]{:S(2)}) %collective-permute-start.9) | collective-permute-done | bytes 524320 | tf_op jit(solution)/shard_map/ppermute | solution.py:43
  47.2 2.7 %collective-permute-start.5 = (bf16[528,256]{1,0:T(8,128)(2,1)S(1)}, bf16[528,256]{1,0:T(8,128)(2,1)S(1)}, u32[]{:S(2)}, u32[]{:S(2)}) collective-permute-start(bf16[528,256]{1,0:T(8,128)(2,1)S(1)} %pack.1.s0), channel_id=1, source_target_pairs={{0,2},{1,3},{2,0},{3,1},{4,6},{5,7},{6,4},{7,5},{8,10},{9,11},{10,... | collective-permute-start | bytes 811016 | tf_op jit(solution)/shard_map/ppermute | solution.py:72
  49.9 0.0 collective-permute-done.8.ol.obs
  49.9 0.9 collective-permute-start.6
  50.8 0.0 collective-permute-done.10.orr.obs
  50.8 0.3 collective-permute-start.12
  51.2 0.0 collective-permute-done.7.oo
  51.2 2.5 %collective-permute-start.13 = (bf16[1040,256]{1,0:T(8,128)(2,1)S(1)}, bf16[1040,256]{1,0:T(8,128)(2,1)S(1)}, u32[]{:S(2)}, u32[]{:S(2)}) collective-permute-start(bf16[1040,256]{1,0:T(8,128)(2,1)S(1)} %relay.3), channel_id=1, source_target_pairs={{0,192},{64,0},{128,64},{192,128},{1,193},{65,1},{129,65},{193,129... | collective-permute-start | bytes 1597448 | tf_op jit(solution)/shard_map/ppermute | solution.py:43
  53.7 0.0 copy-done.1
  53.7 4.5 %lists.1 = s32[456]{0:T(512)S(1)} custom-call(s32[2,16,512]{2,1,0:T(8,128)S(1)} %bitcast.9), custom_call_target="tpu_custom_call" | custom-call | flops 4000000 | bytes 4000000 | tf_op jit(solution)/shard_map/lists/pallas_call | solution.py:100
  58.2 0.0 collective-permute-done.4.s1
  58.3 0.0 collective-permute-done.5.s2
  58.3 3.7 %collective-permute-done.6.s3 = bf16[528,256]{1,0:T(8,128)(2,1)S(1)} collective-permute-done((bf16[528,256]{1,0:T(8,128)(2,1)S(1)}, bf16[528,256]{1,0:T(8,128)(2,1)S(1)}, u32[]{:S(2)}, u32[]{:S(2)}) %collective-permute-start.6) | collective-permute-done | bytes 270368 | tf_op jit(solution)/shard_map/ppermute | solution.py:72
  61.9 0.0 copy-done.3
  61.9 11.3 %near.1 = (bf16[34,64,256]{2,1,0:T(8,128)(2,1)S(1)}, f32[34,64,128]{2,1,0:T(8,128)S(1)}, f32[17,128,256]{2,1,0:T(8,128)S(1)}) custom-call(s32[456]{0:T(512)S(1)} %lists.1, bf16[528,256]{1,0:T(8,128)(2,1)S(1)} %pack.1.s0, bf16[528,256]{1,0:T(8,128)(2,1)S(1)} %collective-permute-done.4.s1, bf16[528,256]{1,0:T(8,128)(2,1)S(1)} %collective-permute-done.5.s2, ...), custom_call_target="tpu_custom_call" | custom-call | flops 4000000000 | bytes 8000000 | tf_op jit(solution)/shard_map/near/pallas_call | solution.py:200
  73.3 0.0 collective-permute-done.12.left
  73.3 0.0 collective-permute-done.13.right
  73.3 3.8 %far.1 = bf16[2048,256]{1,0:T(8,128)(2,1)S(1)} custom-call(s32[456]{0:T(512)S(1)} %lists.1, bf16[34,64,256]{2,1,0:T(8,128)(2,1)S(1)} %get-tuple-element.8.state, f32[34,64,128]{2,1,0:T(8,128)S(1)} %get-tuple-element.9.spot, f32[17,128,256]{2,1,0:T(8,128)S(1)} %get-tuple-element.10.near_acc, bf16[1040,256]{1,0:T(8,128)(2,1)S(1)} %collective-permute-done.12.left, ...), custom_call_target="tpu_custom_call" | custom-call | flops 1000000000 | bytes 8000000 | tf_op jit(solution)/shard_map/far/pallas_call | solution.py:232
  77.1 37.3 %all_to_all.9 = bf16[32,64,256]{2,1,0:T(8,128)(2,1)S(1)} all-to-all(bf16[32,64,256]{2,1,0:T(8,128)(2,1)S(1)} %bitcast.7), channel_id=1, replica_groups=mesh['rows'=4,'half'=2,'obs'=32] {'obs'}, dimensions={0} | all-to-all | bytes 2097152 | tf_op jit(solution)/shard_map/all_to_all | solution.py:359
  114.4 0.8 convert_reduce_fusion
  (6 shorter events, 0.2 us)
Async XLA Ops:
  0.8 8.4 %collective-permute-start = (bf16[80,256]{1,0:T(8,128)(2,1)S(1)}, bf16[80,256]{1,0:T(8,128)(2,1)S(1)}, u32[]{:S(2)}, u32[]{:S(2)}) collective-permute-start(bf16[80,256]{1,0:T(8,128)(2,1)S(1)} %fusion.1), channel_id=1, source_target_pairs={{0,32},{32,0},{1,33},{33,1},{2,34},{34,2},{3,35},{35,3},{4,36},{36... | collective-permute-start | bytes 122888 | tf_op jit(solution)/shard_map/ppermute | solution.py:39
  4.0 7.3 %collective-permute-start.1 = (bf16[80,256]{1,0:T(8,128)(2,1)S(1)}, bf16[80,256]{1,0:T(8,128)(2,1)S(1)}, u32[]{:S(2)}, u32[]{:S(2)}) collective-permute-start(bf16[80,256]{1,0:T(8,128)(2,1)S(1)} %fusion.1), channel_id=1, source_target_pairs={{0,48},{1,49},{2,50},{3,51},{4,52},{5,53},{6,54},{7,55},{8,56},{9,... | collective-permute-start | bytes 122888 | tf_op jit(solution)/shard_map/ppermute | solution.py:67
  11.3 6.7 %collective-permute-start.2 = (bf16[160,256]{1,0:T(8,128)(2,1)S(1)}, bf16[160,256]{1,0:T(8,128)(2,1)S(1)}, u32[]{:S(2)}, u32[]{:S(2)}) collective-permute-start(bf16[160,256]{1,0:T(8,128)(2,1)S(1)} %join.2.refs_0_), channel_id=1, source_target_pairs={{0,8},{1,9},{2,10},{3,11},{4,12},{5,13},{6,14},{7,15},{8,0},{9,1},... | collective-permute-start | bytes 245768 | tf_op jit(solution)/shard_map/ppermute | solution.py:57
  18.1 8.8 %collective-permute-start.3 = (bf16[320,256]{1,0:T(8,128)(2,1)S(1)}, bf16[320,256]{1,0:T(8,128)(2,1)S(1)}, u32[]{:S(2)}, u32[]{:S(2)}) collective-permute-start(bf16[320,256]{1,0:T(8,128)(2,1)S(1)} %join.3.a), channel_id=1, source_target_pairs={{0,4},{1,5},{2,6},{3,7},{4,0},{5,1},{6,2},{7,3},{8,12},{9,13},{10,... | collective-permute-start | bytes 491528 | tf_op jit(solution)/shard_map/ppermute | solution.py:57
  18.2 1.0 copy-start
  19.2 0.7 copy-start.2
  20.0 33.8 %copy-start.1 = (s32[2,512,16]{1,2,0:T(8,128)S(1)}, s32[2,512,16]{1,2,0:T(8,128)}, u32[]{:S(2)}) copy-start(s32[2,512,16]{1,2,0:T(8,128)} %param.11) | copy-start | bytes 196612
  20.0 42.0 %copy-start.3 = (bf16[2,1,512,256]{3,2,1,0:T(8,128)(2,1)S(1)}, bf16[2,1,512,256]{3,2,1,0:T(8,128)(2,1)}, u32[]{:S(2)}) copy-start(bf16[2,1,512,256]{3,2,1,0:T(8,128)(2,1)} %param.10) | copy-start | bytes 1572868
  20.0 29.9 %collective-permute-start.8 = (bf16[2,528,256]{2,1,0:T(8,128)(2,1)S(1)}, bf16[2,528,256]{2,1,0:T(8,128)(2,1)S(1)}, u32[]{:S(2)}, u32[]{:S(2)}) collective-permute-start(bf16[2,528,256]{2,1,0:T(8,128)(2,1)S(1)} %load.1), channel_id=1, source_target_pairs={{0,96},{32,64},{64,160},{96,128},{128,224},{160,192},{192,32},{224... | collective-permute-start | bytes 1622024 | tf_op jit(solution)/shard_map/ppermute | solution.py:52
  22.1 14.1 %collective-permute-start.11 = (bf16[2,512,256]{2,1,0:T(8,128)(2,1)}, bf16[2,512,256]{2,1,0:T(8,128)(2,1)S(1)}, u32[]{:S(2)}, u32[]{:S(2)}) collective-permute-start(bf16[2,512,256]{2,1,0:T(8,128)(2,1)} %bitcast.10), channel_id=1, source_target_pairs={{0,192},{64,0},{128,64},{192,128},{1,193},{65,1},{129,65},{193,129... | collective-permute-start | bytes 1572872 | tf_op jit(solution)/shard_map/ppermute | solution.py:43
  23.5 23.7 %collective-permute-start.9 = (bf16[2,512,256]{2,1,0:T(8,128)(2,1)}, bf16[2,512,256]{2,1,0:T(8,128)(2,1)S(1)}, u32[]{:S(2)}, u32[]{:S(2)}) collective-permute-start(bf16[2,512,256]{2,1,0:T(8,128)(2,1)} %bitcast.11), channel_id=1, source_target_pairs={{0,64},{64,128},{128,192},{192,0},{1,65},{65,129},{129,193},{193,1... | collective-permute-start | bytes 1572872 | tf_op jit(solution)/shard_map/ppermute | solution.py:43
  23.6 27.3 %collective-permute-start.10 = (bf16[2,528,256]{2,1,0:T(8,128)(2,1)S(1)}, bf16[2,528,256]{2,1,0:T(8,128)(2,1)S(1)}, u32[]{:S(2)}, u32[]{:S(2)}) collective-permute-start(bf16[2,528,256]{2,1,0:T(8,128)(2,1)S(1)} %load.1), channel_id=1, source_target_pairs={{0,224},{32,192},{64,32},{96,0},{128,96},{160,64},{192,160},{224,1... | collective-permute-start | bytes 1622024 | tf_op jit(solution)/shard_map/ppermute | solution.py:52
  26.9 24.4 %collective-permute-start.7 = (bf16[2,528,256]{2,1,0:T(8,128)(2,1)S(1)}, bf16[2,528,256]{2,1,0:T(8,128)(2,1)S(1)}, u32[]{:S(2)}, u32[]{:S(2)}) collective-permute-start(bf16[2,528,256]{2,1,0:T(8,128)(2,1)S(1)} %load.1), channel_id=1, source_target_pairs={{0,32},{32,0},{1,33},{33,1},{2,34},{34,2},{3,35},{35,3},{4,36},{36... | collective-permute-start | bytes 1622024 | tf_op jit(solution)/shard_map/ppermute | solution.py:39
  36.1 22.1 %collective-permute-start.4 = (bf16[528,256]{1,0:T(8,128)(2,1)S(1)}, bf16[528,256]{1,0:T(8,128)(2,1)S(1)}, u32[]{:S(2)}, u32[]{:S(2)}) collective-permute-start(bf16[528,256]{1,0:T(8,128)(2,1)S(1)} %pack.1.s0), channel_id=1, source_target_pairs={{0,1},{1,2},{2,3},{3,0},{4,5},{5,6},{6,7},{7,4},{8,9},{9,10},{10,1... | collective-permute-start | bytes 811016 | tf_op jit(solution)/shard_map/ppermute | solution.py:72
  47.2 11.1 %collective-permute-start.5 = (bf16[528,256]{1,0:T(8,128)(2,1)S(1)}, bf16[528,256]{1,0:T(8,128)(2,1)S(1)}, u32[]{:S(2)}, u32[]{:S(2)}) collective-permute-start(bf16[528,256]{1,0:T(8,128)(2,1)S(1)} %pack.1.s0), channel_id=1, source_target_pairs={{0,2},{1,3},{2,0},{3,1},{4,6},{5,7},{6,4},{7,5},{8,10},{9,11},{10,... | collective-permute-start | bytes 811016 | tf_op jit(solution)/shard_map/ppermute | solution.py:72
  49.9 12.0 %collective-permute-start.6 = (bf16[528,256]{1,0:T(8,128)(2,1)S(1)}, bf16[528,256]{1,0:T(8,128)(2,1)S(1)}, u32[]{:S(2)}, u32[]{:S(2)}) collective-permute-start(bf16[528,256]{1,0:T(8,128)(2,1)S(1)} %pack.1.s0), channel_id=1, source_target_pairs={{0,3},{1,0},{2,1},{3,2},{4,7},{5,4},{6,5},{7,6},{8,11},{9,8},{10,9... | collective-permute-start | bytes 811016 | tf_op jit(solution)/shard_map/ppermute | solution.py:72
  50.8 22.4 %collective-permute-start.12 = (bf16[1040,256]{1,0:T(8,128)(2,1)S(1)}, bf16[1040,256]{1,0:T(8,128)(2,1)S(1)}, u32[]{:S(2)}, u32[]{:S(2)}) collective-permute-start(bf16[1040,256]{1,0:T(8,128)(2,1)S(1)} %relay.2), channel_id=1, source_target_pairs={{0,64},{64,128},{128,192},{192,0},{1,65},{65,129},{129,193},{193,1... | collective-permute-start | bytes 1597448 | tf_op jit(solution)/shard_map/ppermute | solution.py:43
  51.2 22.1 %collective-permute-start.13 = (bf16[1040,256]{1,0:T(8,128)(2,1)S(1)}, bf16[1040,256]{1,0:T(8,128)(2,1)S(1)}, u32[]{:S(2)}, u32[]{:S(2)}) collective-permute-start(bf16[1040,256]{1,0:T(8,128)(2,1)S(1)} %relay.3), channel_id=1, source_target_pairs={{0,192},{64,0},{128,64},{192,128},{1,193},{65,1},{129,65},{193,129... | collective-permute-start | bytes 1597448 | tf_op jit(solution)/shard_map/ppermute | solution.py:43
where the time goes:
time: 117 us; the launch traced here: 115 us
  blocking collectives  37.3 us (32%)
  waiting for transfers between devices  29.5 us (25%)
  starting transfers between devices  25.2 us (22%)
  Pallas kernels  19.8 us (17%)
  local copies, waits for them, and re-layouts  1.73 us (1%)
  other arithmetic  1.56 us (1%)
    all_to_all x1, blocking collectives, local(): shares = lax.all_to_all(partial, 'obs', 0, 0, tiled=True)  37.3 us
    ppermute x4, waiting for transfers between devices, along_rows(): lax.ppermute(value, 'rows', [(s, (s + step) % ROWS) for s in range(ROWS)])  19.1 us
    pallas_call x1, Pallas kernels, near(): pl.pallas_call(near_kernel, out_shape=(jax.ShapeDtypeStruct((OBS + 2, SHA...  11.3 us
    ppermute x2, starting transfers between devices, along_rows_flip(): return lax.ppermute(value, ('rows', 'half'), pairs)  5.41 us
    ppermute x1, starting transfers between devices, swap_z_flip(): return lax.ppermute(value, ('half', 'obs'), pairs)  5.18 us
    ppermute x3, starting transfers between devices, along_x(): return lax.ppermute(value, 'obs', pairs)  4.82 us
    ppermute x2, waiting for transfers between devices, swap_z(): return lax.ppermute(value, 'obs', pairs)  4.58 us
    pallas_call x1, Pallas kernels, make_lists(): pl.pallas_call(lists_kernel, out_shape=jax.ShapeDtypeStruct((TOTALS + 8,)...  4.52 us
  transfers between devices with their start and end apart: 14, of which 5 were waited for; matrix products, arithmetic and copies ran while one was open for 0% of the time, Pallas kernels for 14%

commit v1 on v0

--- a/solution.py
+++ b/solution.py
@@ -331,10 +331,10 @@
         [ens_state[0], jnp.pad(state_pos[None, :], ((0, PAD - 1), (0, MEMBERS - SHARD)))], axis=0
     )
     mine = flip(state)
-    other = swap_z_flip(state, 4)
-    state = join(mine, other)
-    other = swap_z(state, 2)
-    state = join(state, other)
+    parts = [mine]
+    for mask in (4, 2, 6):
+        parts.append(swap_z_flip(state, mask))
+    state = join(*parts)
     other = swap_z(state, 1)
     state = pack(state, other)
     pieces = [state]

time: 117 us -> 100 us (0.85)
  waiting for transfers between devices: 29.5 us -> 8.08 us
  starting transfers between devices: 25.2 us -> 31.5 us
  blocking collectives: 37.3 us -> 35.3 us
    ppermute x4, waiting for transfers between devices: 19.1 us -> 0.01 us  [along_rows(): lax.ppermute(value, 'rows', [(s, (s + step) % ROWS) for s in range(ROWS)])]
    ppermute x1 -> x3, starting transfers between devices: 5.18 us -> 11.5 us  [swap_z_flip(): return lax.ppermute(value, ('half', 'obs'), pairs)]
    ppermute x2, waiting for transfers between devices: 0.01 us -> 4 us  [along_rows_flip(): return lax.ppermute(value, ('rows', 'half'), pairs)]
    ppermute x3, waiting for transfers between devices: 3.68 us -> 0.01 us  [along_x(): return lax.ppermute(value, 'obs', pairs)]
    ppermute x2 -> x1, waiting for transfers between devices: 4.58 us -> 1.76 us  [swap_z(): return lax.ppermute(value, 'obs', pairs)]
    ppermute x4, starting transfers between devices: 4.3 us -> 7.08 us  [along_rows(): lax.ppermute(value, 'rows', [(s, (s + step) % ROWS) for s in range(ROWS)])]
    all_to_all x1, blocking collectives: 37.3 us -> 35.3 us  [local(): shares = lax.all_to_all(partial, 'obs', 0, 0, tiled=True)]
    ppermute x2, starting transfers between devices: 5.41 us -> 3.48 us  [along_rows_flip(): return lax.ppermute(value, ('rows', 'half'), pairs)]
  transfers between devices with their start and end apart: 14 -> 15, of which waited for: 5 -> 4; matrix products, arithmetic and copies ran while one was open for 0% -> 1% of each run, Pallas kernels for 14% -> 16%
where the time goes in v1:
time: 100 us; the launch traced here: 98.1 us
  blocking collectives  35.3 us (35%)
  starting transfers between devices  31.5 us (32%)
  Pallas kernels  19.8 us (20%)
  waiting for transfers between devices  8.08 us (8%)
  local copies, waits for them, and re-layouts  1.73 us (2%)
  other arithmetic  1.59 us (2%)
    all_to_all x1, blocking collectives, local(): shares = lax.all_to_all(partial, 'obs', 0, 0, tiled=True)  35.3 us
    ppermute x3, starting transfers between devices, swap_z_flip(): return lax.ppermute(value, ('half', 'obs'), pairs)  11.5 us
    pallas_call x1, Pallas kernels, near(): pl.pallas_call(near_kernel, out_shape=(jax.ShapeDtypeStruct((OBS + 2, SHA...  11.3 us
    ppermute x4, starting transfers between devices, along_rows(): lax.ppermute(value, 'rows', [(s, (s + step) % ROWS) for s in range(ROWS)])  7.08 us
    ppermute x3, starting transfers between devices, along_x(): return lax.ppermute(value, 'obs', pairs)  4.89 us
    pallas_call x1, Pallas kernels, make_lists(): pl.pallas_call(lists_kernel, out_shape=jax.ShapeDtypeStruct((TOTALS + 8,)...  4.52 us
    ppermute x2, waiting for transfers between devices, along_rows_flip(): return lax.ppermute(value, ('rows', 'half'), pairs)  4 us
    pallas_call x1, Pallas kernels, far(): pl.pallas_call(far_kernel, out_shape=jax.ShapeDtypeStruct((RANGE_BLOCKS *...  3.83 us
  transfers between devices with their start and end apart: 15, of which 4 were waited for; matrix products, arithmetic and copies ran while one was open for 1% of the time, Pallas kernels for 16%

profile of v1, /device:TPU:1, one launch (start us, length us, event | category | flops | bytes accessed | tf_op | source)
XLA Modules:
  0.0 98.1 jit_solution(1753065297324194183)
XLA Ops:
  0.0 2.1 %collective-permute-start.10 = (bf16[2,512,256]{2,1,0:T(8,128)(2,1)}, bf16[2,512,256]{2,1,0:T(8,128)(2,1)S(1)}, u32[]{:S(2)}, u32[]{:S(2)}) collective-permute-start(bf16[2,512,256]{2,1,0:T(8,128)(2,1)} %bitcast.10), channel_id=1, source_target_pairs={{0,64},{64,128},{128,192},{192,0},{1,65},{65,129},{129,193},{193,1... | collective-permute-start | bytes 1572872 | tf_op jit(solution)/shard_map/ppermute | solution.py:43
  2.1 1.4 %collective-permute-start.12 = (bf16[2,512,256]{2,1,0:T(8,128)(2,1)}, bf16[2,512,256]{2,1,0:T(8,128)(2,1)S(1)}, u32[]{:S(2)}, u32[]{:S(2)}) collective-permute-start(bf16[2,512,256]{2,1,0:T(8,128)(2,1)} %bitcast.11), channel_id=1, source_target_pairs={{0,192},{64,0},{128,64},{192,128},{1,193},{65,1},{129,65},{193,129... | collective-permute-start | bytes 1572872 | tf_op jit(solution)/shard_map/ppermute | solution.py:43
  3.6 0.0 copy-start
  3.6 1.0 %copy-done = bf16[2,1,512,256]{3,2,1,0:T(8,128)(2,1)S(1)} copy-done((bf16[2,1,512,256]{3,2,1,0:T(8,128)(2,1)S(1)}, bf16[2,1,512,256]{3,2,1,0:T(8,128)(2,1)}, u32[]{:S(2)}) %copy-start) | copy-done | bytes 524312
  4.6 0.0 copy-start.2
  4.6 0.7 copy-done.2
  5.3 1.4 %collective-permute-start.9 = (bf16[2,528,256]{2,1,0:T(8,128)(2,1)S(1)}, bf16[2,528,256]{2,1,0:T(8,128)(2,1)S(1)}, u32[]{:S(2)}, u32[]{:S(2)}) collective-permute-start(bf16[2,528,256]{2,1,0:T(8,128)(2,1)S(1)} %load.1), channel_id=1, source_target_pairs={{0,96},{32,64},{64,160},{96,128},{128,224},{160,192},{192,32},{224... | collective-permute-start | bytes 1622024 | tf_op jit(solution)/shard_map/ppermute | solution.py:52
  6.7 0.0 copy-start.1
  6.7 0.8 fusion.1
  7.5 0.0 copy-start.3
  7.5 1.7 %collective-permute-start = (bf16[80,256]{1,0:T(8,128)(2,1)S(1)}, bf16[80,256]{1,0:T(8,128)(2,1)S(1)}, u32[]{:S(2)}, u32[]{:S(2)}) collective-permute-start(bf16[80,256]{1,0:T(8,128)(2,1)S(1)} %fusion.1), channel_id=1, source_target_pairs={{0,32},{32,0},{1,33},{33,1},{2,34},{34,2},{3,35},{35,3},{4,36},{36... | collective-permute-start | bytes 122888 | tf_op jit(solution)/shard_map/ppermute | solution.py:39
  9.2 5.5 %collective-permute-start.1 = (bf16[80,256]{1,0:T(8,128)(2,1)S(1)}, bf16[80,256]{1,0:T(8,128)(2,1)S(1)}, u32[]{:S(2)}, u32[]{:S(2)}) collective-permute-start(bf16[80,256]{1,0:T(8,128)(2,1)S(1)} %fusion.1), channel_id=1, source_target_pairs={{0,48},{1,49},{2,50},{3,51},{4,52},{5,53},{6,54},{7,55},{8,56},{9,... | collective-permute-start | bytes 122888 | tf_op jit(solution)/shard_map/ppermute | solution.py:67
  14.8 0.0 collective-permute-done.refs_0_
  14.8 1.2 %collective-permute-start.2 = (bf16[80,256]{1,0:T(8,128)(2,1)S(1)}, bf16[80,256]{1,0:T(8,128)(2,1)S(1)}, u32[]{:S(2)}, u32[]{:S(2)}) collective-permute-start(bf16[80,256]{1,0:T(8,128)(2,1)S(1)} %fusion.1), channel_id=1, source_target_pairs={{0,40},{1,41},{2,42},{3,43},{4,44},{5,45},{6,46},{7,47},{8,32},{9,... | collective-permute-start | bytes 122888 | tf_op jit(solution)/shard_map/ppermute | solution.py:67
  15.9 0.6 collective-permute-done.1.refs_1_
  16.5 4.8 %collective-permute-start.3 = (bf16[80,256]{1,0:T(8,128)(2,1)S(1)}, bf16[80,256]{1,0:T(8,128)(2,1)S(1)}, u32[]{:S(2)}, u32[]{:S(2)}) collective-permute-start(bf16[80,256]{1,0:T(8,128)(2,1)S(1)} %fusion.1), channel_id=1, source_target_pairs={{0,56},{1,57},{2,58},{3,59},{4,60},{5,61},{6,62},{7,63},{8,48},{9,... | collective-permute-start | bytes 122888 | tf_op jit(solution)/shard_map/ppermute | solution.py:67
  21.4 0.0 collective-permute-done.2.refs_2_
  21.4 1.7 %collective-permute-done.3.refs_3_ = bf16[80,256]{1,0:T(8,128)(2,1)S(1)} collective-permute-done((bf16[80,256]{1,0:T(8,128)(2,1)S(1)}, bf16[80,256]{1,0:T(8,128)(2,1)S(1)}, u32[]{:S(2)}, u32[]{:S(2)}) %collective-permute-start.3) | collective-permute-done | bytes 40992 | tf_op jit(solution)/shard_map/ppermute | solution.py:67
  23.1 1.6 %collective-permute-start.4 = (bf16[320,256]{1,0:T(8,128)(2,1)S(1)}, bf16[320,256]{1,0:T(8,128)(2,1)S(1)}, u32[]{:S(2)}, u32[]{:S(2)}) collective-permute-start(bf16[320,256]{1,0:T(8,128)(2,1)S(1)} %join.1.a), channel_id=1, source_target_pairs={{0,4},{1,5},{2,6},{3,7},{4,0},{5,1},{6,2},{7,3},{8,12},{9,13},{10,... | collective-permute-start | bytes 491528 | tf_op jit(solution)/shard_map/ppermute | solution.py:57
  24.6 2.1 %collective-permute-start.11 = (bf16[2,528,256]{2,1,0:T(8,128)(2,1)S(1)}, bf16[2,528,256]{2,1,0:T(8,128)(2,1)S(1)}, u32[]{:S(2)}, u32[]{:S(2)}) collective-permute-start(bf16[2,528,256]{2,1,0:T(8,128)(2,1)S(1)} %load.1), channel_id=1, source_target_pairs={{0,224},{32,192},{64,32},{96,0},{128,96},{160,64},{192,160},{224,1... | collective-permute-start | bytes 1622024 | tf_op jit(solution)/shard_map/ppermute | solution.py:52
  26.8 1.8 %collective-permute-done.4.b = bf16[320,256]{1,0:T(8,128)(2,1)S(1)} collective-permute-done((bf16[320,256]{1,0:T(8,128)(2,1)S(1)}, bf16[320,256]{1,0:T(8,128)(2,1)S(1)}, u32[]{:S(2)}, u32[]{:S(2)}) %collective-permute-start.4) | collective-permute-done | bytes 163872 | tf_op jit(solution)/shard_map/ppermute | solution.py:57
  28.5 1.3 %collective-permute-start.8 = (bf16[2,528,256]{2,1,0:T(8,128)(2,1)S(1)}, bf16[2,528,256]{2,1,0:T(8,128)(2,1)S(1)}, u32[]{:S(2)}, u32[]{:S(2)}) collective-permute-start(bf16[2,528,256]{2,1,0:T(8,128)(2,1)S(1)} %load.1), channel_id=1, source_target_pairs={{0,32},{32,0},{1,33},{33,1},{2,34},{34,2},{3,35},{35,3},{4,36},{36... | collective-permute-start | bytes 1622024 | tf_op jit(solution)/shard_map/ppermute | solution.py:39
  29.8 0.0 collective-permute-done.10.wl.weights
  29.8 1.3 %collective-permute-start.5 = (bf16[528,256]{1,0:T(8,128)(2,1)S(1)}, bf16[528,256]{1,0:T(8,128)(2,1)S(1)}, u32[]{:S(2)}, u32[]{:S(2)}) collective-permute-start(bf16[528,256]{1,0:T(8,128)(2,1)S(1)} %pack.1.s0), channel_id=1, source_target_pairs={{0,1},{1,2},{2,3},{3,0},{4,5},{5,6},{6,7},{7,4},{8,9},{9,10},{10,1... | collective-permute-start | bytes 811016 | tf_op jit(solution)/shard_map/ppermute | solution.py:72
  31.1 0.0 collective-permute-done.12.wr.weights
  31.1 2.5 %collective-permute-start.6 = (bf16[528,256]{1,0:T(8,128)(2,1)S(1)}, bf16[528,256]{1,0:T(8,128)(2,1)S(1)}, u32[]{:S(2)}, u32[]{:S(2)}) collective-permute-start(bf16[528,256]{1,0:T(8,128)(2,1)S(1)} %pack.1.s0), channel_id=1, source_target_pairs={{0,2},{1,3},{2,0},{3,1},{4,6},{5,7},{6,4},{7,5},{8,10},{9,11},{10,... | collective-permute-start | bytes 811016 | tf_op jit(solution)/shard_map/ppermute | solution.py:72
  33.6 0.0 collective-permute-done.9.ol.obs
  33.6 1.2 %collective-permute-start.7 = (bf16[528,256]{1,0:T(8,128)(2,1)S(1)}, bf16[528,256]{1,0:T(8,128)(2,1)S(1)}, u32[]{:S(2)}, u32[]{:S(2)}) collective-permute-start(bf16[528,256]{1,0:T(8,128)(2,1)S(1)} %pack.1.s0), channel_id=1, source_target_pairs={{0,3},{1,0},{2,1},{3,2},{4,7},{5,4},{6,5},{7,6},{8,11},{9,8},{10,9... | collective-permute-start | bytes 811016 | tf_op jit(solution)/shard_map/ppermute | solution.py:72
  34.8 4.0 %collective-permute-done.11.orr.obs = bf16[2,528,256]{2,1,0:T(8,128)(2,1)S(1)} collective-permute-done((bf16[2,528,256]{2,1,0:T(8,128)(2,1)S(1)}, bf16[2,528,256]{2,1,0:T(8,128)(2,1)S(1)}, u32[]{:S(2)}, u32[]{:S(2)}) %collective-permute-start.11) | collective-permute-done | bytes 540704 | tf_op jit(solution)/shard_map/ppermute | solution.py:52
  38.8 1.0 %collective-permute-start.13 = (bf16[1040,256]{1,0:T(8,128)(2,1)S(1)}, bf16[1040,256]{1,0:T(8,128)(2,1)S(1)}, u32[]{:S(2)}, u32[]{:S(2)}) collective-permute-start(bf16[1040,256]{1,0:T(8,128)(2,1)S(1)} %relay.2), channel_id=1, source_target_pairs={{0,64},{64,128},{128,192},{192,0},{1,65},{65,129},{129,193},{193,1... | collective-permute-start | bytes 1597448 | tf_op jit(solution)/shard_map/ppermute | solution.py:43
  39.8 0.0 collective-permute-done.5.s1
  39.8 2.5 %collective-permute-start.14 = (bf16[1040,256]{1,0:T(8,128)(2,1)S(1)}, bf16[1040,256]{1,0:T(8,128)(2,1)S(1)}, u32[]{:S(2)}, u32[]{:S(2)}) collective-permute-start(bf16[1040,256]{1,0:T(8,128)(2,1)S(1)} %relay.3), channel_id=1, source_target_pairs={{0,192},{64,0},{128,64},{192,128},{1,193},{65,1},{129,65},{193,129... | collective-permute-start | bytes 1597448 | tf_op jit(solution)/shard_map/ppermute | solution.py:43
  42.3 0.0 copy-done.1
  42.3 4.5 %lists.1 = s32[456]{0:T(512)S(1)} custom-call(s32[2,16,512]{2,1,0:T(8,128)S(1)} %bitcast.9), custom_call_target="tpu_custom_call" | custom-call | flops 4000000 | bytes 4000000 | tf_op jit(solution)/shard_map/lists/pallas_call | solution.py:100
  46.9 0.0 collective-permute-done.6.s2
  46.9 0.0 collective-permute-done.7.s3
  46.9 0.0 collective-permute-done.8.oo
  46.9 0.0 copy-done.3
  46.9 11.3 %near.1 = (bf16[34,64,256]{2,1,0:T(8,128)(2,1)S(1)}, f32[34,64,128]{2,1,0:T(8,128)S(1)}, f32[17,128,256]{2,1,0:T(8,128)S(1)}) custom-call(s32[456]{0:T(512)S(1)} %lists.1, bf16[528,256]{1,0:T(8,128)(2,1)S(1)} %pack.1.s0, bf16[528,256]{1,0:T(8,128)(2,1)S(1)} %collective-permute-done.5.s1, bf16[528,256]{1,0:T(8,128)(2,1)S(1)} %collective-permute-done.6.s2, ...), custom_call_target="tpu_custom_call" | custom-call | flops 4000000000 | bytes 8000000 | tf_op jit(solution)/shard_map/near/pallas_call | solution.py:200
  58.2 0.0 collective-permute-done.13.left
  58.2 0.0 collective-permute-done.14.right
  58.2 3.8 %far.1 = bf16[2048,256]{1,0:T(8,128)(2,1)S(1)} custom-call(s32[456]{0:T(512)S(1)} %lists.1, bf16[34,64,256]{2,1,0:T(8,128)(2,1)S(1)} %get-tuple-element.8.state, f32[34,64,128]{2,1,0:T(8,128)S(1)} %get-tuple-element.9.spot, f32[17,128,256]{2,1,0:T(8,128)S(1)} %get-tuple-element.10.near_acc, bf16[1040,256]{1,0:T(8,128)(2,1)S(1)} %collective-permute-done.13.left, ...), custom_call_target="tpu_custom_call" | custom-call | flops 1000000000 | bytes 8000000 | tf_op jit(solution)/shard_map/far/pallas_call | solution.py:232
  62.1 35.3 %all_to_all.9 = bf16[32,64,256]{2,1,0:T(8,128)(2,1)S(1)} all-to-all(bf16[32,64,256]{2,1,0:T(8,128)(2,1)S(1)} %bitcast.7), channel_id=1, replica_groups=mesh['rows'=4,'half'=2,'obs'=32] {'obs'}, dimensions={0} | all-to-all | bytes 2097152 | tf_op jit(solution)/shard_map/all_to_all | solution.py:359
  97.3 0.8 convert_reduce_fusion
  (5 shorter events, 0.1 us)
Async XLA Ops:
  0.0 29.8 %collective-permute-start.10 = (bf16[2,512,256]{2,1,0:T(8,128)(2,1)}, bf16[2,512,256]{2,1,0:T(8,128)(2,1)S(1)}, u32[]{:S(2)}, u32[]{:S(2)}) collective-permute-start(bf16[2,512,256]{2,1,0:T(8,128)(2,1)} %bitcast.10), channel_id=1, source_target_pairs={{0,64},{64,128},{128,192},{192,0},{1,65},{65,129},{129,193},{193,1... | collective-permute-start | bytes 1572872 | tf_op jit(solution)/shard_map/ppermute | solution.py:43
  2.1 29.0 %collective-permute-start.12 = (bf16[2,512,256]{2,1,0:T(8,128)(2,1)}, bf16[2,512,256]{2,1,0:T(8,128)(2,1)S(1)}, u32[]{:S(2)}, u32[]{:S(2)}) collective-permute-start(bf16[2,512,256]{2,1,0:T(8,128)(2,1)} %bitcast.11), channel_id=1, source_target_pairs={{0,192},{64,0},{128,64},{192,128},{1,193},{65,1},{129,65},{193,129... | collective-permute-start | bytes 1572872 | tf_op jit(solution)/shard_map/ppermute | solution.py:43
  3.6 1.0 %copy-start = (bf16[2,1,512,256]{3,2,1,0:T(8,128)(2,1)S(1)}, bf16[2,1,512,256]{3,2,1,0:T(8,128)(2,1)}, u32[]{:S(2)}) copy-start(bf16[2,1,512,256]{3,2,1,0:T(8,128)(2,1)} %param.8) | copy-start | bytes 1572868
  4.6 0.7 copy-start.2
  5.3 28.2 %collective-permute-start.9 = (bf16[2,528,256]{2,1,0:T(8,128)(2,1)S(1)}, bf16[2,528,256]{2,1,0:T(8,128)(2,1)S(1)}, u32[]{:S(2)}, u32[]{:S(2)}) collective-permute-start(bf16[2,528,256]{2,1,0:T(8,128)(2,1)S(1)} %load.1), channel_id=1, source_target_pairs={{0,96},{32,64},{64,160},{96,128},{128,224},{160,192},{192,32},{224... | collective-permute-start | bytes 1622024 | tf_op jit(solution)/shard_map/ppermute | solution.py:52
  6.7 35.7 %copy-start.1 = (s32[2,512,16]{1,2,0:T(8,128)S(1)}, s32[2,512,16]{1,2,0:T(8,128)}, u32[]{:S(2)}) copy-start(s32[2,512,16]{1,2,0:T(8,128)} %param.11) | copy-start | bytes 196612
  7.5 39.4 %copy-start.3 = (bf16[2,1,512,256]{3,2,1,0:T(8,128)(2,1)S(1)}, bf16[2,1,512,256]{3,2,1,0:T(8,128)(2,1)}, u32[]{:S(2)}) copy-start(bf16[2,1,512,256]{3,2,1,0:T(8,128)(2,1)} %param.10) | copy-start | bytes 1572868
  7.5 7.3 %collective-permute-start = (bf16[80,256]{1,0:T(8,128)(2,1)S(1)}, bf16[80,256]{1,0:T(8,128)(2,1)S(1)}, u32[]{:S(2)}, u32[]{:S(2)}) collective-permute-start(bf16[80,256]{1,0:T(8,128)(2,1)S(1)} %fusion.1), channel_id=1, source_target_pairs={{0,32},{32,0},{1,33},{33,1},{2,34},{34,2},{3,35},{35,3},{4,36},{36... | collective-permute-start | bytes 122888 | tf_op jit(solution)/shard_map/ppermute | solution.py:39
  9.2 7.3 %collective-permute-start.1 = (bf16[80,256]{1,0:T(8,128)(2,1)S(1)}, bf16[80,256]{1,0:T(8,128)(2,1)S(1)}, u32[]{:S(2)}, u32[]{:S(2)}) collective-permute-start(bf16[80,256]{1,0:T(8,128)(2,1)S(1)} %fusion.1), channel_id=1, source_target_pairs={{0,48},{1,49},{2,50},{3,51},{4,52},{5,53},{6,54},{7,55},{8,56},{9,... | collective-permute-start | bytes 122888 | tf_op jit(solution)/shard_map/ppermute | solution.py:67
  14.8 6.6 %collective-permute-start.2 = (bf16[80,256]{1,0:T(8,128)(2,1)S(1)}, bf16[80,256]{1,0:T(8,128)(2,1)S(1)}, u32[]{:S(2)}, u32[]{:S(2)}) collective-permute-start(bf16[80,256]{1,0:T(8,128)(2,1)S(1)} %fusion.1), channel_id=1, source_target_pairs={{0,40},{1,41},{2,42},{3,43},{4,44},{5,45},{6,46},{7,47},{8,32},{9,... | collective-permute-start | bytes 122888 | tf_op jit(solution)/shard_map/ppermute | solution.py:67
  16.5 6.5 %collective-permute-start.3 = (bf16[80,256]{1,0:T(8,128)(2,1)S(1)}, bf16[80,256]{1,0:T(8,128)(2,1)S(1)}, u32[]{:S(2)}, u32[]{:S(2)}) collective-permute-start(bf16[80,256]{1,0:T(8,128)(2,1)S(1)} %fusion.1), channel_id=1, source_target_pairs={{0,56},{1,57},{2,58},{3,59},{4,60},{5,61},{6,62},{7,63},{8,48},{9,... | collective-permute-start | bytes 122888 | tf_op jit(solution)/shard_map/ppermute | solution.py:67
  23.1 5.5 %collective-permute-start.4 = (bf16[320,256]{1,0:T(8,128)(2,1)S(1)}, bf16[320,256]{1,0:T(8,128)(2,1)S(1)}, u32[]{:S(2)}, u32[]{:S(2)}) collective-permute-start(bf16[320,256]{1,0:T(8,128)(2,1)S(1)} %join.1.a), channel_id=1, source_target_pairs={{0,4},{1,5},{2,6},{3,7},{4,0},{5,1},{6,2},{7,3},{8,12},{9,13},{10,... | collective-permute-start | bytes 491528 | tf_op jit(solution)/shard_map/ppermute | solution.py:57
  24.6 14.1 %collective-permute-start.11 = (bf16[2,528,256]{2,1,0:T(8,128)(2,1)S(1)}, bf16[2,528,256]{2,1,0:T(8,128)(2,1)S(1)}, u32[]{:S(2)}, u32[]{:S(2)}) collective-permute-start(bf16[2,528,256]{2,1,0:T(8,128)(2,1)S(1)} %load.1), channel_id=1, source_target_pairs={{0,224},{32,192},{64,32},{96,0},{128,96},{160,64},{192,160},{224,1... | collective-permute-start | bytes 1622024 | tf_op jit(solution)/shard_map/ppermute | solution.py:52
  28.5 18.4 %collective-permute-start.8 = (bf16[2,528,256]{2,1,0:T(8,128)(2,1)S(1)}, bf16[2,528,256]{2,1,0:T(8,128)(2,1)S(1)}, u32[]{:S(2)}, u32[]{:S(2)}) collective-permute-start(bf16[2,528,256]{2,1,0:T(8,128)(2,1)S(1)} %load.1), channel_id=1, source_target_pairs={{0,32},{32,0},{1,33},{33,1},{2,34},{34,2},{3,35},{35,3},{4,36},{36... | collective-permute-start | bytes 1622024 | tf_op jit(solution)/shard_map/ppermute | solution.py:39
  29.8 10.0 %collective-permute-start.5 = (bf16[528,256]{1,0:T(8,128)(2,1)S(1)}, bf16[528,256]{1,0:T(8,128)(2,1)S(1)}, u32[]{:S(2)}, u32[]{:S(2)}) collective-permute-start(bf16[528,256]{1,0:T(8,128)(2,1)S(1)} %pack.1.s0), channel_id=1, source_target_pairs={{0,1},{1,2},{2,3},{3,0},{4,5},{5,6},{6,7},{7,4},{8,9},{9,10},{10,1... | collective-permute-start | bytes 811016 | tf_op jit(solution)/shard_map/ppermute | solution.py:72
  31.1 15.8 %collective-permute-start.6 = (bf16[528,256]{1,0:T(8,128)(2,1)S(1)}, bf16[528,256]{1,0:T(8,128)(2,1)S(1)}, u32[]{:S(2)}, u32[]{:S(2)}) collective-permute-start(bf16[528,256]{1,0:T(8,128)(2,1)S(1)} %pack.1.s0), channel_id=1, source_target_pairs={{0,2},{1,3},{2,0},{3,1},{4,6},{5,7},{6,4},{7,5},{8,10},{9,11},{10,... | collective-permute-start | bytes 811016 | tf_op jit(solution)/shard_map/ppermute | solution.py:72
  33.6 13.3 %collective-permute-start.7 = (bf16[528,256]{1,0:T(8,128)(2,1)S(1)}, bf16[528,256]{1,0:T(8,128)(2,1)S(1)}, u32[]{:S(2)}, u32[]{:S(2)}) collective-permute-start(bf16[528,256]{1,0:T(8,128)(2,1)S(1)} %pack.1.s0), channel_id=1, source_target_pairs={{0,3},{1,0},{2,1},{3,2},{4,7},{5,4},{6,5},{7,6},{8,11},{9,8},{10,9... | collective-permute-start | bytes 811016 | tf_op jit(solution)/shard_map/ppermute | solution.py:72
  38.8 19.5 %collective-permute-start.13 = (bf16[1040,256]{1,0:T(8,128)(2,1)S(1)}, bf16[1040,256]{1,0:T(8,128)(2,1)S(1)}, u32[]{:S(2)}, u32[]{:S(2)}) collective-permute-start(bf16[1040,256]{1,0:T(8,128)(2,1)S(1)} %relay.2), channel_id=1, source_target_pairs={{0,64},{64,128},{128,192},{192,0},{1,65},{65,129},{129,193},{193,1... | collective-permute-start | bytes 1597448 | tf_op jit(solution)/shard_map/ppermute | solution.py:43
  39.8 18.4 %collective-permute-start.14 = (bf16[1040,256]{1,0:T(8,128)(2,1)S(1)}, bf16[1040,256]{1,0:T(8,128)(2,1)S(1)}, u32[]{:S(2)}, u32[]{:S(2)}) collective-permute-start(bf16[1040,256]{1,0:T(8,128)(2,1)S(1)} %relay.3), channel_id=1, source_target_pairs={{0,192},{64,0},{128,64},{192,128},{1,193},{65,1},{129,65},{193,129... | collective-permute-start | bytes 1597448 | tf_op jit(solution)/shard_map/ppermute | solution.py:43

commit v2 on v1

--- a/solution.py
+++ b/solution.py
@@ -24,8 +24,8 @@
 
 GROUP = 8
 SOURCES = ((0, 2, 0), (3, 2, 0), (1, 2, 0), (2, 1, 0), (2, 1, 1))
-PICKS = 8 * GROUP + NAMED
-VISITS = 8
+PICKS = 10 * GROUP + NAMED
+VISITS = 10
 BLOCKS = len(SOURCES) * PICKS
 TOTALS = BLOCKS + len(SOURCES) * VISITS + 8
 LIVE = math.log2(1.0 / (MEMBERS - 1))
@@ -65,6 +65,11 @@
         for x in range(NX)
     ]
     return lax.ppermute(value, ("half", "obs"), pairs)
+
+
+def swap_x(value, mask):
+    pairs = [(z * NX + x, z * NX + (x ^ mask)) for z in range(NZ) for x in range(NX)]
+    return lax.ppermute(value, "obs", pairs)
 
 
 def along_x(value, step):
@@ -93,7 +98,11 @@
             lists[BLOCKS + s * VISITS + visits] = i
             return visits + (write > start).astype(jnp.int32)
 
-        lists[TOTALS + s] = lax.fori_loop(0, batches * SPAN, fill, jnp.int32(0))
+        visits = lax.fori_loop(0, batches * SPAN, fill, jnp.int32(0))
+        lists[TOTALS + s] = visits
+        lists[BLOCKS + s * VISITS + visits] = 0
+        for k in range(GROUP):
+            lists[s * PICKS + visits * GROUP + k] = RANGE_BLOCKS
 
 
 def make_lists(named):
@@ -111,7 +120,7 @@
 def visit(s, obs, weights, places, state, spot, acc, tiles, lists):
     total = lists[TOTALS + s]
 
-    def make_tiles(g):
+    def make_tiles(g, lane):
         i = lists[BLOCKS + s * VISITS + g]
         here = obs(i)
         place = places[pl.ds(i, 1), :]
@@ -125,26 +134,32 @@
         for k, b in enumerate(chosen):
             d = spot[pl.ds(2 * b, 2)].reshape(EDGE, EDGE) - place
             damped = products[k * EDGE : (k + 1) * EDGE] * jnp.exp2(LIVE - d * d)
-            tiles[k * EDGE : (k + 1) * EDGE] = damped.astype(jnp.bfloat16)
-
-    def add_tiles(g):
+            tiles[lane, k * EDGE : (k + 1) * EDGE] = damped.astype(jnp.bfloat16)
+
+    def add_tiles(g, lane):
         weight = weights(lists[BLOCKS + s * VISITS + g])
         chosen = [lists[s * PICKS + g * GROUP + k] for k in range(GROUP)]
-        added = jnp.dot(tiles[...], weight, preferred_element_type=jnp.float32)
+        added = jnp.dot(tiles[lane], weight, preferred_element_type=jnp.float32)
         for k, b in enumerate(chosen):
             acc[b] += added[k * EDGE : (k + 1) * EDGE]
 
     @pl.when(total > 0)
     def _():
-        make_tiles(0)
-
-        def step(g, carry):
-            add_tiles(g - 1)
-            make_tiles(g)
+        make_tiles(0, 0)
+        make_tiles(1, 1)
+
+        def step(h, carry):
+            g = 2 * h
+            add_tiles(g - 2, 0)
+            make_tiles(g, 0)
+            add_tiles(g - 1, 1)
+            make_tiles(g + 1, 1)
             return carry
 
-        lax.fori_loop(1, total, step, 0)
-        add_tiles(total - 1)
+        pairs = lax.shift_right_logical(total + 1, 1)
+        lax.fori_loop(1, pairs, step, 0)
+        add_tiles(2 * pairs - 2, 0)
+        add_tiles(2 * pairs - 1, 1)
 
 
 def split(ref):
@@ -208,7 +223,7 @@
         out_specs=(VMEM,) * 3,
         scratch_shapes=[
             pltpu.VMEM((8, EDGE), jnp.float32),
-            pltpu.VMEM((GROUP * EDGE, EDGE), jnp.bfloat16),
+            pltpu.VMEM((2, GROUP * EDGE, EDGE), jnp.bfloat16),
         ],
         compiler_params=pltpu.CompilerParams(vmem_limit_bytes=24 << 20),
         cost_estimate=pl.CostEstimate(
@@ -218,25 +233,34 @@
     )(lists, *arrays)
 
 
-def far_kernel(lists, state, spot, near_acc, left, right, out, places, tiles, acc):
+def far_kernel(lists, state, spot, near_acc, left, right, own, x1, x2, x3, places, tiles, acc):
     acc[...] = near_acc[...]
     for s, both in ((3, left), (4, right)):
         spread_places(both[OBS_ROWS : OBS_ROWS + PAD, :EDGE], places, 0)
         visit(
             s, flat(both, 0), flat(both, OBS_ROWS + PAD), places, state, spot, acc, tiles, lists
         )
-    out[...] = acc[:RANGE_BLOCKS].reshape(RANGE_BLOCKS * EDGE, MEMBERS).astype(jnp.bfloat16)
+    my_x = jnp.bitwise_and(lax.axis_index("obs"), NX - 1)
+    for mask, out in enumerate((own, x1, x2, x3)):
+        x = jnp.bitwise_xor(my_x, mask)
+        start = pl.multiple_of(jnp.bitwise_and(x, 1) * SHARD, SHARD)
+        for z in range(NZ):
+            block = 2 * z + lax.shift_right_logical(x, 1)
+            part = acc[block, pl.ds(start, SHARD), :]
+            out[z * SHARD : (z + 1) * SHARD] = part.astype(out.dtype)
 
 
 def far(lists, state, spot, acc, arrays):
+    rows = NZ * SHARD
     return pl.pallas_call(
         far_kernel,
-        out_shape=jax.ShapeDtypeStruct((RANGE_BLOCKS * EDGE, MEMBERS), jnp.bfloat16),
+        out_shape=(jax.ShapeDtypeStruct((rows, MEMBERS), jnp.float32),)
+        + (jax.ShapeDtypeStruct((rows, MEMBERS), jnp.bfloat16),) * 3,
         in_specs=[SMEM] + [VMEM] * 5,
-        out_specs=VMEM,
+        out_specs=(VMEM,) * 4,
         scratch_shapes=[
             pltpu.VMEM((8, EDGE), jnp.float32),
-            pltpu.VMEM((GROUP * EDGE, EDGE), jnp.bfloat16),
+            pltpu.VMEM((2, GROUP * EDGE, EDGE), jnp.bfloat16),
             pltpu.VMEM((RANGE_BLOCKS + 1, EDGE, MEMBERS), jnp.float32),
         ],
         compiler_params=pltpu.CompilerParams(vmem_limit_bytes=24 << 20),
@@ -245,6 +269,37 @@
         ),
         name="far",
     )(lists, state, spot, acc, *arrays)
+
+
+def sum_x_kernel(own, x1, x2, x3, keep, send):
+    my_z = lax.shift_right_logical(lax.axis_index("obs"), 2)
+    for mask in range(NZ):
+        rows = pl.ds(pl.multiple_of(jnp.bitwise_xor(my_z, mask) * SHARD, SHARD), SHARD)
+        total = own[rows, :]
+        for ref in (x1, x2, x3):
+            total += ref[rows, :].astype(jnp.float32)
+        out, k = (send if mask & 1 else keep), mask // 2
+        out[k * SHARD : (k + 1) * SHARD] = total
+
+
+def sum_z1_kernel(keep, got, own, z2, z4, z6):
+    for k, out in enumerate((own, z2, z4, z6)):
+        rows = slice(k * SHARD, (k + 1) * SHARD)
+        out[...] = keep[rows] + got[rows]
+
+
+def sum_z_kernel(own, z2, z4, z6, out):
+    out[...] = own[...] + z2[...] + z4[...] + z6[...]
+
+
+def small(body, out_rows, *arrays):
+    return pl.pallas_call(
+        body,
+        out_shape=tuple(jax.ShapeDtypeStruct((r, MEMBERS), jnp.float32) for r in out_rows),
+        in_specs=[VMEM] * len(arrays),
+        out_specs=(VMEM,) * len(out_rows),
+        compiler_params=pltpu.CompilerParams(vmem_limit_bytes=6 << 20),
+    )(*arrays)
 
 
 def pack_kernel(a, b, out):
@@ -355,10 +410,16 @@
 
     lists = make_lists(jnp.transpose(block_rows, (0, 2, 1)))
     held = near(lists, (*pieces, obs_own, weight, obs_left, weight_left, obs_right, weight_right))
-    partial = far(lists, *held, (far0, far1))
-    shares = lax.all_to_all(partial, "obs", 0, 0, tiled=True)
-    shares = shares.reshape(OBS, SHARD, MEMBERS).astype(jnp.float32)
-    return jnp.sum(shares, axis=0)[None]
+    own, *parts = far(lists, *held, (far0, far1))
+    for mask in (2, 1, 3):
+        parts[mask - 1] = swap_x(parts[mask - 1], mask)
+    keep, send = small(sum_x_kernel, (4 * SHARD, 4 * SHARD), own, *parts)
+    got = swap_z(send, 1)
+    own, *parts = small(sum_z1_kernel, (SHARD,) * 4, keep, got)
+    for k, mask in ((1, 4), (0, 2), (2, 6)):
+        parts[k] = swap_z(parts[k], mask)
+    (total,) = small(sum_z_kernel, (SHARD,), own, *parts)
+    return total[None]
 
 
 def solution(mesh):

time: 100 us -> 99.4 us (level)
  the two profiles are of different devices: /device:TPU:1 before, /device:TPU:56 now
where the time goes in v2:
time: 99.4 us; the launch traced here: 99.2 us
  starting transfers between devices  40.7 us (41%)
  waiting for transfers between devices  36.2 us (36%)
  Pallas kernels  19.6 us (20%)
  local copies, waits for them, and re-layouts  1.73 us (2%)
    ppermute x5, waiting for transfers between devices, swap_z(): return lax.ppermute(value, 'obs', pairs)  17.2 us
    ppermute x3, waiting for transfers between devices, swap_x(): return lax.ppermute(value, 'obs', pairs)  12.9 us
    ppermute x3, starting transfers between devices, swap_z_flip(): return lax.ppermute(value, ('half', 'obs'), pairs)  12.4 us
    ppermute x5, starting transfers between devices, swap_z(): return lax.ppermute(value, 'obs', pairs)  11.7 us
    pallas_call x1, Pallas kernels, near(): pl.pallas_call(near_kernel, out_shape=(jax.ShapeDtypeStruct((OBS + 2, SHA...  9.86 us
    ppermute x3, starting transfers between devices, along_x(): return lax.ppermute(value, 'obs', pairs)  5.73 us
    ppermute x3, starting transfers between devices, swap_x(): return lax.ppermute(value, 'obs', pairs)  4.79 us
    pallas_call x1, Pallas kernels, make_lists(): pl.pallas_call(lists_kernel, out_shape=jax.ShapeDtypeStruct((TOTALS + 8,)...  4.56 us
  transfers between devices with their start and end apart: 22, of which 10 were waited for; matrix products, arithmetic and copies ran while one was open for 1% of the time, Pallas kernels for 15%

profile of v2, /device:TPU:56, one launch (start us, length us, event | category | flops | bytes accessed | tf_op | source)
XLA Modules:
  0.0 99.2 jit_solution(16169982381006803269)
XLA Ops:
  0.0 0.2 collective-permute-start.10
  0.2 1.8 %collective-permute-start.12 = (bf16[2,512,256]{2,1,0:T(8,128)(2,1)}, bf16[2,512,256]{2,1,0:T(8,128)(2,1)S(1)}, u32[]{:S(2)}, u32[]{:S(2)}) collective-permute-start(bf16[2,512,256]{2,1,0:T(8,128)(2,1)} %bitcast.9), channel_id=1, source_target_pairs={{0,192},{64,0},{128,64},{192,128},{1,193},{65,1},{129,65},{193,129... | collective-permute-start | bytes 1572872 | tf_op jit(solution)/shard_map/ppermute | solution.py:43
  2.0 1.0 %copy-done = bf16[2,1,512,256]{3,2,1,0:T(8,128)(2,1)S(1)} copy-done((bf16[2,1,512,256]{3,2,1,0:T(8,128)(2,1)S(1)}, bf16[2,1,512,256]{3,2,1,0:T(8,128)(2,1)}, u32[]{:S(2)}) %copy-start) | copy-done | bytes 524312
  3.1 0.7 copy-done.2
  3.8 0.5 collective-permute-start.9
  4.2 0.8 fusion.1
  5.0 1.2 %collective-permute-start = (bf16[80,256]{1,0:T(8,128)(2,1)S(1)}, bf16[80,256]{1,0:T(8,128)(2,1)S(1)}, u32[]{:S(2)}, u32[]{:S(2)}) collective-permute-start(bf16[80,256]{1,0:T(8,128)(2,1)S(1)} %fusion.1), channel_id=1, source_target_pairs={{0,32},{32,0},{1,33},{33,1},{2,34},{34,2},{3,35},{35,3},{4,36},{36... | collective-permute-start | bytes 122888 | tf_op jit(solution)/shard_map/ppermute | solution.py:39
  6.2 6.0 %collective-permute-start.1 = (bf16[80,256]{1,0:T(8,128)(2,1)S(1)}, bf16[80,256]{1,0:T(8,128)(2,1)S(1)}, u32[]{:S(2)}, u32[]{:S(2)}) collective-permute-start(bf16[80,256]{1,0:T(8,128)(2,1)S(1)} %fusion.1), channel_id=1, source_target_pairs={{0,48},{1,49},{2,50},{3,51},{4,52},{5,53},{6,54},{7,55},{8,56},{9,... | collective-permute-start | bytes 122888 | tf_op jit(solution)/shard_map/ppermute | solution.py:67
  12.2 0.0 collective-permute-done.refs_0_
  12.2 1.5 %collective-permute-start.2 = (bf16[80,256]{1,0:T(8,128)(2,1)S(1)}, bf16[80,256]{1,0:T(8,128)(2,1)S(1)}, u32[]{:S(2)}, u32[]{:S(2)}) collective-permute-start(bf16[80,256]{1,0:T(8,128)(2,1)S(1)} %fusion.1), channel_id=1, source_target_pairs={{0,40},{1,41},{2,42},{3,43},{4,44},{5,45},{6,46},{7,47},{8,32},{9,... | collective-permute-start | bytes 122888 | tf_op jit(solution)/shard_map/ppermute | solution.py:67
  13.7 0.2 collective-permute-done.1.refs_1_
  13.9 4.9 %collective-permute-start.3 = (bf16[80,256]{1,0:T(8,128)(2,1)S(1)}, bf16[80,256]{1,0:T(8,128)(2,1)S(1)}, u32[]{:S(2)}, u32[]{:S(2)}) collective-permute-start(bf16[80,256]{1,0:T(8,128)(2,1)S(1)} %fusion.1), channel_id=1, source_target_pairs={{0,56},{1,57},{2,58},{3,59},{4,60},{5,61},{6,62},{7,63},{8,48},{9,... | collective-permute-start | bytes 122888 | tf_op jit(solution)/shard_map/ppermute | solution.py:67
  18.8 0.0 collective-permute-done.2.refs_2_
  18.8 1.7 %collective-permute-done.3.refs_3_ = bf16[80,256]{1,0:T(8,128)(2,1)S(1)} collective-permute-done((bf16[80,256]{1,0:T(8,128)(2,1)S(1)}, bf16[80,256]{1,0:T(8,128)(2,1)S(1)}, u32[]{:S(2)}, u32[]{:S(2)}) %collective-permute-start.3) | collective-permute-done | bytes 40992 | tf_op jit(solution)/shard_map/ppermute | solution.py:67
  20.5 2.0 %collective-permute-start.4 = (bf16[320,256]{1,0:T(8,128)(2,1)S(1)}, bf16[320,256]{1,0:T(8,128)(2,1)S(1)}, u32[]{:S(2)}, u32[]{:S(2)}) collective-permute-start(bf16[320,256]{1,0:T(8,128)(2,1)S(1)} %join.1.a), channel_id=1, source_target_pairs={{0,4},{1,5},{2,6},{3,7},{4,0},{5,1},{6,2},{7,3},{8,12},{9,13},{10,... | collective-permute-start | bytes 491528 | tf_op jit(solution)/shard_map/ppermute | solution.py:57
  22.5 5.0 %collective-permute-done.4.b = bf16[320,256]{1,0:T(8,128)(2,1)S(1)} collective-permute-done((bf16[320,256]{1,0:T(8,128)(2,1)S(1)}, bf16[320,256]{1,0:T(8,128)(2,1)S(1)}, u32[]{:S(2)}, u32[]{:S(2)}) %collective-permute-start.4) | collective-permute-done | bytes 163872 | tf_op jit(solution)/shard_map/ppermute | solution.py:57
  27.5 0.3 collective-permute-start.8
  27.8 0.0 collective-permute-done.10.wl.weights
  27.8 1.6 %collective-permute-start.5 = (bf16[528,256]{1,0:T(8,128)(2,1)S(1)}, bf16[528,256]{1,0:T(8,128)(2,1)S(1)}, u32[]{:S(2)}, u32[]{:S(2)}) collective-permute-start(bf16[528,256]{1,0:T(8,128)(2,1)S(1)} %pack.1.s0), channel_id=1, source_target_pairs={{0,1},{1,2},{2,3},{3,0},{4,5},{5,6},{6,7},{7,4},{8,9},{9,10},{10,1... | collective-permute-start | bytes 811016 | tf_op jit(solution)/shard_map/ppermute | solution.py:77
  29.4 2.7 %collective-permute-start.6 = (bf16[528,256]{1,0:T(8,128)(2,1)S(1)}, bf16[528,256]{1,0:T(8,128)(2,1)S(1)}, u32[]{:S(2)}, u32[]{:S(2)}) collective-permute-start(bf16[528,256]{1,0:T(8,128)(2,1)S(1)} %pack.1.s0), channel_id=1, source_target_pairs={{0,2},{1,3},{2,0},{3,1},{4,6},{5,7},{6,4},{7,5},{8,10},{9,11},{10,... | collective-permute-start | bytes 811016 | tf_op jit(solution)/shard_map/ppermute | solution.py:77
  32.1 0.0 collective-permute-done.9.ol.obs
  32.1 1.4 %collective-permute-start.7 = (bf16[528,256]{1,0:T(8,128)(2,1)S(1)}, bf16[528,256]{1,0:T(8,128)(2,1)S(1)}, u32[]{:S(2)}, u32[]{:S(2)}) collective-permute-start(bf16[528,256]{1,0:T(8,128)(2,1)S(1)} %pack.1.s0), channel_id=1, source_target_pairs={{0,3},{1,0},{2,1},{3,2},{4,7},{5,4},{6,5},{7,6},{8,11},{9,8},{10,9... | collective-permute-start | bytes 811016 | tf_op jit(solution)/shard_map/ppermute | solution.py:77
  33.6 0.0 copy-start.1
  33.6 0.0 copy-start.3
  33.6 4.2 %collective-permute-done.11.orr.obs = bf16[2,528,256]{2,1,0:T(8,128)(2,1)S(1)} collective-permute-done((bf16[2,528,256]{2,1,0:T(8,128)(2,1)S(1)}, bf16[2,528,256]{2,1,0:T(8,128)(2,1)S(1)}, u32[]{:S(2)}, u32[]{:S(2)}) %collective-permute-start.11) | collective-permute-done | bytes 540704 | tf_op jit(solution)/shard_map/ppermute | solution.py:52
  37.9 0.0 collective-permute-done.5.s1
  37.9 2.1 %collective-permute-start.14 = (bf16[1040,256]{1,0:T(8,128)(2,1)S(1)}, bf16[1040,256]{1,0:T(8,128)(2,1)S(1)}, u32[]{:S(2)}, u32[]{:S(2)}) collective-permute-start(bf16[1040,256]{1,0:T(8,128)(2,1)S(1)} %relay.3), channel_id=1, source_target_pairs={{0,192},{64,0},{128,64},{192,128},{1,193},{65,1},{129,65},{193,129... | collective-permute-start | bytes 1597448 | tf_op jit(solution)/shard_map/ppermute | solution.py:43
  40.0 4.6 %lists.1 = s32[546]{0:T(1024)S(1)} custom-call(s32[2,16,512]{2,1,0:T(8,128)S(1)} %bitcast.7), custom_call_target="tpu_custom_call" | custom-call | flops 4000000 | bytes 4000000 | tf_op jit(solution)/shard_map/lists/pallas_call | solution.py:109
  44.5 0.0 collective-permute-done.7.s3
  44.5 0.0 collective-permute-done.8.oo
  44.6 9.9 %near.1 = (bf16[34,64,256]{2,1,0:T(8,128)(2,1)S(1)}, f32[34,64,128]{2,1,0:T(8,128)S(1)}, f32[17,128,256]{2,1,0:T(8,128)S(1)}) custom-call(s32[546]{0:T(1024)S(1)} %lists.1, bf16[528,256]{1,0:T(8,128)(2,1)S(1)} %pack.1.s0, bf16[528,256]{1,0:T(8,128)(2,1)S(1)} %collective-permute-done.5.s1, bf16[528,256]{1,0:T(8,128)(2,1)S(1)} %collective-permute-done.6.s2, ...), custom_call_target="tpu_custom_call" | custom-call | flops 4000000000 | bytes 8000000 | tf_op jit(solution)/shard_map/near/pallas_call | solution.py:215
  54.4 0.0 collective-permute-done.14.right
  54.5 4.2 %far.1 = (f32[512,256]{1,0:T(8,128)S(1)}, bf16[512,256]{1,0:T(8,128)(2,1)S(1)}, bf16[512,256]{1,0:T(8,128)(2,1)S(1)}, bf16[512,256]{1,0:T(8,128)(2,1)S(1)}) custom-call(s32[546]{0:T(1024)S(1)} %lists.1, bf16[34,64,256]{2,1,0:T(8,128)(2,1)S(1)} %get-tuple-element.18.state, f32[34,64,128]{2,1,0:T(8,128)S(1)} %get-tuple-element.19.spot, ...), custom_call_target="tpu_custom_call" | custom-call | flops 1000000000 | bytes 8000000 | tf_op jit(solution)/shard_map/far/pallas_call | solution.py:255
  58.7 0.8 collective-permute-start.15
  59.5 3.1 %collective-permute-start.16 = (bf16[512,256]{1,0:T(8,128)(2,1)S(1)}, bf16[512,256]{1,0:T(8,128)(2,1)S(1)}, u32[]{:S(2)}, u32[]{:S(2)}) collective-permute-start(bf16[512,256]{1,0:T(8,128)(2,1)S(1)} %get-tuple-element.23), channel_id=1, source_target_pairs={{0,2},{1,3},{2,0},{3,1},{4,6},{5,7},{6,4},{7,5},{8,10},{9,11},{10,... | collective-permute-start | bytes 786440 | tf_op jit(solution)/shard_map/ppermute | solution.py:72
  62.6 0.9 collective-permute-start.17
  63.5 4.5 %collective-permute-done.15.x1 = bf16[512,256]{1,0:T(8,128)(2,1)S(1)} collective-permute-done((bf16[512,256]{1,0:T(8,128)(2,1)S(1)}, bf16[512,256]{1,0:T(8,128)(2,1)S(1)}, u32[]{:S(2)}, u32[]{:S(2)}) %collective-permute-start.15) | collective-permute-done | bytes 262176 | tf_op jit(solution)/shard_map/ppermute | solution.py:72
  68.0 5.8 %collective-permute-done.16.x2 = bf16[512,256]{1,0:T(8,128)(2,1)S(1)} collective-permute-done((bf16[512,256]{1,0:T(8,128)(2,1)S(1)}, bf16[512,256]{1,0:T(8,128)(2,1)S(1)}, u32[]{:S(2)}, u32[]{:S(2)}) %collective-permute-start.16) | collective-permute-done | bytes 262176 | tf_op jit(solution)/shard_map/ppermute | solution.py:72
  73.8 2.7 %collective-permute-done.17.x3 = bf16[512,256]{1,0:T(8,128)(2,1)S(1)} collective-permute-done((bf16[512,256]{1,0:T(8,128)(2,1)S(1)}, bf16[512,256]{1,0:T(8,128)(2,1)S(1)}, u32[]{:S(2)}, u32[]{:S(2)}) %collective-permute-start.17) | collective-permute-done | bytes 262176 | tf_op jit(solution)/shard_map/ppermute | solution.py:72
  76.4 0.1 shard_map.64
  76.6 1.3 %collective-permute-start.18 = (f32[256,256]{1,0:T(8,128)S(1)}, f32[256,256]{1,0:T(8,128)S(1)}, u32[]{:S(2)}, u32[]{:S(2)}) collective-permute-start(f32[256,256]{1,0:T(8,128)S(1)} %get-tuple-element.26), channel_id=1, source_target_pairs={{0,4},{1,5},{2,6},{3,7},{4,0},{5,1},{6,2},{7,3},{8,12},{9,13},{10,... | collective-permute-start | bytes 786440 | tf_op jit(solution)/shard_map/ppermute | solution.py:57
  77.9 5.4 %collective-permute-done.18.got = f32[256,256]{1,0:T(8,128)S(1)} collective-permute-done((f32[256,256]{1,0:T(8,128)S(1)}, f32[256,256]{1,0:T(8,128)S(1)}, u32[]{:S(2)}, u32[]{:S(2)}) %collective-permute-start.18) | collective-permute-done | bytes 262176 | tf_op jit(solution)/shard_map/ppermute | solution.py:57
  83.3 2.7 %collective-permute-start.19 = (f32[64,256]{1,0:T(8,128)S(1)}, f32[64,256]{1,0:T(8,128)S(1)}, u32[]{:S(2)}, u32[]{:S(2)}) collective-permute-start(f32[64,256]{1,0:T(8,128)S(1)} %get-tuple-element.28), channel_id=1, source_target_pairs={{0,8},{1,9},{2,10},{3,11},{4,12},{5,13},{6,14},{7,15},{8,0},{9,1},... | collective-permute-start | bytes 196616 | tf_op jit(solution)/shard_map/ppermute | solution.py:57
  85.9 5.8 %collective-permute-start.20 = (f32[64,256]{1,0:T(8,128)S(1)}, f32[64,256]{1,0:T(8,128)S(1)}, u32[]{:S(2)}, u32[]{:S(2)}) collective-permute-start(f32[64,256]{1,0:T(8,128)S(1)} %get-tuple-element.29), channel_id=1, source_target_pairs={{0,16},{1,17},{2,18},{3,19},{4,20},{5,21},{6,22},{7,23},{8,24},{9,... | collective-permute-start | bytes 196616 | tf_op jit(solution)/shard_map/ppermute | solution.py:57
  91.7 0.0 collective-permute-start.21
  91.8 3.4 %collective-permute-done.20.z4 = f32[64,256]{1,0:T(8,128)S(1)} collective-permute-done((f32[64,256]{1,0:T(8,128)S(1)}, f32[64,256]{1,0:T(8,128)S(1)}, u32[]{:S(2)}, u32[]{:S(2)}) %collective-permute-start.20) | collective-permute-done | bytes 65568 | tf_op jit(solution)/shard_map/ppermute | solution.py:57
  95.1 3.4 %collective-permute-done.21.z6 = f32[64,256]{1,0:T(8,128)S(1)} collective-permute-done((f32[64,256]{1,0:T(8,128)S(1)}, f32[64,256]{1,0:T(8,128)S(1)}, u32[]{:S(2)}, u32[]{:S(2)}) %collective-permute-start.21) | collective-permute-done | bytes 65568 | tf_op jit(solution)/shard_map/ppermute | solution.py:57
  98.5 0.6 shard_map.66
  (16 shorter events, 0.2 us)
Async XLA Ops:
  0.0 27.8 %collective-permute-start.10 = (bf16[2,512,256]{2,1,0:T(8,128)(2,1)}, bf16[2,512,256]{2,1,0:T(8,128)(2,1)S(1)}, u32[]{:S(2)}, u32[]{:S(2)}) collective-permute-start(bf16[2,512,256]{2,1,0:T(8,128)(2,1)} %bitcast.8), channel_id=1, source_target_pairs={{0,64},{64,128},{128,192},{192,0},{1,65},{65,129},{129,193},{193,1... | collective-permute-start | bytes 1572872 | tf_op jit(solution)/shard_map/ppermute | solution.py:43
  0.2 29.2 %collective-permute-start.12 = (bf16[2,512,256]{2,1,0:T(8,128)(2,1)}, bf16[2,512,256]{2,1,0:T(8,128)(2,1)S(1)}, u32[]{:S(2)}, u32[]{:S(2)}) collective-permute-start(bf16[2,512,256]{2,1,0:T(8,128)(2,1)} %bitcast.9), channel_id=1, source_target_pairs={{0,192},{64,0},{128,64},{192,128},{1,193},{65,1},{129,65},{193,129... | collective-permute-start | bytes 1572872 | tf_op jit(solution)/shard_map/ppermute | solution.py:43
  2.0 1.0 %copy-start = (bf16[2,1,512,256]{3,2,1,0:T(8,128)(2,1)S(1)}, bf16[2,1,512,256]{3,2,1,0:T(8,128)(2,1)}, u32[]{:S(2)}) copy-start(bf16[2,1,512,256]{3,2,1,0:T(8,128)(2,1)} %param.8) | copy-start | bytes 1572868
  3.1 0.7 copy-start.2
  3.8 28.4 %collective-permute-start.9 = (bf16[2,528,256]{2,1,0:T(8,128)(2,1)S(1)}, bf16[2,528,256]{2,1,0:T(8,128)(2,1)S(1)}, u32[]{:S(2)}, u32[]{:S(2)}) collective-permute-start(bf16[2,528,256]{2,1,0:T(8,128)(2,1)S(1)} %load.1), channel_id=1, source_target_pairs={{0,96},{32,64},{64,160},{96,128},{128,224},{160,192},{192,32},{224... | collective-permute-start | bytes 1622024 | tf_op jit(solution)/shard_map/ppermute | solution.py:52
  5.0 7.2 %collective-permute-start = (bf16[80,256]{1,0:T(8,128)(2,1)S(1)}, bf16[80,256]{1,0:T(8,128)(2,1)S(1)}, u32[]{:S(2)}, u32[]{:S(2)}) collective-permute-start(bf16[80,256]{1,0:T(8,128)(2,1)S(1)} %fusion.1), channel_id=1, source_target_pairs={{0,32},{32,0},{1,33},{33,1},{2,34},{34,2},{3,35},{35,3},{4,36},{36... | collective-permute-start | bytes 122888 | tf_op jit(solution)/shard_map/ppermute | solution.py:39
  6.2 7.7 %collective-permute-start.1 = (bf16[80,256]{1,0:T(8,128)(2,1)S(1)}, bf16[80,256]{1,0:T(8,128)(2,1)S(1)}, u32[]{:S(2)}, u32[]{:S(2)}) collective-permute-start(bf16[80,256]{1,0:T(8,128)(2,1)S(1)} %fusion.1), channel_id=1, source_target_pairs={{0,48},{1,49},{2,50},{3,51},{4,52},{5,53},{6,54},{7,55},{8,56},{9,... | collective-permute-start | bytes 122888 | tf_op jit(solution)/shard_map/ppermute | solution.py:67
  12.2 6.6 %collective-permute-start.2 = (bf16[80,256]{1,0:T(8,128)(2,1)S(1)}, bf16[80,256]{1,0:T(8,128)(2,1)S(1)}, u32[]{:S(2)}, u32[]{:S(2)}) collective-permute-start(bf16[80,256]{1,0:T(8,128)(2,1)S(1)} %fusion.1), channel_id=1, source_target_pairs={{0,40},{1,41},{2,42},{3,43},{4,44},{5,45},{6,46},{7,47},{8,32},{9,... | collective-permute-start | bytes 122888 | tf_op jit(solution)/shard_map/ppermute | solution.py:67
  13.9 6.6 %collective-permute-start.3 = (bf16[80,256]{1,0:T(8,128)(2,1)S(1)}, bf16[80,256]{1,0:T(8,128)(2,1)S(1)}, u32[]{:S(2)}, u32[]{:S(2)}) collective-permute-start(bf16[80,256]{1,0:T(8,128)(2,1)S(1)} %fusion.1), channel_id=1, source_target_pairs={{0,56},{1,57},{2,58},{3,59},{4,60},{5,61},{6,62},{7,63},{8,48},{9,... | collective-permute-start | bytes 122888 | tf_op jit(solution)/shard_map/ppermute | solution.py:67
  20.5 7.0 %collective-permute-start.4 = (bf16[320,256]{1,0:T(8,128)(2,1)S(1)}, bf16[320,256]{1,0:T(8,128)(2,1)S(1)}, u32[]{:S(2)}, u32[]{:S(2)}) collective-permute-start(bf16[320,256]{1,0:T(8,128)(2,1)S(1)} %join.1.a), channel_id=1, source_target_pairs={{0,4},{1,5},{2,6},{3,7},{4,0},{5,1},{6,2},{7,3},{8,12},{9,13},{10,... | collective-permute-start | bytes 491528 | tf_op jit(solution)/shard_map/ppermute | solution.py:57
  22.5 15.3 %collective-permute-start.11 = (bf16[2,528,256]{2,1,0:T(8,128)(2,1)S(1)}, bf16[2,528,256]{2,1,0:T(8,128)(2,1)S(1)}, u32[]{:S(2)}, u32[]{:S(2)}) collective-permute-start(bf16[2,528,256]{2,1,0:T(8,128)(2,1)S(1)} %load.1), channel_id=1, source_target_pairs={{0,224},{32,192},{64,32},{96,0},{128,96},{160,64},{192,160},{224,1... | collective-permute-start | bytes 1622024 | tf_op jit(solution)/shard_map/ppermute | solution.py:52
  27.5 17.0 %collective-permute-start.8 = (bf16[2,528,256]{2,1,0:T(8,128)(2,1)S(1)}, bf16[2,528,256]{2,1,0:T(8,128)(2,1)S(1)}, u32[]{:S(2)}, u32[]{:S(2)}) collective-permute-start(bf16[2,528,256]{2,1,0:T(8,128)(2,1)S(1)} %load.1), channel_id=1, source_target_pairs={{0,32},{32,0},{1,33},{33,1},{2,34},{34,2},{3,35},{35,3},{4,36},{36... | collective-permute-start | bytes 1622024 | tf_op jit(solution)/shard_map/ppermute | solution.py:39
  27.8 10.0 %collective-permute-start.5 = (bf16[528,256]{1,0:T(8,128)(2,1)S(1)}, bf16[528,256]{1,0:T(8,128)(2,1)S(1)}, u32[]{:S(2)}, u32[]{:S(2)}) collective-permute-start(bf16[528,256]{1,0:T(8,128)(2,1)S(1)} %pack.1.s0), channel_id=1, source_target_pairs={{0,1},{1,2},{2,3},{3,0},{4,5},{5,6},{6,7},{7,4},{8,9},{9,10},{10,1... | collective-permute-start | bytes 811016 | tf_op jit(solution)/shard_map/ppermute | solution.py:77
  29.4 15.1 %collective-permute-start.6 = (bf16[528,256]{1,0:T(8,128)(2,1)S(1)}, bf16[528,256]{1,0:T(8,128)(2,1)S(1)}, u32[]{:S(2)}, u32[]{:S(2)}) collective-permute-start(bf16[528,256]{1,0:T(8,128)(2,1)S(1)} %pack.1.s0), channel_id=1, source_target_pairs={{0,2},{1,3},{2,0},{3,1},{4,6},{5,7},{6,4},{7,5},{8,10},{9,11},{10,... | collective-permute-start | bytes 811016 | tf_op jit(solution)/shard_map/ppermute | solution.py:77
  32.1 12.4 %collective-permute-start.7 = (bf16[528,256]{1,0:T(8,128)(2,1)S(1)}, bf16[528,256]{1,0:T(8,128)(2,1)S(1)}, u32[]{:S(2)}, u32[]{:S(2)}) collective-permute-start(bf16[528,256]{1,0:T(8,128)(2,1)S(1)} %pack.1.s0), channel_id=1, source_target_pairs={{0,3},{1,0},{2,1},{3,2},{4,7},{5,4},{6,5},{7,6},{8,11},{9,8},{10,9... | collective-permute-start | bytes 811016 | tf_op jit(solution)/shard_map/ppermute | solution.py:77
  33.6 6.3 %copy-start.1 = (s32[2,512,16]{1,2,0:T(8,128)S(1)}, s32[2,512,16]{1,2,0:T(8,128)}, u32[]{:S(2)}) copy-start(s32[2,512,16]{1,2,0:T(8,128)} %param.11) | copy-start | bytes 196612
  33.6 10.9 %copy-start.3 = (bf16[2,1,512,256]{3,2,1,0:T(8,128)(2,1)S(1)}, bf16[2,1,512,256]{3,2,1,0:T(8,128)(2,1)}, u32[]{:S(2)}) copy-start(bf16[2,1,512,256]{3,2,1,0:T(8,128)(2,1)} %param.10) | copy-start | bytes 1572868
  37.8 16.6 %collective-permute-start.13 = (bf16[1040,256]{1,0:T(8,128)(2,1)S(1)}, bf16[1040,256]{1,0:T(8,128)(2,1)S(1)}, u32[]{:S(2)}, u32[]{:S(2)}) collective-permute-start(bf16[1040,256]{1,0:T(8,128)(2,1)S(1)} %relay.2), channel_id=1, source_target_pairs={{0,64},{64,128},{128,192},{192,0},{1,65},{65,129},{129,193},{193,1... | collective-permute-start | bytes 1597448 | tf_op jit(solution)/shard_map/ppermute | solution.py:43
  37.9 16.6 %collective-permute-start.14 = (bf16[1040,256]{1,0:T(8,128)(2,1)S(1)}, bf16[1040,256]{1,0:T(8,128)(2,1)S(1)}, u32[]{:S(2)}, u32[]{:S(2)}) collective-permute-start(bf16[1040,256]{1,0:T(8,128)(2,1)S(1)} %relay.3), channel_id=1, source_target_pairs={{0,192},{64,0},{128,64},{192,128},{1,193},{65,1},{129,65},{193,129... | collective-permute-start | bytes 1597448 | tf_op jit(solution)/shard_map/ppermute | solution.py:43
  58.7 9.3 %collective-permute-start.15 = (bf16[512,256]{1,0:T(8,128)(2,1)S(1)}, bf16[512,256]{1,0:T(8,128)(2,1)S(1)}, u32[]{:S(2)}, u32[]{:S(2)}) collective-permute-start(bf16[512,256]{1,0:T(8,128)(2,1)S(1)} %get-tuple-element.22), channel_id=1, source_target_pairs={{0,1},{1,0},{2,3},{3,2},{4,5},{5,4},{6,7},{7,6},{8,9},{9,8},{10,11... | collective-permute-start | bytes 786440 | tf_op jit(solution)/shard_map/ppermute | solution.py:72
  59.5 14.2 %collective-permute-start.16 = (bf16[512,256]{1,0:T(8,128)(2,1)S(1)}, bf16[512,256]{1,0:T(8,128)(2,1)S(1)}, u32[]{:S(2)}, u32[]{:S(2)}) collective-permute-start(bf16[512,256]{1,0:T(8,128)(2,1)S(1)} %get-tuple-element.23), channel_id=1, source_target_pairs={{0,2},{1,3},{2,0},{3,1},{4,6},{5,7},{6,4},{7,5},{8,10},{9,11},{10,... | collective-permute-start | bytes 786440 | tf_op jit(solution)/shard_map/ppermute | solution.py:72
  62.6 13.8 %collective-permute-start.17 = (bf16[512,256]{1,0:T(8,128)(2,1)S(1)}, bf16[512,256]{1,0:T(8,128)(2,1)S(1)}, u32[]{:S(2)}, u32[]{:S(2)}) collective-permute-start(bf16[512,256]{1,0:T(8,128)(2,1)S(1)} %get-tuple-element.24), channel_id=1, source_target_pairs={{0,3},{1,2},{2,1},{3,0},{4,7},{5,6},{6,5},{7,4},{8,11},{9,10},{10,... | collective-permute-start | bytes 786440 | tf_op jit(solution)/shard_map/ppermute | solution.py:72
  76.6 6.7 %collective-permute-start.18 = (f32[256,256]{1,0:T(8,128)S(1)}, f32[256,256]{1,0:T(8,128)S(1)}, u32[]{:S(2)}, u32[]{:S(2)}) collective-permute-start(f32[256,256]{1,0:T(8,128)S(1)} %get-tuple-element.26), channel_id=1, source_target_pairs={{0,4},{1,5},{2,6},{3,7},{4,0},{5,1},{6,2},{7,3},{8,12},{9,13},{10,... | collective-permute-start | bytes 786440 | tf_op jit(solution)/shard_map/ppermute | solution.py:57
  83.3 8.5 %collective-permute-start.19 = (f32[64,256]{1,0:T(8,128)S(1)}, f32[64,256]{1,0:T(8,128)S(1)}, u32[]{:S(2)}, u32[]{:S(2)}) collective-permute-start(f32[64,256]{1,0:T(8,128)S(1)} %get-tuple-element.28), channel_id=1, source_target_pairs={{0,8},{1,9},{2,10},{3,11},{4,12},{5,13},{6,14},{7,15},{8,0},{9,1},... | collective-permute-start | bytes 196616 | tf_op jit(solution)/shard_map/ppermute | solution.py:57
  85.9 9.2 %collective-permute-start.20 = (f32[64,256]{1,0:T(8,128)S(1)}, f32[64,256]{1,0:T(8,128)S(1)}, u32[]{:S(2)}, u32[]{:S(2)}) collective-permute-start(f32[64,256]{1,0:T(8,128)S(1)} %get-tuple-element.29), channel_id=1, source_target_pairs={{0,16},{1,17},{2,18},{3,19},{4,20},{5,21},{6,22},{7,23},{8,24},{9,... | collective-permute-start | bytes 196616 | tf_op jit(solution)/shard_map/ppermute | solution.py:57
  91.7 6.8 %collective-permute-start.21 = (f32[64,256]{1,0:T(8,128)S(1)}, f32[64,256]{1,0:T(8,128)S(1)}, u32[]{:S(2)}, u32[]{:S(2)}) collective-permute-start(f32[64,256]{1,0:T(8,128)S(1)} %get-tuple-element.30), channel_id=1, source_target_pairs={{0,24},{1,25},{2,26},{3,27},{4,28},{5,29},{6,30},{7,31},{8,16},{9,... | collective-permute-start | bytes 196616 | tf_op jit(solution)/shard_map/ppermute | solution.py:57

commit v3 on v2

v3 whole, which is shorter than its diff:
```python
import functools
import math

import jax
import jax.numpy as jnp
from jax import lax
from jax.experimental import pallas as pl
from jax.experimental.pallas import tpu as pltpu
from jax.sharding import PartitionSpec as P


BATCHES = 2
ROWS, HALVES, OBS = 4, 2, 32
NX, NZ = 4, 8
EDGE = 128
SHARD = 64
MEMBERS = 256
RANGE_BLOCKS = 16
SPAN = 4
NAMED = 16
OBS_ROWS = SPAN * EDGE
PAD = 16
Z_ORDER = (0, 4, 2, 6, 1, 5, 3, 7)

GROUP = 4
SPANS = 8
SOURCES = 5
PICKS = 24
META = SOURCES * 2 * PICKS
TOTALS = META + SOURCES * 2 * 8
KEYS = RANGE_BLOCKS + 2
TURNS = 0b10_01_11_00
DEAD = -1e30
LIVE = math.log2(1.0 / (MEMBERS - 1))
STRETCH = 2.0 * math.sqrt(math.log2(math.e))

VMEM = pl.BlockSpec(memory_space=pltpu.VMEM)
SMEM = pl.BlockSpec(memory_space=pltpu.SMEM)


def flip(value):
    return lax.ppermute(value, "half", [(0, 1), (1, 0)])


def along_rows(value, step):
    return lax.ppermute(value, "rows", [(s, (s + step) % ROWS) for s in range(ROWS)])


def along_rows_flip(value, step):
    pairs = [
        (r * HALVES + h, ((r + step) % ROWS) * HALVES + 1 - h)
        for r in range(ROWS)
        for h in range(HALVES)
    ]
    return lax.ppermute(value, ("rows", "half"), pairs)


def swap_z(value, mask):
    pairs = [(z * NX + x, (z ^ mask) * NX + x) for z in range(NZ) for x in range(NX)]
    return lax.ppermute(value, "obs", pairs)


def swap_z_flip(value, mask):
    pairs = [
        (h * OBS + z * NX + x, (1 - h) * OBS + (z ^ mask) * NX + x)
        for h in range(HALVES)
        for z in range(NZ)
        for x in range(NX)
    ]
    return lax.ppermute(value, ("half", "obs"), pairs)


def swap_x(value, mask):
    pairs = [(z * NX + x, z * NX + (x ^ mask)) for z in range(NZ) for x in range(NX)]
    return lax.ppermute(value, "obs", pairs)


def lists_kernel(named_ref, lists, shifts, used):
    row, column = lax.axis_index("rows"), lax.axis_index("obs")
    first = row * RANGE_BLOCKS

    def span(n, carry):
        near_side = n < 6
        source = jnp.where(near_side, lax.shift_right_logical(n, 1), n - 3)
        local_t = jnp.where(near_side, jnp.bitwise_and(n, 1), 0)
        turn = jnp.bitwise_and(
            lax.shift_right_logical(TURNS, 2 * lax.shift_right_logical(n, 1)), ROWS - 1
        )
        place = (jnp.bitwise_and(row + turn, ROWS - 1) * OBS + column) * SPAN
        batch = jnp.bitwise_and(n, 1)
        key = n * KEYS
        for k in range(KEYS):
            used[key + k] = 0
            for j in range(SPAN):
                shifts[(key + k) * SPAN + j] = DEAD
        for j in range(SPAN):
            for e in range(NAMED):
                relative = named_ref[batch, e, place + j] - first
                inside = jnp.bitwise_and(relative, -RANGE_BLOCKS) == 0
                at = jnp.where(inside, key + relative, SPANS * KEYS)
                used[at] = 1
                shifts[at * SPAN + j] = LIVE
        for parity in range(2):
            r = source * 2 + parity
            before = jnp.where(local_t == 0, 0, lists[TOTALS + r])
            start = r * PICKS + before * GROUP
            write = start
            for z in range(NZ):
                lists[write] = z
                write = write + used[key + 2 * z + parity]
            for k in range(GROUP - 1):
                lists[write + k] = NZ
            visits = lax.shift_right_logical(write - start + GROUP - 1, 2)
            for k in range(2):
                lists[META + r * 8 + before + k] = local_t
            total = before + visits

            @pl.when(total == 0)
            def _(start=start):
                for k in range(GROUP):
                    lists[start + k] = NZ

            last = jnp.logical_or(local_t == 1, jnp.logical_not(near_side))
            lists[TOTALS + r] = jnp.where(last, jnp.maximum(total, 1), total)
        return carry

    lax.fori_loop(0, SPANS, span, 0)


def make_lists(named):
    return pl.pallas_call(
        lists_kernel,
        out_shape=(
            jax.ShapeDtypeStruct((TOTALS + 16,), jnp.int32),
            jax.ShapeDtypeStruct(((SPANS * KEYS + 1) * SPAN,), jnp.float32),
        ),
        in_specs=[SMEM],
        out_specs=(SMEM, SMEM),
        scratch_shapes=[pltpu.SMEM((SPANS * KEYS + 1,), jnp.int32)],
        compiler_params=pltpu.CompilerParams(vmem_limit_bytes=1 << 20),
        cost_estimate=pl.CostEstimate(flops=4_000_000, transcendentals=0, bytes_accessed=4_000_000),
        name="lists",
    )(named)


def tile_loop(segments, parity, state, spot, acc, places, tiles, lists, shifts):
    def chosen(s, g):
        return [lists[(s * 2 + parity) * PICKS + g * GROUP + k] for k in range(GROUP)]

    def batch_of(s, g):
        return lists[META + (s * 2 + parity) * 8 + g]

    def make(segment, g):
        s, n, rows, obs, _ = segment
        t = batch_of(s, g)
        picks = chosen(s, g)
        gathered = jnp.concatenate(
            [state[pl.ds(2 * z, 2)].reshape(EDGE, MEMBERS) for z in picks], axis=0
        )
        products = lax.dot_general(
            gathered, obs(t), (((1,), (1,)), ((), ())), preferred_element_type=jnp.float32
        )
        for k, z in enumerate(picks):
            key = ((n + t) * KEYS + 2 * z + parity) * SPAN
            positions = spot[pl.ds(2 * z, 2)].reshape(EDGE, EDGE)
            for j in range(SPAN):
                d = positions - places[pl.ds(rows + t * SPAN + j, 1), :]
                part = products[k * EDGE : (k + 1) * EDGE, j * EDGE : (j + 1) * EDGE]
                damped = part * jnp.exp2(shifts[key + j] - d * d)
                tiles[k * EDGE : (k + 1) * EDGE, j * EDGE : (j + 1) * EDGE] = damped.astype(
                    jnp.bfloat16
                )

    def add(segment, g):
        s, weights = segment[0], segment[4]
        added = jnp.dot(
            tiles[...], weights(batch_of(s, g)), preferred_element_type=jnp.float32
        )
        for k, z in enumerate(chosen(s, g)):
            acc[z] += added[k * EDGE : (k + 1) * EDGE]

    before = None
    for segment in segments:
        total = lists[TOTALS + segment[0] * 2 + parity]
        if before is not None:
            add(*before)
        make(segment, 0)

        def step(g, carry, segment=segment):
            add(segment, g - 1)
            make(segment, g)
            return carry

        lax.fori_loop(1, total, step, 0)
        before = (segment, total - 1)
    add(*before)


def spread_places(held, places, start):
    places[start : start + SPAN] = held.astype(jnp.float32)[:SPAN] * STRETCH


def own_place(late):
    column = lax.axis_index("obs")
    my_z = lax.shift_right_logical(column, 2)
    x = jnp.bitwise_xor(jnp.bitwise_and(column, NX - 1), 2 * late)
    return my_z, x


def near_kernel(
    late, lists, shifts, p0, p1, oo, wo, ol, wl, orr, wr, state, spot, acc, places, tiles
):
    my_z, x = own_place(late)
    lanes = lax.broadcasted_iota(jnp.int32, (SHARD, EDGE), 1)
    sublanes = lax.broadcasted_iota(jnp.int32, (SHARD, EDGE), 0)
    same = lanes == sublanes
    ones = jnp.ones((EDGE, EDGE), jnp.bfloat16)
    for k, piece in enumerate((p0, p1)):
        half = jnp.bitwise_and(jnp.bitwise_xor(x, k), 1)
        held = piece[NZ * SHARD : NZ * SHARD + PAD, :EDGE].astype(jnp.float32)
        spread = jnp.concatenate(
            [jnp.where(same, held[p : p + 1], 0.0) for p in range(NZ)], axis=0
        ).astype(jnp.bfloat16)
        columns = jnp.dot(spread, ones, preferred_element_type=jnp.float32) * STRETCH
        for p, mask in enumerate(Z_ORDER):
            at = jnp.bitwise_xor(my_z, mask) * 2 + half
            state[at] = piece[p * SHARD : (p + 1) * SHARD, :]
            spot[at] = columns[p * SHARD : (p + 1) * SHARD]
    state[2 * NZ :] = jnp.zeros((2, SHARD, MEMBERS), jnp.bfloat16)
    spot[2 * NZ :] = jnp.zeros((2, SHARD, EDGE), jnp.float32)
    acc[...] = jnp.zeros_like(acc)
    segments = []
    for s, (o, w) in enumerate(((oo, wo), (ol, wl), (orr, wr))):
        for t in range(BATCHES):
            spread_places(o[t, OBS_ROWS : OBS_ROWS + PAD, :EDGE], places, s * 8 + t * SPAN)
        segments.append(
            (s, 2 * s, 8 * s, lambda t, o=o: o[t, :OBS_ROWS, :], lambda t, w=w: w[t])
        )
    parity = lax.shift_right_logical(x, 1)
    tile_loop(segments, parity, state, spot, acc, places, tiles, lists, shifts)


SCRATCH = [
    pltpu.VMEM((24, EDGE), jnp.float32),
    pltpu.VMEM((GROUP * EDGE, SPAN * EDGE), jnp.bfloat16),
]


def near(late, lists, arrays):
    return pl.pallas_call(
        functools.partial(near_kernel, late),
        out_shape=(
            jax.ShapeDtypeStruct((2 * NZ + 2, SHARD, MEMBERS), jnp.bfloat16),
            jax.ShapeDtypeStruct((2 * NZ + 2, SHARD, EDGE), jnp.float32),
            jax.ShapeDtypeStruct((NZ + 1, EDGE, MEMBERS), jnp.float32),
        ),
        in_specs=[SMEM, SMEM] + [VMEM] * 8,
        out_specs=(VMEM,) * 3,
        scratch_shapes=SCRATCH,
        compiler_params=pltpu.CompilerParams(vmem_limit_bytes=16 << 20),
        cost_estimate=pl.CostEstimate(
            flops=2_000_000_000, transcendentals=2_000_000, bytes_accessed=4_000_000
        ),
        name="near_late" if late else "near_early",
    )(*lists, *arrays)


def far_kernel(
    late, lists, shifts, state, spot, near_acc, left, right, r0, r1, places, tiles, acc
):
    acc[...] = near_acc[...]
    segments = []
    for k, both in enumerate((left, right)):
        spread_places(both[OBS_ROWS : OBS_ROWS + PAD, :EDGE], places, 8 * k)
        segments.append(
            (
                3 + k, 6 + k, 8 * k, lambda t, both=both: both[:OBS_ROWS, :],
                lambda t, both=both: both[OBS_ROWS + PAD :, :],
            )
        )
    _, x = own_place(late)
    parity = lax.shift_right_logical(x, 1)
    tile_loop(segments, parity, state, spot, acc, places, tiles, lists, shifts)
    for k, out in enumerate((r0, r1)):
        half = jnp.bitwise_and(jnp.bitwise_xor(x, k), 1)
        start = pl.multiple_of(half * SHARD, SHARD)
        for z in range(NZ):
            out[z * SHARD : (z + 1) * SHARD] = acc[z, pl.ds(start, SHARD), :].astype(out.dtype)


def far(late, lists, state, spot, acc, arrays):
    rows = NZ * SHARD
    return pl.pallas_call(
        functools.partial(far_kernel, late),
        out_shape=(
            jax.ShapeDtypeStruct((rows, MEMBERS), jnp.bfloat16 if late else jnp.float32),
            jax.ShapeDtypeStruct((rows, MEMBERS), jnp.bfloat16),
        ),
        in_specs=[SMEM, SMEM] + [VMEM] * 5,
        out_specs=(VMEM, VMEM),
        scratch_shapes=SCRATCH + [pltpu.VMEM((NZ + 1, EDGE, MEMBERS), jnp.float32)],
        compiler_params=pltpu.CompilerParams(vmem_limit_bytes=16 << 20),
        cost_estimate=pl.CostEstimate(
            flops=500_000_000, transcendentals=500_000, bytes_accessed=4_000_000
        ),
        name="far_late" if late else "far_early",
    )(*lists, state, spot, acc, *arrays)


def sum_x_kernel(own, x1, x2, x3, keep, send):
    my_z = lax.shift_right_logical(lax.axis_index("obs"), 2)
    for mask in range(NZ):
        rows = pl.ds(pl.multiple_of(jnp.bitwise_xor(my_z, mask) * SHARD, SHARD), SHARD)
        total = own[rows, :]
        for ref in (x1, x2, x3):
            total += ref[rows, :].astype(jnp.float32)
        out, k = (send if mask & 1 else keep), mask // 2
        out[k * SHARD : (k + 1) * SHARD] = total


def sum_z1_kernel(keep, got, own, z2, z4, z6):
    for k, out in enumerate((own, z2, z4, z6)):
        rows = slice(k * SHARD, (k + 1) * SHARD)
        out[...] = keep[rows] + got[rows]


def sum_z_kernel(own, z2, z4, z6, out):
    out[...] = own[...] + z2[...] + z4[...] + z6[...]


def small(body, out_rows, *arrays):
    return pl.pallas_call(
        body,
        out_shape=tuple(jax.ShapeDtypeStruct((r, MEMBERS), jnp.float32) for r in out_rows),
        in_specs=[VMEM] * len(arrays),
        out_specs=(VMEM,) * len(out_rows),
        compiler_params=pltpu.CompilerParams(vmem_limit_bytes=6 << 20),
    )(*arrays)


def pack_kernel(a, b, out):
    held = SHARD + PAD
    places = []
    for p in range(NZ):
        ref, q = (a, p) if p < NZ // 2 else (b, p - NZ // 2)
        out[p * SHARD : (p + 1) * SHARD] = ref[q * held : q * held + SHARD]
        places.append(ref[q * held + SHARD : (q + 1) * held].astype(jnp.float32)[:1])
    places.append(jnp.zeros((PAD - NZ, MEMBERS), jnp.float32))
    out[NZ * SHARD :] = jnp.concatenate(places, axis=0).astype(jnp.bfloat16)


def pack(a, b):
    return pl.pallas_call(
        pack_kernel,
        out_shape=jax.ShapeDtypeStruct((NZ * SHARD + PAD, MEMBERS), jnp.bfloat16),
        in_specs=[VMEM, VMEM],
        out_specs=VMEM,
        compiler_params=pltpu.CompilerParams(vmem_limit_bytes=4 << 20),
        name="pack",
    )(a, b)


def join_kernel(*refs):
    out = refs[-1]
    start = 0
    for ref in refs[:-1]:
        out[start : start + ref.shape[0]] = ref[...]
        start += ref.shape[0]


def join(*parts):
    rows = sum(part.shape[0] for part in parts)
    return pl.pallas_call(
        join_kernel,
        out_shape=jax.ShapeDtypeStruct((rows, MEMBERS), jnp.bfloat16),
        in_specs=[VMEM] * len(parts),
        out_specs=VMEM,
        compiler_params=pltpu.CompilerParams(vmem_limit_bytes=4 << 20),
        name="join",
    )(*parts)


def load_kernel(obs, places, out):
    for t in range(BATCHES):
        out[t, :OBS_ROWS] = obs[t]
        held = places[t : t + 1].astype(jnp.float32)
        rows = [held[:, r * EDGE : (r + 1) * EDGE] for r in range(SPAN)]
        rows.append(jnp.zeros((PAD - SPAN, EDGE), jnp.float32))
        out[t, OBS_ROWS:, :EDGE] = jnp.concatenate(rows, axis=0).astype(jnp.bfloat16)
        out[t, OBS_ROWS:, EDGE:] = jnp.zeros((PAD, MEMBERS - EDGE), jnp.bfloat16)


def load(obs, places):
    return pl.pallas_call(
        load_kernel,
        out_shape=jax.ShapeDtypeStruct((BATCHES, OBS_ROWS + PAD, MEMBERS), jnp.bfloat16),
        in_specs=[VMEM, VMEM],
        out_specs=VMEM,
        compiler_params=pltpu.CompilerParams(vmem_limit_bytes=8 << 20),
        name="load",
    )(obs, places)


def relay_kernel(batch, obs, weights, out):
    out[: OBS_ROWS + PAD] = obs[batch]
    out[OBS_ROWS + PAD :] = weights[batch]


def relay(batch, obs, weights):
    return pl.pallas_call(
        functools.partial(relay_kernel, batch),
        out_shape=jax.ShapeDtypeStruct((2 * OBS_ROWS + PAD, MEMBERS), jnp.bfloat16),
        in_specs=[VMEM, VMEM],
        out_specs=VMEM,
        compiler_params=pltpu.CompilerParams(vmem_limit_bytes=8 << 20),
        name="relay",
    )(obs, weights)


def local(ens_state, state_pos, obs_ens, obs_pos, innov_weight, block_rows):
    state = jnp.concatenate(
        [ens_state[0], jnp.pad(state_pos[None, :], ((0, PAD - 1), (0, MEMBERS - SHARD)))], axis=0
    )
    mine = flip(state)
    parts = [mine]
    for mask in (4, 2, 6):
        parts.append(swap_z_flip(state, mask))
    state = join(*parts)
    other = swap_z(state, 1)
    state = pack(state, other)
    pieces = [state]
    for k in range(1, NX):
        pieces.append(swap_x(state, k))

    weight = innov_weight[:, 0]
    weight_left = along_rows(weight, 1)
    weight_right = along_rows(weight, ROWS - 1)
    obs = load(obs_ens[:, 0], obs_pos)
    obs_left = along_rows_flip(obs, 1)
    obs_right = along_rows_flip(obs, ROWS - 1)
    obs_own = flip(obs)
    far0 = relay(0, obs_left, weight_left)
    far0 = along_rows(far0, 1)
    far1 = relay(1, obs_right, weight_right)
    far1 = along_rows(far1, ROWS - 1)

    lists = make_lists(jnp.transpose(block_rows, (0, 2, 1)))
    seen = (obs_own, weight, obs_left, weight_left, obs_right, weight_right)
    early = near(0, lists, (pieces[0], pieces[1], *seen))
    later = near(1, lists, (pieces[2], pieces[3], *seen))
    part2, part3 = far(1, lists, *later, (far0, far1))
    part2 = swap_x(part2, 2)
    part3 = swap_x(part3, 3)
    own, part1 = far(0, lists, *early, (far0, far1))
    part1 = swap_x(part1, 1)
    parts = [part1, part2, part3]
    keep, send = small(sum_x_kernel, (4 * SHARD, 4 * SHARD), own, *parts)
    got = swap_z(send, 1)
    own, *parts = small(sum_z1_kernel, (SHARD,) * 4, keep, got)
    for k, mask in ((1, 4), (0, 2), (2, 6)):
        parts[k] = swap_z(parts[k], mask)
    (total,) = small(sum_z_kernel, (SHARD,), own, *parts)
    return total[None]


def solution(mesh):
    in_specs = (
        P("half", ("rows", "obs"), None),
        P(("rows", "obs")),
        P(None, "half", ("rows", "obs"), None),
        P(None, ("rows", "obs")),
        P(None, "half", ("rows", "obs"), None),
        P(),
    )
    out_specs = P("half", ("rows", "obs"), None)
    return jax.shard_map(local, mesh=mesh, in_specs=in_specs, out_specs=out_specs, check_vma=False)
```

time: 99.4 us -> 108 us (1.087)
  the two profiles are of different devices: /device:TPU:56 before, /device:TPU:1 now
where the time goes in v3:
time: 108 us; the launch traced here: 107 us
  waiting for transfers between devices  48.5 us (45%)
  starting transfers between devices  33.3 us (31%)
  Pallas kernels  22.7 us (21%)
  local copies, waits for them, and re-layouts  1.73 us (2%)
    pallas_call x2, Pallas kernels, near(): pl.pallas_call(functools.partial(near_kernel, late), out_shape=(jax.Shape...  12.1 us
    ppermute x4, waiting for transfers between devices, along_rows(): lax.ppermute(value, 'rows', [(s, (s + step) % ROWS) for s in range(ROWS)])  11.7 us
    ppermute x5, waiting for transfers between devices, swap_z(): return lax.ppermute(value, 'obs', pairs)  10.8 us
    ppermute x6, waiting for transfers between devices, swap_x(): return lax.ppermute(value, 'obs', pairs)  10.7 us
    ppermute x2, waiting for transfers between devices, along_rows_flip(): return lax.ppermute(value, ('rows', 'half'), pairs)  9.73 us
    ppermute x3, starting transfers between devices, swap_z_flip(): return lax.ppermute(value, ('half', 'obs'), pairs)  8.25 us
    ppermute x6, starting transfers between devices, swap_x(): return lax.ppermute(value, 'obs', pairs)  7.78 us
    ppermute x5, starting transfers between devices, swap_z(): return lax.ppermute(value, 'obs', pairs)  7.39 us
  transfers between devices with their start and end apart: 22, of which 11 were waited for; matrix products, arithmetic and copies ran while one was open for 1% of the time, Pallas kernels for 18%

profile of v3, /device:TPU:1, one launch (start us, length us, event | category | flops | bytes accessed | tf_op | source)
XLA Modules:
  0.0 107.2 jit_solution(3399671435897078610)
XLA Ops:
  0.0 2.1 %collective-permute-start.8 = (bf16[2,512,256]{2,1,0:T(8,128)(2,1)}, bf16[2,512,256]{2,1,0:T(8,128)(2,1)S(1)}, u32[]{:S(2)}, u32[]{:S(2)}) collective-permute-start(bf16[2,512,256]{2,1,0:T(8,128)(2,1)} %bitcast.8), channel_id=1, source_target_pairs={{0,64},{64,128},{128,192},{192,0},{1,65},{65,129},{129,193},{193,1... | collective-permute-start | bytes 1572872 | tf_op jit(solution)/shard_map/ppermute | solution.py:46
  2.1 0.8 fusion.1
  2.9 1.1 %collective-permute-start = (bf16[80,256]{1,0:T(8,128)(2,1)S(1)}, bf16[80,256]{1,0:T(8,128)(2,1)S(1)}, u32[]{:S(2)}, u32[]{:S(2)}) collective-permute-start(bf16[80,256]{1,0:T(8,128)(2,1)S(1)} %fusion.1), channel_id=1, source_target_pairs={{0,32},{32,0},{1,33},{33,1},{2,34},{34,2},{3,35},{35,3},{4,36},{36... | collective-permute-start | bytes 122888 | tf_op jit(solution)/shard_map/ppermute | solution.py:42
  4.0 6.8 %collective-permute-start.1 = (bf16[80,256]{1,0:T(8,128)(2,1)S(1)}, bf16[80,256]{1,0:T(8,128)(2,1)S(1)}, u32[]{:S(2)}, u32[]{:S(2)}) collective-permute-start(bf16[80,256]{1,0:T(8,128)(2,1)S(1)} %fusion.1), channel_id=1, source_target_pairs={{0,48},{1,49},{2,50},{3,51},{4,52},{5,53},{6,54},{7,55},{8,56},{9,... | collective-permute-start | bytes 122888 | tf_op jit(solution)/shard_map/ppermute | solution.py:70
  10.7 1.5 %collective-permute-start.2 = (bf16[80,256]{1,0:T(8,128)(2,1)S(1)}, bf16[80,256]{1,0:T(8,128)(2,1)S(1)}, u32[]{:S(2)}, u32[]{:S(2)}) collective-permute-start(bf16[80,256]{1,0:T(8,128)(2,1)S(1)} %fusion.1), channel_id=1, source_target_pairs={{0,40},{1,41},{2,42},{3,43},{4,44},{5,45},{6,46},{7,47},{8,32},{9,... | collective-permute-start | bytes 122888 | tf_op jit(solution)/shard_map/ppermute | solution.py:70
  12.2 0.0 collective-permute-start.3
  12.2 0.0 collective-permute-done.refs_0_
  12.2 0.4 collective-permute-done.1.refs_1_
  12.7 3.6 %collective-permute-done.2.refs_2_ = bf16[80,256]{1,0:T(8,128)(2,1)S(1)} collective-permute-done((bf16[80,256]{1,0:T(8,128)(2,1)S(1)}, bf16[80,256]{1,0:T(8,128)(2,1)S(1)}, u32[]{:S(2)}, u32[]{:S(2)}) %collective-permute-start.2) | collective-permute-done | bytes 40992 | tf_op jit(solution)/shard_map/ppermute | solution.py:70
  16.2 1.5 %collective-permute-done.3.refs_3_ = bf16[80,256]{1,0:T(8,128)(2,1)S(1)} collective-permute-done((bf16[80,256]{1,0:T(8,128)(2,1)S(1)}, bf16[80,256]{1,0:T(8,128)(2,1)S(1)}, u32[]{:S(2)}, u32[]{:S(2)}) %collective-permute-start.3) | collective-permute-done | bytes 40992 | tf_op jit(solution)/shard_map/ppermute | solution.py:70
  17.8 1.5 %collective-permute-start.4 = (bf16[320,256]{1,0:T(8,128)(2,1)S(1)}, bf16[320,256]{1,0:T(8,128)(2,1)S(1)}, u32[]{:S(2)}, u32[]{:S(2)}) collective-permute-start(bf16[320,256]{1,0:T(8,128)(2,1)S(1)} %join.1.a), channel_id=1, source_target_pairs={{0,4},{1,5},{2,6},{3,7},{4,0},{5,1},{6,2},{7,3},{8,12},{9,13},{10,... | collective-permute-start | bytes 491528 | tf_op jit(solution)/shard_map/ppermute | solution.py:60
  19.3 1.0 copy-done
  20.4 0.7 copy-done.2
  21.1 0.9 collective-permute-start.7
  22.0 2.1 %collective-permute-start.9 = (bf16[2,528,256]{2,1,0:T(8,128)(2,1)S(1)}, bf16[2,528,256]{2,1,0:T(8,128)(2,1)S(1)}, u32[]{:S(2)}, u32[]{:S(2)}) collective-permute-start(bf16[2,528,256]{2,1,0:T(8,128)(2,1)S(1)} %load.1), channel_id=1, source_target_pairs={{0,224},{32,192},{64,32},{96,0},{128,96},{160,64},{192,160},{224,1... | collective-permute-start | bytes 1622024 | tf_op jit(solution)/shard_map/ppermute | solution.py:55
  24.1 0.2 collective-permute-start.10
  24.3 0.5 collective-permute-start.6
  24.9 1.3 %collective-permute-start.5 = (bf16[528,256]{1,0:T(8,128)(2,1)S(1)}, bf16[528,256]{1,0:T(8,128)(2,1)S(1)}, u32[]{:S(2)}, u32[]{:S(2)}) collective-permute-start(bf16[528,256]{1,0:T(8,128)(2,1)S(1)} %pack.1.p0), channel_id=1, source_target_pairs={{0,1},{1,0},{2,3},{3,2},{4,5},{5,4},{6,7},{7,6},{8,9},{9,8},{10,11... | collective-permute-start | bytes 811016 | tf_op jit(solution)/shard_map/ppermute | solution.py:75
  26.2 9.7 %collective-permute-done.7.ol.obs = bf16[2,528,256]{2,1,0:T(8,128)(2,1)S(1)} collective-permute-done((bf16[2,528,256]{2,1,0:T(8,128)(2,1)S(1)}, bf16[2,528,256]{2,1,0:T(8,128)(2,1)S(1)}, u32[]{:S(2)}, u32[]{:S(2)}) %collective-permute-start.7) | collective-permute-done | bytes 540704 | tf_op jit(solution)/shard_map/ppermute | solution.py:55
  36.0 0.0 copy-start.1
  36.0 0.0 copy-start.3
  36.0 0.5 collective-permute-start.11
  36.4 11.7 %collective-permute-done.10.wr.weights = bf16[2,512,256]{2,1,0:T(8,128)(2,1)S(1)} collective-permute-done((bf16[2,512,256]{2,1,0:T(8,128)(2,1)}, bf16[2,512,256]{2,1,0:T(8,128)(2,1)S(1)}, u32[]{:S(2)}, u32[]{:S(2)}) %collective-permute-start.10) | collective-permute-done | bytes 524320 | tf_op jit(solution)/shard_map/ppermute | solution.py:46
  48.2 2.5 %collective-permute-start.12 = (bf16[1040,256]{1,0:T(8,128)(2,1)S(1)}, bf16[1040,256]{1,0:T(8,128)(2,1)S(1)}, u32[]{:S(2)}, u32[]{:S(2)}) collective-permute-start(bf16[1040,256]{1,0:T(8,128)(2,1)S(1)} %relay.3), channel_id=1, source_target_pairs={{0,192},{64,0},{128,64},{192,128},{1,193},{65,1},{129,65},{193,129... | collective-permute-start | bytes 1597448 | tf_op jit(solution)/shard_map/ppermute | solution.py:46
  50.7 2.7 %collective-permute-start.14 = (bf16[528,256]{1,0:T(8,128)(2,1)S(1)}, bf16[528,256]{1,0:T(8,128)(2,1)S(1)}, u32[]{:S(2)}, u32[]{:S(2)}) collective-permute-start(bf16[528,256]{1,0:T(8,128)(2,1)S(1)} %pack.1.p0), channel_id=1, source_target_pairs={{0,2},{1,3},{2,0},{3,1},{4,6},{5,7},{6,4},{7,5},{8,10},{9,11},{10,... | collective-permute-start | bytes 811016 | tf_op jit(solution)/shard_map/ppermute | solution.py:75
  53.4 0.0 collective-permute-done.5.p1
  53.4 0.9 collective-permute-start.15
  54.3 5.1 %lists.1 = (s32[336]{0:T(512)S(1)}, f32[580]{0:T(1024)S(1)}) custom-call(s32[2,16,512]{2,1,0:T(8,128)S(1)} %bitcast.7), custom_call_target="tpu_custom_call" | custom-call | flops 4000000 | bytes 4000000 | tf_op jit(solution)/shard_map/lists/pallas_call | solution.py:131
  59.4 6.2 %near_early.1 = (bf16[18,64,256]{2,1,0:T(8,128)(2,1)S(1)}, f32[18,64,128]{2,1,0:T(8,128)S(1)}, f32[9,128,256]{2,1,0:T(8,128)S(1)}) custom-call(s32[336]{0:T(512)S(1)} %get-tuple-element.23.lists, f32[580]{0:T(1024)S(1)} %get-tuple-element.24.shifts, bf16[528,256]{1,0:T(8,128)(2,1)S(1)} %pack.1.p0, bf16[528,256]{1,0:T(8,128)(2,1)S(1)} %collective-permute-done.5.p1, ...), custom_call_target="tpu_custom_call" | custom-call | flops 2000000000 | bytes 4000000 | tf_op jit(solution)/shard_map/near_early/pallas_call | solution.py:250
  65.5 0.0 collective-permute-done.14.p0
  65.6 0.8 collective-permute-done.15.p1
  66.4 6.0 %near_late.1 = (bf16[18,64,256]{2,1,0:T(8,128)(2,1)S(1)}, f32[18,64,128]{2,1,0:T(8,128)S(1)}, f32[9,128,256]{2,1,0:T(8,128)S(1)}) custom-call(s32[336]{0:T(512)S(1)} %get-tuple-element.23.lists, f32[580]{0:T(1024)S(1)} %get-tuple-element.24.shifts, bf16[528,256]{1,0:T(8,128)(2,1)S(1)} %collective-permute-done.14.p0, ...), custom_call_target="tpu_custom_call" | custom-call | flops 2000000000 | bytes 4000000 | tf_op jit(solution)/shard_map/near_late/pallas_call | solution.py:250
  72.3 2.3 %far_late.1 = (bf16[512,256]{1,0:T(8,128)(2,1)S(1)}, bf16[512,256]{1,0:T(8,128)(2,1)S(1)}) custom-call(s32[336]{0:T(512)S(1)} %get-tuple-element.23.lists, f32[580]{0:T(1024)S(1)} %get-tuple-element.24.shifts, bf16[18,64,256]{2,1,0:T(8,128)(2,1)S(1)} %get-tuple-element.30.state, f32[18,64,128]{2,1,0:T(8,128)S(1)} %get-tuple-element.31.spot, ...), custom_call_target="tpu_custom_call" | custom-call | flops 500000000 | bytes 4000000 | tf_op jit(solution)/shard_map/far_late/pallas_call | solution.py:293
  74.6 0.2 collective-permute-start.16
  74.8 2.6 %collective-permute-start.17 = (bf16[512,256]{1,0:T(8,128)(2,1)S(1)}, bf16[512,256]{1,0:T(8,128)(2,1)S(1)}, u32[]{:S(2)}, u32[]{:S(2)}) collective-permute-start(bf16[512,256]{1,0:T(8,128)(2,1)S(1)} %get-tuple-element.34), channel_id=1, source_target_pairs={{0,3},{1,2},{2,1},{3,0},{4,7},{5,6},{6,5},{7,4},{8,11},{9,10},{10,... | collective-permute-start | bytes 786440 | tf_op jit(solution)/shard_map/ppermute | solution.py:75
  77.4 2.3 %far_early.1 = (f32[512,256]{1,0:T(8,128)S(1)}, bf16[512,256]{1,0:T(8,128)(2,1)S(1)}) custom-call(s32[336]{0:T(512)S(1)} %get-tuple-element.23.lists, f32[580]{0:T(1024)S(1)} %get-tuple-element.24.shifts, bf16[18,64,256]{2,1,0:T(8,128)(2,1)S(1)} %get-tuple-element.25.state, f32[18,64,128]{2,1,0:T(8,128)S(1)} %get-tuple-element.26.spot, ...), custom_call_target="tpu_custom_call" | custom-call | flops 500000000 | bytes 4000000 | tf_op jit(solution)/shard_map/far_early/pallas_call | solution.py:293
  79.7 0.1 collective-permute-start.13
  79.8 3.8 %collective-permute-done.16.x2 = bf16[512,256]{1,0:T(8,128)(2,1)S(1)} collective-permute-done((bf16[512,256]{1,0:T(8,128)(2,1)S(1)}, bf16[512,256]{1,0:T(8,128)(2,1)S(1)}, u32[]{:S(2)}, u32[]{:S(2)}) %collective-permute-start.16) | collective-permute-done | bytes 262176 | tf_op jit(solution)/shard_map/ppermute | solution.py:75
  83.6 6.1 %collective-permute-done.17.x3 = bf16[512,256]{1,0:T(8,128)(2,1)S(1)} collective-permute-done((bf16[512,256]{1,0:T(8,128)(2,1)S(1)}, bf16[512,256]{1,0:T(8,128)(2,1)S(1)}, u32[]{:S(2)}, u32[]{:S(2)}) %collective-permute-start.17) | collective-permute-done | bytes 262176 | tf_op jit(solution)/shard_map/ppermute | solution.py:75
  89.7 0.1 shard_map.64
  89.8 0.1 collective-permute-start.18
  89.9 7.2 %collective-permute-done.18.got = f32[256,256]{1,0:T(8,128)S(1)} collective-permute-done((f32[256,256]{1,0:T(8,128)S(1)}, f32[256,256]{1,0:T(8,128)S(1)}, u32[]{:S(2)}, u32[]{:S(2)}) %collective-permute-start.18) | collective-permute-done | bytes 262176 | tf_op jit(solution)/shard_map/ppermute | solution.py:60
  97.2 0.3 collective-permute-start.19
  97.5 1.8 %collective-permute-start.20 = (f32[64,256]{1,0:T(8,128)S(1)}, f32[64,256]{1,0:T(8,128)S(1)}, u32[]{:S(2)}, u32[]{:S(2)}) collective-permute-start(f32[64,256]{1,0:T(8,128)S(1)} %get-tuple-element.39), channel_id=1, source_target_pairs={{0,16},{1,17},{2,18},{3,19},{4,20},{5,21},{6,22},{7,23},{8,24},{9,... | collective-permute-start | bytes 196616 | tf_op jit(solution)/shard_map/ppermute | solution.py:60
  99.2 3.7 %collective-permute-start.21 = (f32[64,256]{1,0:T(8,128)S(1)}, f32[64,256]{1,0:T(8,128)S(1)}, u32[]{:S(2)}, u32[]{:S(2)}) collective-permute-start(f32[64,256]{1,0:T(8,128)S(1)} %get-tuple-element.40), channel_id=1, source_target_pairs={{0,24},{1,25},{2,26},{3,27},{4,28},{5,29},{6,30},{7,31},{8,16},{9,... | collective-permute-start | bytes 196616 | tf_op jit(solution)/shard_map/ppermute | solution.py:60
  102.9 1.7 %collective-permute-done.20.z4 = f32[64,256]{1,0:T(8,128)S(1)} collective-permute-done((f32[64,256]{1,0:T(8,128)S(1)}, f32[64,256]{1,0:T(8,128)S(1)}, u32[]{:S(2)}, u32[]{:S(2)}) %collective-permute-start.20) | collective-permute-done | bytes 65568 | tf_op jit(solution)/shard_map/ppermute | solution.py:60
  104.6 1.9 %collective-permute-done.21.z6 = f32[64,256]{1,0:T(8,128)S(1)} collective-permute-done((f32[64,256]{1,0:T(8,128)S(1)}, f32[64,256]{1,0:T(8,128)S(1)}, u32[]{:S(2)}, u32[]{:S(2)}) %collective-permute-start.21) | collective-permute-done | bytes 65568 | tf_op jit(solution)/shard_map/ppermute | solution.py:60
  106.5 0.6 shard_map.66
  (18 shorter events, 0.2 us)
Async XLA Ops:
  0.0 24.9 %collective-permute-start.8 = (bf16[2,512,256]{2,1,0:T(8,128)(2,1)}, bf16[2,512,256]{2,1,0:T(8,128)(2,1)S(1)}, u32[]{:S(2)}, u32[]{:S(2)}) collective-permute-start(bf16[2,512,256]{2,1,0:T(8,128)(2,1)} %bitcast.8), channel_id=1, source_target_pairs={{0,64},{64,128},{128,192},{192,0},{1,65},{65,129},{129,193},{193,1... | collective-permute-start | bytes 1572872 | tf_op jit(solution)/shard_map/ppermute | solution.py:46
  2.9 9.3 %collective-permute-start = (bf16[80,256]{1,0:T(8,128)(2,1)S(1)}, bf16[80,256]{1,0:T(8,128)(2,1)S(1)}, u32[]{:S(2)}, u32[]{:S(2)}) collective-permute-start(bf16[80,256]{1,0:T(8,128)(2,1)S(1)} %fusion.1), channel_id=1, source_target_pairs={{0,32},{32,0},{1,33},{33,1},{2,34},{34,2},{3,35},{35,3},{4,36},{36... | collective-permute-start | bytes 122888 | tf_op jit(solution)/shard_map/ppermute | solution.py:42
  4.0 8.7 %collective-permute-start.1 = (bf16[80,256]{1,0:T(8,128)(2,1)S(1)}, bf16[80,256]{1,0:T(8,128)(2,1)S(1)}, u32[]{:S(2)}, u32[]{:S(2)}) collective-permute-start(bf16[80,256]{1,0:T(8,128)(2,1)S(1)} %fusion.1), channel_id=1, source_target_pairs={{0,48},{1,49},{2,50},{3,51},{4,52},{5,53},{6,54},{7,55},{8,56},{9,... | collective-permute-start | bytes 122888 | tf_op jit(solution)/shard_map/ppermute | solution.py:70
  10.7 5.5 %collective-permute-start.2 = (bf16[80,256]{1,0:T(8,128)(2,1)S(1)}, bf16[80,256]{1,0:T(8,128)(2,1)S(1)}, u32[]{:S(2)}, u32[]{:S(2)}) collective-permute-start(bf16[80,256]{1,0:T(8,128)(2,1)S(1)} %fusion.1), channel_id=1, source_target_pairs={{0,40},{1,41},{2,42},{3,43},{4,44},{5,45},{6,46},{7,47},{8,32},{9,... | collective-permute-start | bytes 122888 | tf_op jit(solution)/shard_map/ppermute | solution.py:70
  12.2 5.5 %collective-permute-start.3 = (bf16[80,256]{1,0:T(8,128)(2,1)S(1)}, bf16[80,256]{1,0:T(8,128)(2,1)S(1)}, u32[]{:S(2)}, u32[]{:S(2)}) collective-permute-start(bf16[80,256]{1,0:T(8,128)(2,1)S(1)} %fusion.1), channel_id=1, source_target_pairs={{0,56},{1,57},{2,58},{3,59},{4,60},{5,61},{6,62},{7,63},{8,48},{9,... | collective-permute-start | bytes 122888 | tf_op jit(solution)/shard_map/ppermute | solution.py:70
  17.8 6.5 %collective-permute-start.4 = (bf16[320,256]{1,0:T(8,128)(2,1)S(1)}, bf16[320,256]{1,0:T(8,128)(2,1)S(1)}, u32[]{:S(2)}, u32[]{:S(2)}) collective-permute-start(bf16[320,256]{1,0:T(8,128)(2,1)S(1)} %join.1.a), channel_id=1, source_target_pairs={{0,4},{1,5},{2,6},{3,7},{4,0},{5,1},{6,2},{7,3},{8,12},{9,13},{10,... | collective-permute-start | bytes 491528 | tf_op jit(solution)/shard_map/ppermute | solution.py:60
  19.3 1.0 copy-start
  20.4 0.7 copy-start.2
  21.1 14.8 %collective-permute-start.7 = (bf16[2,528,256]{2,1,0:T(8,128)(2,1)S(1)}, bf16[2,528,256]{2,1,0:T(8,128)(2,1)S(1)}, u32[]{:S(2)}, u32[]{:S(2)}) collective-permute-start(bf16[2,528,256]{2,1,0:T(8,128)(2,1)S(1)} %load.1), channel_id=1, source_target_pairs={{0,96},{32,64},{64,160},{96,128},{128,224},{160,192},{192,32},{224... | collective-permute-start | bytes 1622024 | tf_op jit(solution)/shard_map/ppermute | solution.py:55
  22.0 26.1 %collective-permute-start.9 = (bf16[2,528,256]{2,1,0:T(8,128)(2,1)S(1)}, bf16[2,528,256]{2,1,0:T(8,128)(2,1)S(1)}, u32[]{:S(2)}, u32[]{:S(2)}) collective-permute-start(bf16[2,528,256]{2,1,0:T(8,128)(2,1)S(1)} %load.1), channel_id=1, source_target_pairs={{0,224},{32,192},{64,32},{96,0},{128,96},{160,64},{192,160},{224,1... | collective-permute-start | bytes 1622024 | tf_op jit(solution)/shard_map/ppermute | solution.py:55
  24.1 24.0 %collective-permute-start.10 = (bf16[2,512,256]{2,1,0:T(8,128)(2,1)}, bf16[2,512,256]{2,1,0:T(8,128)(2,1)S(1)}, u32[]{:S(2)}, u32[]{:S(2)}) collective-permute-start(bf16[2,512,256]{2,1,0:T(8,128)(2,1)} %bitcast.9), channel_id=1, source_target_pairs={{0,192},{64,0},{128,64},{192,128},{1,193},{65,1},{129,65},{193,129... | collective-permute-start | bytes 1572872 | tf_op jit(solution)/shard_map/ppermute | solution.py:46
  24.3 35.1 %collective-permute-start.6 = (bf16[2,528,256]{2,1,0:T(8,128)(2,1)S(1)}, bf16[2,528,256]{2,1,0:T(8,128)(2,1)S(1)}, u32[]{:S(2)}, u32[]{:S(2)}) collective-permute-start(bf16[2,528,256]{2,1,0:T(8,128)(2,1)S(1)} %load.1), channel_id=1, source_target_pairs={{0,32},{32,0},{1,33},{33,1},{2,34},{34,2},{3,35},{35,3},{4,36},{36... | collective-permute-start | bytes 1622024 | tf_op jit(solution)/shard_map/ppermute | solution.py:42
  24.9 28.5 %collective-permute-start.5 = (bf16[528,256]{1,0:T(8,128)(2,1)S(1)}, bf16[528,256]{1,0:T(8,128)(2,1)S(1)}, u32[]{:S(2)}, u32[]{:S(2)}) collective-permute-start(bf16[528,256]{1,0:T(8,128)(2,1)S(1)} %pack.1.p0), channel_id=1, source_target_pairs={{0,1},{1,0},{2,3},{3,2},{4,5},{5,4},{6,7},{7,6},{8,9},{9,8},{10,11... | collective-permute-start | bytes 811016 | tf_op jit(solution)/shard_map/ppermute | solution.py:75
  36.0 18.3 %copy-start.1 = (s32[2,512,16]{1,2,0:T(8,128)S(1)}, s32[2,512,16]{1,2,0:T(8,128)}, u32[]{:S(2)}) copy-start(s32[2,512,16]{1,2,0:T(8,128)} %param.11) | copy-start | bytes 196612
  36.0 23.4 %copy-start.3 = (bf16[2,1,512,256]{3,2,1,0:T(8,128)(2,1)S(1)}, bf16[2,1,512,256]{3,2,1,0:T(8,128)(2,1)}, u32[]{:S(2)}) copy-start(bf16[2,1,512,256]{3,2,1,0:T(8,128)(2,1)} %param.10) | copy-start | bytes 1572868
  36.0 36.3 %collective-permute-start.11 = (bf16[1040,256]{1,0:T(8,128)(2,1)S(1)}, bf16[1040,256]{1,0:T(8,128)(2,1)S(1)}, u32[]{:S(2)}, u32[]{:S(2)}) collective-permute-start(bf16[1040,256]{1,0:T(8,128)(2,1)S(1)} %relay.2), channel_id=1, source_target_pairs={{0,64},{64,128},{128,192},{192,0},{1,65},{65,129},{129,193},{193,1... | collective-permute-start | bytes 1597448 | tf_op jit(solution)/shard_map/ppermute | solution.py:46
  48.2 24.2 %collective-permute-start.12 = (bf16[1040,256]{1,0:T(8,128)(2,1)S(1)}, bf16[1040,256]{1,0:T(8,128)(2,1)S(1)}, u32[]{:S(2)}, u32[]{:S(2)}) collective-permute-start(bf16[1040,256]{1,0:T(8,128)(2,1)S(1)} %relay.3), channel_id=1, source_target_pairs={{0,192},{64,0},{128,64},{192,128},{1,193},{65,1},{129,65},{193,129... | collective-permute-start | bytes 1597448 | tf_op jit(solution)/shard_map/ppermute | solution.py:46
  50.7 14.9 %collective-permute-start.14 = (bf16[528,256]{1,0:T(8,128)(2,1)S(1)}, bf16[528,256]{1,0:T(8,128)(2,1)S(1)}, u32[]{:S(2)}, u32[]{:S(2)}) collective-permute-start(bf16[528,256]{1,0:T(8,128)(2,1)S(1)} %pack.1.p0), channel_id=1, source_target_pairs={{0,2},{1,3},{2,0},{3,1},{4,6},{5,7},{6,4},{7,5},{8,10},{9,11},{10,... | collective-permute-start | bytes 811016 | tf_op jit(solution)/shard_map/ppermute | solution.py:75
  53.4 13.0 %collective-permute-start.15 = (bf16[528,256]{1,0:T(8,128)(2,1)S(1)}, bf16[528,256]{1,0:T(8,128)(2,1)S(1)}, u32[]{:S(2)}, u32[]{:S(2)}) collective-permute-start(bf16[528,256]{1,0:T(8,128)(2,1)S(1)} %pack.1.p0), channel_id=1, source_target_pairs={{0,3},{1,2},{2,1},{3,0},{4,7},{5,6},{6,5},{7,4},{8,11},{9,10},{10,... | collective-permute-start | bytes 811016 | tf_op jit(solution)/shard_map/ppermute | solution.py:75
  74.6 9.0 %collective-permute-start.16 = (bf16[512,256]{1,0:T(8,128)(2,1)S(1)}, bf16[512,256]{1,0:T(8,128)(2,1)S(1)}, u32[]{:S(2)}, u32[]{:S(2)}) collective-permute-start(bf16[512,256]{1,0:T(8,128)(2,1)S(1)} %get-tuple-element.33), channel_id=1, source_target_pairs={{0,2},{1,3},{2,0},{3,1},{4,6},{5,7},{6,4},{7,5},{8,10},{9,11},{10,... | collective-permute-start | bytes 786440 | tf_op jit(solution)/shard_map/ppermute | solution.py:75
  74.8 14.9 %collective-permute-start.17 = (bf16[512,256]{1,0:T(8,128)(2,1)S(1)}, bf16[512,256]{1,0:T(8,128)(2,1)S(1)}, u32[]{:S(2)}, u32[]{:S(2)}) collective-permute-start(bf16[512,256]{1,0:T(8,128)(2,1)S(1)} %get-tuple-element.34), channel_id=1, source_target_pairs={{0,3},{1,2},{2,1},{3,0},{4,7},{5,6},{6,5},{7,4},{8,11},{9,10},{10,... | collective-permute-start | bytes 786440 | tf_op jit(solution)/shard_map/ppermute | solution.py:75
  79.7 10.0 %collective-permute-start.13 = (bf16[512,256]{1,0:T(8,128)(2,1)S(1)}, bf16[512,256]{1,0:T(8,128)(2,1)S(1)}, u32[]{:S(2)}, u32[]{:S(2)}) collective-permute-start(bf16[512,256]{1,0:T(8,128)(2,1)S(1)} %get-tuple-element.29), channel_id=1, source_target_pairs={{0,1},{1,0},{2,3},{3,2},{4,5},{5,4},{6,7},{7,6},{8,9},{9,8},{10,11... | collective-permute-start | bytes 786440 | tf_op jit(solution)/shard_map/ppermute | solution.py:75
  89.8 7.3 %collective-permute-start.18 = (f32[256,256]{1,0:T(8,128)S(1)}, f32[256,256]{1,0:T(8,128)S(1)}, u32[]{:S(2)}, u32[]{:S(2)}) collective-permute-start(f32[256,256]{1,0:T(8,128)S(1)} %get-tuple-element.36), channel_id=1, source_target_pairs={{0,4},{1,5},{2,6},{3,7},{4,0},{5,1},{6,2},{7,3},{8,12},{9,13},{10,... | collective-permute-start | bytes 786440 | tf_op jit(solution)/shard_map/ppermute | solution.py:60
  97.2 5.7 %collective-permute-start.19 = (f32[64,256]{1,0:T(8,128)S(1)}, f32[64,256]{1,0:T(8,128)S(1)}, u32[]{:S(2)}, u32[]{:S(2)}) collective-permute-start(f32[64,256]{1,0:T(8,128)S(1)} %get-tuple-element.38), channel_id=1, source_target_pairs={{0,8},{1,9},{2,10},{3,11},{4,12},{5,13},{6,14},{7,15},{8,0},{9,1},... | collective-permute-start | bytes 196616 | tf_op jit(solution)/shard_map/ppermute | solution.py:60
  97.5 7.1 %collective-permute-start.20 = (f32[64,256]{1,0:T(8,128)S(1)}, f32[64,256]{1,0:T(8,128)S(1)}, u32[]{:S(2)}, u32[]{:S(2)}) collective-permute-start(f32[64,256]{1,0:T(8,128)S(1)} %get-tuple-element.39), channel_id=1, source_target_pairs={{0,16},{1,17},{2,18},{3,19},{4,20},{5,21},{6,22},{7,23},{8,24},{9,... | collective-permute-start | bytes 196616 | tf_op jit(solution)/shard_map/ppermute | solution.py:60
  99.2 7.3 %collective-permute-start.21 = (f32[64,256]{1,0:T(8,128)S(1)}, f32[64,256]{1,0:T(8,128)S(1)}, u32[]{:S(2)}, u32[]{:S(2)}) collective-permute-start(f32[64,256]{1,0:T(8,128)S(1)} %get-tuple-element.40), channel_id=1, source_target_pairs={{0,24},{1,25},{2,26},{3,27},{4,28},{5,29},{6,30},{7,31},{8,16},{9,... | collective-permute-start | bytes 196616 | tf_op jit(solution)/shard_map/ppermute | solution.py:60

commit v4 on v3

--- a/solution.py
+++ b/solution.py
@@ -22,20 +22,13 @@
 PAD = 16
 Z_ORDER = (0, 4, 2, 6, 1, 5, 3, 7)
 
-GROUP = 4
-SPANS = 8
-SOURCES = 5
-PICKS = 24
-META = SOURCES * 2 * PICKS
-TOTALS = META + SOURCES * 2 * 8
-KEYS = RANGE_BLOCKS + 2
-TURNS = 0b10_01_11_00
+TURNS = (0, ROWS - 1, 1, 2)
+SPAN_KEYS = BATCHES * RANGE_BLOCKS
 DEAD = -1e30
 LIVE = math.log2(1.0 / (MEMBERS - 1))
 STRETCH = 2.0 * math.sqrt(math.log2(math.e))
 
 VMEM = pl.BlockSpec(memory_space=pltpu.VMEM)
-SMEM = pl.BlockSpec(memory_space=pltpu.SMEM)
 
 
 def flip(value):
@@ -75,125 +68,90 @@
     return lax.ppermute(value, "obs", pairs)
 
 
-def lists_kernel(named_ref, lists, shifts, used):
+def masks_kernel(named, masks, hits):
     row, column = lax.axis_index("rows"), lax.axis_index("obs")
-    first = row * RANGE_BLOCKS
-
-    def span(n, carry):
-        near_side = n < 6
-        source = jnp.where(near_side, lax.shift_right_logical(n, 1), n - 3)
-        local_t = jnp.where(near_side, jnp.bitwise_and(n, 1), 0)
-        turn = jnp.bitwise_and(
-            lax.shift_right_logical(TURNS, 2 * lax.shift_right_logical(n, 1)), ROWS - 1
-        )
-        place = (jnp.bitwise_and(row + turn, ROWS - 1) * OBS + column) * SPAN
-        batch = jnp.bitwise_and(n, 1)
-        key = n * KEYS
-        for k in range(KEYS):
-            used[key + k] = 0
-            for j in range(SPAN):
-                shifts[(key + k) * SPAN + j] = DEAD
+    blocks = lax.broadcasted_iota(jnp.int32, (RANGE_BLOCKS, EDGE), 0) + row * RANGE_BLOCKS
+    for chunk in range(ROWS):
+        for t in range(BATCHES):
+            hit = jnp.zeros((RANGE_BLOCKS, EDGE), jnp.float32)
+            for e in range(NAMED):
+                picked = named[t, e : e + 1, chunk * EDGE : (chunk + 1) * EDGE]
+                hit = jnp.where(picked == blocks, 1.0, hit)
+            hits[chunk, t * RANGE_BLOCKS : (t + 1) * RANGE_BLOCKS] = hit
+    shift = jnp.bitwise_and(EDGE - column * SPAN, EDGE - 1)
+    for k, turn in enumerate(TURNS):
+        chunk = hits[jnp.bitwise_and(row + turn, ROWS - 1)]
+        rolled = pltpu.roll(chunk, shift, 1)
         for j in range(SPAN):
-            for e in range(NAMED):
-                relative = named_ref[batch, e, place + j] - first
-                inside = jnp.bitwise_and(relative, -RANGE_BLOCKS) == 0
-                at = jnp.where(inside, key + relative, SPANS * KEYS)
-                used[at] = 1
-                shifts[at * SPAN + j] = LIVE
-        for parity in range(2):
-            r = source * 2 + parity
-            before = jnp.where(local_t == 0, 0, lists[TOTALS + r])
-            start = r * PICKS + before * GROUP
-            write = start
-            for z in range(NZ):
-                lists[write] = z
-                write = write + used[key + 2 * z + parity]
-            for k in range(GROUP - 1):
-                lists[write + k] = NZ
-            visits = lax.shift_right_logical(write - start + GROUP - 1, 2)
-            for k in range(2):
-                lists[META + r * 8 + before + k] = local_t
-            total = before + visits
-
-            @pl.when(total == 0)
-            def _(start=start):
-                for k in range(GROUP):
-                    lists[start + k] = NZ
-
-            last = jnp.logical_or(local_t == 1, jnp.logical_not(near_side))
-            lists[TOTALS + r] = jnp.where(last, jnp.maximum(total, 1), total)
-        return carry
-
-    lax.fori_loop(0, SPANS, span, 0)
-
-
-def make_lists(named):
-    return pl.pallas_call(
-        lists_kernel,
-        out_shape=(
-            jax.ShapeDtypeStruct((TOTALS + 16,), jnp.int32),
-            jax.ShapeDtypeStruct(((SPANS * KEYS + 1) * SPAN,), jnp.float32),
-        ),
-        in_specs=[SMEM],
-        out_specs=(SMEM, SMEM),
-        scratch_shapes=[pltpu.SMEM((SPANS * KEYS + 1,), jnp.int32)],
-        compiler_params=pltpu.CompilerParams(vmem_limit_bytes=1 << 20),
+            wide = jnp.broadcast_to(rolled[:, j : j + 1], (SPAN_KEYS, EDGE))
+            masks[k * SPAN_KEYS : (k + 1) * SPAN_KEYS, j * EDGE : (j + 1) * EDGE] = jnp.where(
+                wide > 0.5, LIVE, DEAD
+            )
+
+
+def make_masks(named):
+    return pl.pallas_call(
+        masks_kernel,
+        out_shape=jax.ShapeDtypeStruct((len(TURNS) * SPAN_KEYS, SPAN * EDGE), jnp.float32),
+        in_specs=[VMEM],
+        out_specs=VMEM,
+        scratch_shapes=[pltpu.VMEM((ROWS, SPAN_KEYS, EDGE), jnp.float32)],
+        compiler_params=pltpu.CompilerParams(vmem_limit_bytes=4 << 20),
         cost_estimate=pl.CostEstimate(flops=4_000_000, transcendentals=0, bytes_accessed=4_000_000),
-        name="lists",
+        name="masks",
     )(named)
 
 
-def tile_loop(segments, parity, state, spot, acc, places, tiles, lists, shifts):
-    def chosen(s, g):
-        return [lists[(s * 2 + parity) * PICKS + g * GROUP + k] for k in range(GROUP)]
-
-    def batch_of(s, g):
-        return lists[META + (s * 2 + parity) * 8 + g]
-
-    def make(segment, g):
-        s, n, rows, obs, _ = segment
-        t = batch_of(s, g)
-        picks = chosen(s, g)
-        gathered = jnp.concatenate(
-            [state[pl.ds(2 * z, 2)].reshape(EDGE, MEMBERS) for z in picks], axis=0
-        )
-        products = lax.dot_general(
-            gathered, obs(t), (((1,), (1,)), ((), ())), preferred_element_type=jnp.float32
-        )
-        for k, z in enumerate(picks):
-            key = ((n + t) * KEYS + 2 * z + parity) * SPAN
-            positions = spot[pl.ds(2 * z, 2)].reshape(EDGE, EDGE)
-            for j in range(SPAN):
-                d = positions - places[pl.ds(rows + t * SPAN + j, 1), :]
-                part = products[k * EDGE : (k + 1) * EDGE, j * EDGE : (j + 1) * EDGE]
-                damped = part * jnp.exp2(shifts[key + j] - d * d)
-                tiles[k * EDGE : (k + 1) * EDGE, j * EDGE : (j + 1) * EDGE] = damped.astype(
-                    jnp.bfloat16
+def tile_pass(segments, parity, state, spot, acc, places, tiles, masks, base):
+    pair = 2 * EDGE
+    flat_state = state.reshape((2 * NZ) * SHARD, MEMBERS)
+    flat_spot = spot.reshape((2 * NZ) * SHARD, EDGE)
+
+    def make(spans, buffer):
+        for u, (key, place, obs) in enumerate(spans):
+            for h in range(SPAN // 2):
+                here = obs[h * pair : (h + 1) * pair, :]
+                products = lax.dot_general(
+                    flat_state[...], here, (((1,), (1,)), ((), ())),
+                    preferred_element_type=jnp.float32,
                 )
-
-    def add(segment, g):
-        s, weights = segment[0], segment[4]
-        added = jnp.dot(
-            tiles[...], weights(batch_of(s, g)), preferred_element_type=jnp.float32
-        )
-        for k, z in enumerate(chosen(s, g)):
-            acc[z] += added[k * EDGE : (k + 1) * EDGE]
-
-    before = None
-    for segment in segments:
-        total = lists[TOTALS + segment[0] * 2 + parity]
-        if before is not None:
-            add(*before)
-        make(segment, 0)
-
-        def step(g, carry, segment=segment):
-            add(segment, g - 1)
-            make(segment, g)
-            return carry
-
-        lax.fori_loop(1, total, step, 0)
-        before = (segment, total - 1)
-    add(*before)
+                for z in range(NZ):
+                    positions = flat_spot[z * EDGE : (z + 1) * EDGE]
+                    live = masks[pl.ds(key + 2 * z + parity, 1), h * pair : (h + 1) * pair]
+                    for i in range(2):
+                        j = 2 * h + i
+                        d = positions - places[place + j : place + j + 1, :]
+                        part = products[z * EDGE : (z + 1) * EDGE, i * EDGE : (i + 1) * EDGE]
+                        damped = part * jnp.exp2(live[:, i * EDGE : (i + 1) * EDGE] - d * d)
+                        at = (u * SPAN + j) * EDGE
+                        tiles[buffer, z * EDGE : (z + 1) * EDGE, at : at + EDGE] = damped.astype(
+                            jnp.bfloat16
+                        )
+
+    def add(weights, buffer, first):
+        start = 0
+        total = None
+        for weight in weights:
+            depth = weight.shape[0]
+            part = jnp.dot(
+                tiles[buffer, :, start : start + depth], weight[...],
+                preferred_element_type=jnp.float32,
+            )
+            total = part if total is None else total + part
+            start += depth
+        total = total.reshape(NZ, EDGE, MEMBERS)
+        if not first:
+            total = acc[...] + total
+        elif base is not None:
+            total = base[...] + total
+        acc[...] = total
+
+    for n, (spans, weights) in enumerate(segments):
+        if n:
+            add(segments[n - 1][1], (n - 1) % 2, n == 1)
+        make(spans, n % 2)
+    last = len(segments) - 1
+    add(segments[last][1], last % 2, last == 0)
 
 
 def spread_places(held, places, start):
@@ -208,7 +166,7 @@
 
 
 def near_kernel(
-    late, lists, shifts, p0, p1, oo, wo, ol, wl, orr, wr, state, spot, acc, places, tiles
+    late, masks, p0, p1, oo, wo, ol, wl, orr, wr, state, spot, acc, places, tiles
 ):
     my_z, x = own_place(late)
     lanes = lax.broadcasted_iota(jnp.int32, (SHARD, EDGE), 1)
@@ -226,61 +184,53 @@
             at = jnp.bitwise_xor(my_z, mask) * 2 + half
             state[at] = piece[p * SHARD : (p + 1) * SHARD, :]
             spot[at] = columns[p * SHARD : (p + 1) * SHARD]
-    state[2 * NZ :] = jnp.zeros((2, SHARD, MEMBERS), jnp.bfloat16)
-    spot[2 * NZ :] = jnp.zeros((2, SHARD, EDGE), jnp.float32)
-    acc[...] = jnp.zeros_like(acc)
     segments = []
-    for s, (o, w) in enumerate(((oo, wo), (ol, wl), (orr, wr))):
+    for k, (o, w) in enumerate(((oo, wo), (ol, wl), (orr, wr))):
+        spans = []
         for t in range(BATCHES):
-            spread_places(o[t, OBS_ROWS : OBS_ROWS + PAD, :EDGE], places, s * 8 + t * SPAN)
-        segments.append(
-            (s, 2 * s, 8 * s, lambda t, o=o: o[t, :OBS_ROWS, :], lambda t, w=w: w[t])
-        )
+            place = (k * BATCHES + t) * SPAN
+            spread_places(o[t, OBS_ROWS : OBS_ROWS + PAD, :EDGE], places, place)
+            spans.append((k * SPAN_KEYS + t * RANGE_BLOCKS, place, o.at[t]))
+        segments.append((spans, (w.reshape(BATCHES * OBS_ROWS, MEMBERS),)))
     parity = lax.shift_right_logical(x, 1)
-    tile_loop(segments, parity, state, spot, acc, places, tiles, lists, shifts)
+    tile_pass(segments, parity, state, spot, acc, places, tiles, masks, None)
 
 
 SCRATCH = [
     pltpu.VMEM((24, EDGE), jnp.float32),
-    pltpu.VMEM((GROUP * EDGE, SPAN * EDGE), jnp.bfloat16),
+    pltpu.VMEM((2, NZ * EDGE, BATCHES * SPAN * EDGE), jnp.bfloat16),
 ]
 
 
-def near(late, lists, arrays):
+def near(late, masks, arrays):
     return pl.pallas_call(
         functools.partial(near_kernel, late),
         out_shape=(
-            jax.ShapeDtypeStruct((2 * NZ + 2, SHARD, MEMBERS), jnp.bfloat16),
-            jax.ShapeDtypeStruct((2 * NZ + 2, SHARD, EDGE), jnp.float32),
-            jax.ShapeDtypeStruct((NZ + 1, EDGE, MEMBERS), jnp.float32),
+            jax.ShapeDtypeStruct((2 * NZ, SHARD, MEMBERS), jnp.bfloat16),
+            jax.ShapeDtypeStruct((2 * NZ, SHARD, EDGE), jnp.float32),
+            jax.ShapeDtypeStruct((NZ, EDGE, MEMBERS), jnp.float32),
         ),
-        in_specs=[SMEM, SMEM] + [VMEM] * 8,
+        in_specs=[VMEM] * 9,
         out_specs=(VMEM,) * 3,
         scratch_shapes=SCRATCH,
-        compiler_params=pltpu.CompilerParams(vmem_limit_bytes=16 << 20),
+        compiler_params=pltpu.CompilerParams(vmem_limit_bytes=20 << 20),
         cost_estimate=pl.CostEstimate(
             flops=2_000_000_000, transcendentals=2_000_000, bytes_accessed=4_000_000
         ),
         name="near_late" if late else "near_early",
-    )(*lists, *arrays)
-
-
-def far_kernel(
-    late, lists, shifts, state, spot, near_acc, left, right, r0, r1, places, tiles, acc
-):
-    acc[...] = near_acc[...]
-    segments = []
-    for k, both in enumerate((left, right)):
-        spread_places(both[OBS_ROWS : OBS_ROWS + PAD, :EDGE], places, 8 * k)
-        segments.append(
-            (
-                3 + k, 6 + k, 8 * k, lambda t, both=both: both[:OBS_ROWS, :],
-                lambda t, both=both: both[OBS_ROWS + PAD :, :],
-            )
-        )
+    )(masks, *arrays)
+
+
+def far_kernel(late, masks, state, spot, near_acc, left, right, r0, r1, places, tiles, acc):
+    spans, weights = [], []
+    for t, both in enumerate((left, right)):
+        spread_places(both[OBS_ROWS : OBS_ROWS + PAD, :EDGE], places, t * SPAN)
+        spans.append(((len(TURNS) - 1) * SPAN_KEYS + t * RANGE_BLOCKS, t * SPAN, both))
+        weights.append(both.at[OBS_ROWS + PAD :])
     _, x = own_place(late)
     parity = lax.shift_right_logical(x, 1)
-    tile_loop(segments, parity, state, spot, acc, places, tiles, lists, shifts)
+    segments = [(spans, weights)]
+    tile_pass(segments, parity, state, spot, acc, places, tiles, masks, near_acc)
     for k, out in enumerate((r0, r1)):
         half = jnp.bitwise_and(jnp.bitwise_xor(x, k), 1)
         start = pl.multiple_of(half * SHARD, SHARD)
@@ -288,7 +238,7 @@
             out[z * SHARD : (z + 1) * SHARD] = acc[z, pl.ds(start, SHARD), :].astype(out.dtype)
 
 
-def far(late, lists, state, spot, acc, arrays):
+def far(late, masks, state, spot, acc, arrays):
     rows = NZ * SHARD
     return pl.pallas_call(
         functools.partial(far_kernel, late),
@@ -296,15 +246,15 @@
             jax.ShapeDtypeStruct((rows, MEMBERS), jnp.bfloat16 if late else jnp.float32),
             jax.ShapeDtypeStruct((rows, MEMBERS), jnp.bfloat16),
         ),
-        in_specs=[SMEM, SMEM] + [VMEM] * 5,
+        in_specs=[VMEM] * 6,
         out_specs=(VMEM, VMEM),
-        scratch_shapes=SCRATCH + [pltpu.VMEM((NZ + 1, EDGE, MEMBERS), jnp.float32)],
-        compiler_params=pltpu.CompilerParams(vmem_limit_bytes=16 << 20),
+        scratch_shapes=SCRATCH + [pltpu.VMEM((NZ, EDGE, MEMBERS), jnp.float32)],
+        compiler_params=pltpu.CompilerParams(vmem_limit_bytes=20 << 20),
         cost_estimate=pl.CostEstimate(
             flops=500_000_000, transcendentals=500_000, bytes_accessed=4_000_000
         ),
         name="far_late" if late else "far_early",
-    )(*lists, state, spot, acc, *arrays)
+    )(masks, state, spot, acc, *arrays)
 
 
 def sum_x_kernel(own, x1, x2, x3, keep, send):
@@ -444,14 +394,14 @@
     far1 = relay(1, obs_right, weight_right)
     far1 = along_rows(far1, ROWS - 1)
 
-    lists = make_lists(jnp.transpose(block_rows, (0, 2, 1)))
+    masks = make_masks(jnp.transpose(block_rows, (0, 2, 1)))
     seen = (obs_own, weight, obs_left, weight_left, obs_right, weight_right)
-    early = near(0, lists, (pieces[0], pieces[1], *seen))
-    later = near(1, lists, (pieces[2], pieces[3], *seen))
-    part2, part3 = far(1, lists, *later, (far0, far1))
+    early = near(0, masks, (pieces[0], pieces[1], *seen))
+    later = near(1, masks, (pieces[2], pieces[3], *seen))
+    part2, part3 = far(1, masks, *later, (far0, far1))
     part2 = swap_x(part2, 2)
     part3 = swap_x(part3, 3)
-    own, part1 = far(0, lists, *early, (far0, far1))
+    own, part1 = far(0, masks, *early, (far0, far1))
     part1 = swap_x(part1, 1)
     parts = [part1, part2, part3]
     keep, send = small(sum_x_kernel, (4 * SHARD, 4 * SHARD), own, *parts)

time: 108 us -> 108 us (level)
  the two profiles are of different devices: /device:TPU:1 before, /device:TPU:38 now
where the time goes in v4:
time: 108 us
  waiting for transfers between devices  57.4 us (53%)
  starting transfers between devices  33.4 us (31%)
  Pallas kernels  14.1 us (13%)
  local copies, waits for them, and re-layouts  1.71 us (2%)
    ppermute x6, waiting for transfers between devices, swap_x(): return lax.ppermute(value, 'obs', pairs)  17 us
    ppermute x5, waiting for transfers between devices, swap_z(): return lax.ppermute(value, 'obs', pairs)  13.6 us
    ppermute x4, waiting for transfers between devices, along_rows(): lax.ppermute(value, 'rows', [(s, (s + step) % ROWS) for s in range(ROWS)])  12.3 us
    ppermute x2, waiting for transfers between devices, along_rows_flip(): return lax.ppermute(value, ('rows', 'half'), pairs)  8.98 us
    ppermute x5, starting transfers between devices, swap_z(): return lax.ppermute(value, 'obs', pairs)  8.63 us
    pallas_call x2, Pallas kernels, near(): pl.pallas_call(functools.partial(near_kernel, late), out_shape=(jax.Shape...  8.39 us
    ppermute x6, starting transfers between devices, swap_x(): return lax.ppermute(value, 'obs', pairs)  8.07 us
    ppermute x3, starting transfers between devices, swap_z_flip(): return lax.ppermute(value, ('half', 'obs'), pairs)  7.57 us
  transfers between devices with their start and end apart: 22, of which 13 were waited for; matrix products, arithmetic and copies ran while one was open for 1% of the time, Pallas kernels for 10%

profile of v4, /device:TPU:38, one launch (start us, length us, event | category | flops | bytes accessed | tf_op | source)
XLA Modules:
  0.0 107.5 jit_solution(16832749714301777374)
XLA Ops:
  0.0 1.6 %collective-permute-start.8 = (bf16[2,512,256]{2,1,0:T(8,128)(2,1)}, bf16[2,512,256]{2,1,0:T(8,128)(2,1)S(1)}, u32[]{:S(2)}, u32[]{:S(2)}) collective-permute-start(bf16[2,512,256]{2,1,0:T(8,128)(2,1)} %bitcast.8), channel_id=1, source_target_pairs={{0,64},{64,128},{128,192},{192,0},{1,65},{65,129},{129,193},{193,1... | collective-permute-start | bytes 1572872 | tf_op jit(solution)/shard_map/ppermute | solution.py:39
  1.6 0.7 copy-done.4
  2.2 0.8 fusion.1
  3.0 0.0 collective-permute-start
  3.0 6.4 %collective-permute-start.1 = (bf16[80,256]{1,0:T(8,128)(2,1)S(1)}, bf16[80,256]{1,0:T(8,128)(2,1)S(1)}, u32[]{:S(2)}, u32[]{:S(2)}) collective-permute-start(bf16[80,256]{1,0:T(8,128)(2,1)S(1)} %fusion.1), channel_id=1, source_target_pairs={{0,48},{1,49},{2,50},{3,51},{4,52},{5,53},{6,54},{7,55},{8,56},{9,... | collective-permute-start | bytes 122888 | tf_op jit(solution)/shard_map/ppermute | solution.py:63
  9.4 1.2 %collective-permute-start.2 = (bf16[80,256]{1,0:T(8,128)(2,1)S(1)}, bf16[80,256]{1,0:T(8,128)(2,1)S(1)}, u32[]{:S(2)}, u32[]{:S(2)}) collective-permute-start(bf16[80,256]{1,0:T(8,128)(2,1)S(1)} %fusion.1), channel_id=1, source_target_pairs={{0,40},{1,41},{2,42},{3,43},{4,44},{5,45},{6,46},{7,47},{8,32},{9,... | collective-permute-start | bytes 122888 | tf_op jit(solution)/shard_map/ppermute | solution.py:63
  10.6 0.7 collective-permute-done.1.refs_1_
  11.2 2.6 %collective-permute-done.2.refs_2_ = bf16[80,256]{1,0:T(8,128)(2,1)S(1)} collective-permute-done((bf16[80,256]{1,0:T(8,128)(2,1)S(1)}, bf16[80,256]{1,0:T(8,128)(2,1)S(1)}, u32[]{:S(2)}, u32[]{:S(2)}) %collective-permute-start.2) | collective-permute-done | bytes 40992 | tf_op jit(solution)/shard_map/ppermute | solution.py:63
  13.9 2.2 %collective-permute-done.3.refs_3_ = bf16[80,256]{1,0:T(8,128)(2,1)S(1)} collective-permute-done((bf16[80,256]{1,0:T(8,128)(2,1)S(1)}, bf16[80,256]{1,0:T(8,128)(2,1)S(1)}, u32[]{:S(2)}, u32[]{:S(2)}) %collective-permute-start.3) | collective-permute-done | bytes 40992 | tf_op jit(solution)/shard_map/ppermute | solution.py:63
  16.1 1.1 %collective-permute-start.4 = (bf16[320,256]{1,0:T(8,128)(2,1)S(1)}, bf16[320,256]{1,0:T(8,128)(2,1)S(1)}, u32[]{:S(2)}, u32[]{:S(2)}) collective-permute-start(bf16[320,256]{1,0:T(8,128)(2,1)S(1)} %join.1.a), channel_id=1, source_target_pairs={{0,4},{1,5},{2,6},{3,7},{4,0},{5,1},{6,2},{7,3},{8,12},{9,13},{10,... | collective-permute-start | bytes 491528 | tf_op jit(solution)/shard_map/ppermute | solution.py:53
  17.3 1.0 copy-done
  18.3 1.9 %collective-permute-start.7 = (bf16[2,528,256]{2,1,0:T(8,128)(2,1)S(1)}, bf16[2,528,256]{2,1,0:T(8,128)(2,1)S(1)}, u32[]{:S(2)}, u32[]{:S(2)}) collective-permute-start(bf16[2,528,256]{2,1,0:T(8,128)(2,1)S(1)} %load.1), channel_id=1, source_target_pairs={{0,96},{32,64},{64,160},{96,128},{128,224},{160,192},{192,32},{224... | collective-permute-start | bytes 1622024 | tf_op jit(solution)/shard_map/ppermute | solution.py:48
  20.3 1.1 %collective-permute-start.9 = (bf16[2,528,256]{2,1,0:T(8,128)(2,1)S(1)}, bf16[2,528,256]{2,1,0:T(8,128)(2,1)S(1)}, u32[]{:S(2)}, u32[]{:S(2)}) collective-permute-start(bf16[2,528,256]{2,1,0:T(8,128)(2,1)S(1)} %load.1), channel_id=1, source_target_pairs={{0,224},{32,192},{64,32},{96,0},{128,96},{160,64},{192,160},{224,1... | collective-permute-start | bytes 1622024 | tf_op jit(solution)/shard_map/ppermute | solution.py:48
  21.4 0.9 collective-permute-start.10
  22.3 0.9 collective-permute-done.4.b
  23.1 0.3 collective-permute-start.6
  23.4 0.0 collective-permute-done.8.wl.weights
  23.4 0.9 collective-permute-start.5
  24.4 9.0 %collective-permute-done.7.ol.obs = bf16[2,528,256]{2,1,0:T(8,128)(2,1)S(1)} collective-permute-done((bf16[2,528,256]{2,1,0:T(8,128)(2,1)S(1)}, bf16[2,528,256]{2,1,0:T(8,128)(2,1)S(1)}, u32[]{:S(2)}, u32[]{:S(2)}) %collective-permute-start.7) | collective-permute-done | bytes 540704 | tf_op jit(solution)/shard_map/ppermute | solution.py:48
  33.4 0.0 copy-start.1
  33.4 0.4 collective-permute-start.11
  33.8 12.3 %collective-permute-done.10.wr.weights = bf16[2,512,256]{2,1,0:T(8,128)(2,1)S(1)} collective-permute-done((bf16[2,512,256]{2,1,0:T(8,128)(2,1)S(1)}, bf16[2,512,256]{2,1,0:T(8,128)(2,1)S(1)}, u32[]{:S(2)}, u32[]{:S(2)}) %collective-permute-start.10) | collective-permute-done | bytes 524320 | tf_op jit(solution)/shard_map/ppermute | solution.py:39
  46.1 2.9 %collective-permute-start.12 = (bf16[1040,256]{1,0:T(8,128)(2,1)S(1)}, bf16[1040,256]{1,0:T(8,128)(2,1)S(1)}, u32[]{:S(2)}, u32[]{:S(2)}) collective-permute-start(bf16[1040,256]{1,0:T(8,128)(2,1)S(1)} %relay.3), channel_id=1, source_target_pairs={{0,192},{64,0},{128,64},{192,128},{1,193},{65,1},{129,65},{193,129... | collective-permute-start | bytes 1597448 | tf_op jit(solution)/shard_map/ppermute | solution.py:39
  49.1 1.4 %collective-permute-start.14 = (bf16[528,256]{1,0:T(8,128)(2,1)S(1)}, bf16[528,256]{1,0:T(8,128)(2,1)S(1)}, u32[]{:S(2)}, u32[]{:S(2)}) collective-permute-start(bf16[528,256]{1,0:T(8,128)(2,1)S(1)} %pack.1.p0), channel_id=1, source_target_pairs={{0,2},{1,3},{2,0},{3,1},{4,6},{5,7},{6,4},{7,5},{8,10},{9,11},{10,... | collective-permute-start | bytes 811016 | tf_op jit(solution)/shard_map/ppermute | solution.py:68
  50.5 2.1 %collective-permute-start.15 = (bf16[528,256]{1,0:T(8,128)(2,1)S(1)}, bf16[528,256]{1,0:T(8,128)(2,1)S(1)}, u32[]{:S(2)}, u32[]{:S(2)}) collective-permute-start(bf16[528,256]{1,0:T(8,128)(2,1)S(1)} %pack.1.p0), channel_id=1, source_target_pairs={{0,3},{1,2},{2,1},{3,0},{4,7},{5,6},{6,5},{7,4},{8,11},{9,10},{10,... | collective-permute-start | bytes 811016 | tf_op jit(solution)/shard_map/ppermute | solution.py:68
  52.6 0.3 masks.1
  52.9 0.0 collective-permute-done.6.oo
  52.9 4.2 %near_early.1 = (bf16[16,64,256]{2,1,0:T(8,128)(2,1)S(1)}, f32[16,64,128]{2,1,0:T(8,128)S(1)}, f32[8,128,256]{2,1,0:T(8,128)S(1)}) custom-call(f32[128,512]{1,0:T(8,128)S(1)} %masks.1, bf16[528,256]{1,0:T(8,128)(2,1)S(1)} %pack.1.p0, bf16[528,256]{1,0:T(8,128)(2,1)S(1)} %collective-permute-done.5.p1, bf16[2,528,256]{2,1,0:T(8,128)(2,1)S(1)} %collective-permute-done.6.oo, ...), custom_call_target="tpu_custom_call" | custom-call | flops 2000000000 | bytes 4000000 | tf_op jit(solution)/shard_map/near_early/pallas_call | solution.py:206
  57.1 1.8 %collective-permute-done.14.p0 = bf16[528,256]{1,0:T(8,128)(2,1)S(1)} collective-permute-done((bf16[528,256]{1,0:T(8,128)(2,1)S(1)}, bf16[528,256]{1,0:T(8,128)(2,1)S(1)}, u32[]{:S(2)}, u32[]{:S(2)}) %collective-permute-start.14) | collective-permute-done | bytes 270368 | tf_op jit(solution)/shard_map/ppermute | solution.py:68
  58.9 5.7 %collective-permute-done.15.p1 = bf16[528,256]{1,0:T(8,128)(2,1)S(1)} collective-permute-done((bf16[528,256]{1,0:T(8,128)(2,1)S(1)}, bf16[528,256]{1,0:T(8,128)(2,1)S(1)}, u32[]{:S(2)}, u32[]{:S(2)}) %collective-permute-start.15) | collective-permute-done | bytes 270368 | tf_op jit(solution)/shard_map/ppermute | solution.py:68
  64.6 4.2 %near_late.1 = (bf16[16,64,256]{2,1,0:T(8,128)(2,1)S(1)}, f32[16,64,128]{2,1,0:T(8,128)S(1)}, f32[8,128,256]{2,1,0:T(8,128)S(1)}) custom-call(f32[128,512]{1,0:T(8,128)S(1)} %masks.1, bf16[528,256]{1,0:T(8,128)(2,1)S(1)} %collective-permute-done.14.p0, bf16[528,256]{1,0:T(8,128)(2,1)S(1)} %collective-permute-done.15.p1, ...), custom_call_target="tpu_custom_call" | custom-call | flops 2000000000 | bytes 4000000 | tf_op jit(solution)/shard_map/near_late/pallas_call | solution.py:206
  68.8 2.2 %far_late.1 = (bf16[512,256]{1,0:T(8,128)(2,1)S(1)}, bf16[512,256]{1,0:T(8,128)(2,1)S(1)}) custom-call(f32[128,512]{1,0:T(8,128)S(1)} %masks.1, bf16[16,64,256]{2,1,0:T(8,128)(2,1)S(1)} %get-tuple-element.26.state, f32[16,64,128]{2,1,0:T(8,128)S(1)} %get-tuple-element.27.spot, f32[8,128,256]{2,1,0:T(8,128)S(1)} %get-tuple-element.28.near_acc, ...), custom_call_target="tpu_custom_call" | custom-call | flops 500000000 | bytes 4000000 | tf_op jit(solution)/shard_map/far_late/pallas_call | solution.py:243
  71.1 1.5 %collective-permute-start.16 = (bf16[512,256]{1,0:T(8,128)(2,1)S(1)}, bf16[512,256]{1,0:T(8,128)(2,1)S(1)}, u32[]{:S(2)}, u32[]{:S(2)}) collective-permute-start(bf16[512,256]{1,0:T(8,128)(2,1)S(1)} %get-tuple-element.29), channel_id=1, source_target_pairs={{0,2},{1,3},{2,0},{3,1},{4,6},{5,7},{6,4},{7,5},{8,10},{9,11},{10,... | collective-permute-start | bytes 786440 | tf_op jit(solution)/shard_map/ppermute | solution.py:68
  72.5 1.2 %collective-permute-start.17 = (bf16[512,256]{1,0:T(8,128)(2,1)S(1)}, bf16[512,256]{1,0:T(8,128)(2,1)S(1)}, u32[]{:S(2)}, u32[]{:S(2)}) collective-permute-start(bf16[512,256]{1,0:T(8,128)(2,1)S(1)} %get-tuple-element.30), channel_id=1, source_target_pairs={{0,3},{1,2},{2,1},{3,0},{4,7},{5,6},{6,5},{7,4},{8,11},{9,10},{10,... | collective-permute-start | bytes 786440 | tf_op jit(solution)/shard_map/ppermute | solution.py:68
  73.8 2.2 %far_early.1 = (f32[512,256]{1,0:T(8,128)S(1)}, bf16[512,256]{1,0:T(8,128)(2,1)S(1)}) custom-call(f32[128,512]{1,0:T(8,128)S(1)} %masks.1, bf16[16,64,256]{2,1,0:T(8,128)(2,1)S(1)} %get-tuple-element.21.state, f32[16,64,128]{2,1,0:T(8,128)S(1)} %get-tuple-element.22.spot, f32[8,128,256]{2,1,0:T(8,128)S(1)} %get-tuple-element.23.near_acc, ...), custom_call_target="tpu_custom_call" | custom-call | flops 500000000 | bytes 4000000 | tf_op jit(solution)/shard_map/far_early/pallas_call | solution.py:243
  76.0 0.9 collective-permute-start.13
  77.0 4.9 %collective-permute-done.16.x2 = bf16[512,256]{1,0:T(8,128)(2,1)S(1)} collective-permute-done((bf16[512,256]{1,0:T(8,128)(2,1)S(1)}, bf16[512,256]{1,0:T(8,128)(2,1)S(1)}, u32[]{:S(2)}, u32[]{:S(2)}) %collective-permute-start.16) | collective-permute-done | bytes 262176 | tf_op jit(solution)/shard_map/ppermute | solution.py:68
  81.9 4.6 %collective-permute-done.17.x3 = bf16[512,256]{1,0:T(8,128)(2,1)S(1)} collective-permute-done((bf16[512,256]{1,0:T(8,128)(2,1)S(1)}, bf16[512,256]{1,0:T(8,128)(2,1)S(1)}, u32[]{:S(2)}, u32[]{:S(2)}) %collective-permute-start.17) | collective-permute-done | bytes 262176 | tf_op jit(solution)/shard_map/ppermute | solution.py:68
  86.5 0.0 collective-permute-done.13.x1
  86.5 0.1 shard_map.64
  86.6 0.9 collective-permute-start.18
  87.5 7.4 %collective-permute-done.18.got = f32[256,256]{1,0:T(8,128)S(1)} collective-permute-done((f32[256,256]{1,0:T(8,128)S(1)}, f32[256,256]{1,0:T(8,128)S(1)}, u32[]{:S(2)}, u32[]{:S(2)}) %collective-permute-start.18) | collective-permute-done | bytes 262176 | tf_op jit(solution)/shard_map/ppermute | solution.py:53
  94.9 1.3 %collective-permute-start.19 = (f32[64,256]{1,0:T(8,128)S(1)}, f32[64,256]{1,0:T(8,128)S(1)}, u32[]{:S(2)}, u32[]{:S(2)}) collective-permute-start(f32[64,256]{1,0:T(8,128)S(1)} %get-tuple-element.34), channel_id=1, source_target_pairs={{0,8},{1,9},{2,10},{3,11},{4,12},{5,13},{6,14},{7,15},{8,0},{9,1},... | collective-permute-start | bytes 196616 | tf_op jit(solution)/shard_map/ppermute | solution.py:53
  96.3 1.9 %collective-permute-start.20 = (f32[64,256]{1,0:T(8,128)S(1)}, f32[64,256]{1,0:T(8,128)S(1)}, u32[]{:S(2)}, u32[]{:S(2)}) collective-permute-start(f32[64,256]{1,0:T(8,128)S(1)} %get-tuple-element.35), channel_id=1, source_target_pairs={{0,16},{1,17},{2,18},{3,19},{4,20},{5,21},{6,22},{7,23},{8,24},{9,... | collective-permute-start | bytes 196616 | tf_op jit(solution)/shard_map/ppermute | solution.py:53
  98.1 3.4 %collective-permute-start.21 = (f32[64,256]{1,0:T(8,128)S(1)}, f32[64,256]{1,0:T(8,128)S(1)}, u32[]{:S(2)}, u32[]{:S(2)}) collective-permute-start(f32[64,256]{1,0:T(8,128)S(1)} %get-tuple-element.36), channel_id=1, source_target_pairs={{0,24},{1,25},{2,26},{3,27},{4,28},{5,29},{6,30},{7,31},{8,16},{9,... | collective-permute-start | bytes 196616 | tf_op jit(solution)/shard_map/ppermute | solution.py:53
  101.5 3.4 %collective-permute-done.20.z4 = f32[64,256]{1,0:T(8,128)S(1)} collective-permute-done((f32[64,256]{1,0:T(8,128)S(1)}, f32[64,256]{1,0:T(8,128)S(1)}, u32[]{:S(2)}, u32[]{:S(2)}) %collective-permute-start.20) | collective-permute-done | bytes 65568 | tf_op jit(solution)/shard_map/ppermute | solution.py:53
  104.9 2.0 %collective-permute-done.21.z6 = f32[64,256]{1,0:T(8,128)S(1)} collective-permute-done((f32[64,256]{1,0:T(8,128)S(1)}, f32[64,256]{1,0:T(8,128)S(1)}, u32[]{:S(2)}, u32[]{:S(2)}) %collective-permute-start.21) | collective-permute-done | bytes 65568 | tf_op jit(solution)/shard_map/ppermute | solution.py:53
  106.9 0.6 shard_map.66
  (20 shorter events, 0.2 us)
Async XLA Ops:
  0.0 23.4 %collective-permute-start.8 = (bf16[2,512,256]{2,1,0:T(8,128)(2,1)}, bf16[2,512,256]{2,1,0:T(8,128)(2,1)S(1)}, u32[]{:S(2)}, u32[]{:S(2)}) collective-permute-start(bf16[2,512,256]{2,1,0:T(8,128)(2,1)} %bitcast.8), channel_id=1, source_target_pairs={{0,64},{64,128},{128,192},{192,0},{1,65},{65,129},{129,193},{193,1... | collective-permute-start | bytes 1572872 | tf_op jit(solution)/shard_map/ppermute | solution.py:39
  1.6 0.7 copy-start.4
  3.0 7.6 %collective-permute-start = (bf16[80,256]{1,0:T(8,128)(2,1)S(1)}, bf16[80,256]{1,0:T(8,128)(2,1)S(1)}, u32[]{:S(2)}, u32[]{:S(2)}) collective-permute-start(bf16[80,256]{1,0:T(8,128)(2,1)S(1)} %fusion.1), channel_id=1, source_target_pairs={{0,32},{32,0},{1,33},{33,1},{2,34},{34,2},{3,35},{35,3},{4,36},{36... | collective-permute-start | bytes 122888 | tf_op jit(solution)/shard_map/ppermute | solution.py:35
  3.0 8.2 %collective-permute-start.1 = (bf16[80,256]{1,0:T(8,128)(2,1)S(1)}, bf16[80,256]{1,0:T(8,128)(2,1)S(1)}, u32[]{:S(2)}, u32[]{:S(2)}) collective-permute-start(bf16[80,256]{1,0:T(8,128)(2,1)S(1)} %fusion.1), channel_id=1, source_target_pairs={{0,48},{1,49},{2,50},{3,51},{4,52},{5,53},{6,54},{7,55},{8,56},{9,... | collective-permute-start | bytes 122888 | tf_op jit(solution)/shard_map/ppermute | solution.py:63
  9.4 4.5 %collective-permute-start.2 = (bf16[80,256]{1,0:T(8,128)(2,1)S(1)}, bf16[80,256]{1,0:T(8,128)(2,1)S(1)}, u32[]{:S(2)}, u32[]{:S(2)}) collective-permute-start(bf16[80,256]{1,0:T(8,128)(2,1)S(1)} %fusion.1), channel_id=1, source_target_pairs={{0,40},{1,41},{2,42},{3,43},{4,44},{5,45},{6,46},{7,47},{8,32},{9,... | collective-permute-start | bytes 122888 | tf_op jit(solution)/shard_map/ppermute | solution.py:63
  10.6 5.5 %collective-permute-start.3 = (bf16[80,256]{1,0:T(8,128)(2,1)S(1)}, bf16[80,256]{1,0:T(8,128)(2,1)S(1)}, u32[]{:S(2)}, u32[]{:S(2)}) collective-permute-start(bf16[80,256]{1,0:T(8,128)(2,1)S(1)} %fusion.1), channel_id=1, source_target_pairs={{0,56},{1,57},{2,58},{3,59},{4,60},{5,61},{6,62},{7,63},{8,48},{9,... | collective-permute-start | bytes 122888 | tf_op jit(solution)/shard_map/ppermute | solution.py:63
  16.1 1.1 %copy-start.2 = (bf16[2,512]{1,0:T(2,128)(2,1)S(1)}, bf16[2,512]{1,0:T(2,128)(2,1)}, u32[]{:S(2)}) copy-start(bf16[2,512]{1,0:T(2,128)(2,1)} %places.1) | copy-start | bytes 6148
  16.1 7.0 %collective-permute-start.4 = (bf16[320,256]{1,0:T(8,128)(2,1)S(1)}, bf16[320,256]{1,0:T(8,128)(2,1)S(1)}, u32[]{:S(2)}, u32[]{:S(2)}) collective-permute-start(bf16[320,256]{1,0:T(8,128)(2,1)S(1)} %join.1.a), channel_id=1, source_target_pairs={{0,4},{1,5},{2,6},{3,7},{4,0},{5,1},{6,2},{7,3},{8,12},{9,13},{10,... | collective-permute-start | bytes 491528 | tf_op jit(solution)/shard_map/ppermute | solution.py:53
  17.3 1.0 copy-start
  18.3 3.1 %copy-start.3 = (bf16[2,1,512,256]{3,2,1,0:T(8,128)(2,1)S(1)}, bf16[2,1,512,256]{3,2,1,0:T(8,128)(2,1)}, u32[]{:S(2)}) copy-start(bf16[2,1,512,256]{3,2,1,0:T(8,128)(2,1)} %param.10) | copy-start | bytes 1572868
  18.3 15.0 %collective-permute-start.7 = (bf16[2,528,256]{2,1,0:T(8,128)(2,1)S(1)}, bf16[2,528,256]{2,1,0:T(8,128)(2,1)S(1)}, u32[]{:S(2)}, u32[]{:S(2)}) collective-permute-start(bf16[2,528,256]{2,1,0:T(8,128)(2,1)S(1)} %load.1), channel_id=1, source_target_pairs={{0,96},{32,64},{64,160},{96,128},{128,224},{160,192},{192,32},{224... | collective-permute-start | bytes 1622024 | tf_op jit(solution)/shard_map/ppermute | solution.py:48
  20.3 25.8 %collective-permute-start.9 = (bf16[2,528,256]{2,1,0:T(8,128)(2,1)S(1)}, bf16[2,528,256]{2,1,0:T(8,128)(2,1)S(1)}, u32[]{:S(2)}, u32[]{:S(2)}) collective-permute-start(bf16[2,528,256]{2,1,0:T(8,128)(2,1)S(1)} %load.1), channel_id=1, source_target_pairs={{0,224},{32,192},{64,32},{96,0},{128,96},{160,64},{192,160},{224,1... | collective-permute-start | bytes 1622024 | tf_op jit(solution)/shard_map/ppermute | solution.py:48
  21.4 24.7 %collective-permute-start.10 = (bf16[2,512,256]{2,1,0:T(8,128)(2,1)S(1)}, bf16[2,512,256]{2,1,0:T(8,128)(2,1)S(1)}, u32[]{:S(2)}, u32[]{:S(2)}) collective-permute-start(bf16[2,512,256]{2,1,0:T(8,128)(2,1)S(1)} %bitcast.9), channel_id=1, source_target_pairs={{0,192},{64,0},{128,64},{192,128},{1,193},{65,1},{129,65},{193,129... | collective-permute-start | bytes 1572872 | tf_op jit(solution)/shard_map/ppermute | solution.py:39
  23.1 29.8 %collective-permute-start.6 = (bf16[2,528,256]{2,1,0:T(8,128)(2,1)S(1)}, bf16[2,528,256]{2,1,0:T(8,128)(2,1)S(1)}, u32[]{:S(2)}, u32[]{:S(2)}) collective-permute-start(bf16[2,528,256]{2,1,0:T(8,128)(2,1)S(1)} %load.1), channel_id=1, source_target_pairs={{0,32},{32,0},{1,33},{33,1},{2,34},{34,2},{3,35},{35,3},{4,36},{36... | collective-permute-start | bytes 1622024 | tf_op jit(solution)/shard_map/ppermute | solution.py:35
  23.4 27.0 %collective-permute-start.5 = (bf16[528,256]{1,0:T(8,128)(2,1)S(1)}, bf16[528,256]{1,0:T(8,128)(2,1)S(1)}, u32[]{:S(2)}, u32[]{:S(2)}) collective-permute-start(bf16[528,256]{1,0:T(8,128)(2,1)S(1)} %pack.1.p0), channel_id=1, source_target_pairs={{0,1},{1,0},{2,3},{3,2},{4,5},{5,4},{6,7},{7,6},{8,9},{9,8},{10,11... | collective-permute-start | bytes 811016 | tf_op jit(solution)/shard_map/ppermute | solution.py:68
  33.4 19.2 %copy-start.1 = (s32[2,512,16]{1,2,0:T(8,128)S(1)}, s32[2,512,16]{1,2,0:T(8,128)}, u32[]{:S(2)}) copy-start(s32[2,512,16]{1,2,0:T(8,128)} %param.11) | copy-start | bytes 196612
  33.4 35.4 %collective-permute-start.11 = (bf16[1040,256]{1,0:T(8,128)(2,1)S(1)}, bf16[1040,256]{1,0:T(8,128)(2,1)S(1)}, u32[]{:S(2)}, u32[]{:S(2)}) collective-permute-start(bf16[1040,256]{1,0:T(8,128)(2,1)S(1)} %relay.2), channel_id=1, source_target_pairs={{0,64},{64,128},{128,192},{192,0},{1,65},{65,129},{129,193},{193,1... | collective-permute-start | bytes 1597448 | tf_op jit(solution)/shard_map/ppermute | solution.py:39
  46.1 22.7 %collective-permute-start.12 = (bf16[1040,256]{1,0:T(8,128)(2,1)S(1)}, bf16[1040,256]{1,0:T(8,128)(2,1)S(1)}, u32[]{:S(2)}, u32[]{:S(2)}) collective-permute-start(bf16[1040,256]{1,0:T(8,128)(2,1)S(1)} %relay.3), channel_id=1, source_target_pairs={{0,192},{64,0},{128,64},{192,128},{1,193},{65,1},{129,65},{193,129... | collective-permute-start | bytes 1597448 | tf_op jit(solution)/shard_map/ppermute | solution.py:39
  49.1 9.8 %collective-permute-start.14 = (bf16[528,256]{1,0:T(8,128)(2,1)S(1)}, bf16[528,256]{1,0:T(8,128)(2,1)S(1)}, u32[]{:S(2)}, u32[]{:S(2)}) collective-permute-start(bf16[528,256]{1,0:T(8,128)(2,1)S(1)} %pack.1.p0), channel_id=1, source_target_pairs={{0,2},{1,3},{2,0},{3,1},{4,6},{5,7},{6,4},{7,5},{8,10},{9,11},{10,... | collective-permute-start | bytes 811016 | tf_op jit(solution)/shard_map/ppermute | solution.py:68
  50.5 14.1 %collective-permute-start.15 = (bf16[528,256]{1,0:T(8,128)(2,1)S(1)}, bf16[528,256]{1,0:T(8,128)(2,1)S(1)}, u32[]{:S(2)}, u32[]{:S(2)}) collective-permute-start(bf16[528,256]{1,0:T(8,128)(2,1)S(1)} %pack.1.p0), channel_id=1, source_target_pairs={{0,3},{1,2},{2,1},{3,0},{4,7},{5,6},{6,5},{7,4},{8,11},{9,10},{10,... | collective-permute-start | bytes 811016 | tf_op jit(solution)/shard_map/ppermute | solution.py:68
  71.1 10.8 %collective-permute-start.16 = (bf16[512,256]{1,0:T(8,128)(2,1)S(1)}, bf16[512,256]{1,0:T(8,128)(2,1)S(1)}, u32[]{:S(2)}, u32[]{:S(2)}) collective-permute-start(bf16[512,256]{1,0:T(8,128)(2,1)S(1)} %get-tuple-element.29), channel_id=1, source_target_pairs={{0,2},{1,3},{2,0},{3,1},{4,6},{5,7},{6,4},{7,5},{8,10},{9,11},{10,... | collective-permute-start | bytes 786440 | tf_op jit(solution)/shard_map/ppermute | solution.py:68
  72.5 13.9 %collective-permute-start.17 = (bf16[512,256]{1,0:T(8,128)(2,1)S(1)}, bf16[512,256]{1,0:T(8,128)(2,1)S(1)}, u32[]{:S(2)}, u32[]{:S(2)}) collective-permute-start(bf16[512,256]{1,0:T(8,128)(2,1)S(1)} %get-tuple-element.30), channel_id=1, source_target_pairs={{0,3},{1,2},{2,1},{3,0},{4,7},{5,6},{6,5},{7,4},{8,11},{9,10},{10,... | collective-permute-start | bytes 786440 | tf_op jit(solution)/shard_map/ppermute | solution.py:68
  76.0 10.5 %collective-permute-start.13 = (bf16[512,256]{1,0:T(8,128)(2,1)S(1)}, bf16[512,256]{1,0:T(8,128)(2,1)S(1)}, u32[]{:S(2)}, u32[]{:S(2)}) collective-permute-start(bf16[512,256]{1,0:T(8,128)(2,1)S(1)} %get-tuple-element.25), channel_id=1, source_target_pairs={{0,1},{1,0},{2,3},{3,2},{4,5},{5,4},{6,7},{7,6},{8,9},{9,8},{10,11... | collective-permute-start | bytes 786440 | tf_op jit(solution)/shard_map/ppermute | solution.py:68
  86.6 8.3 %collective-permute-start.18 = (f32[256,256]{1,0:T(8,128)S(1)}, f32[256,256]{1,0:T(8,128)S(1)}, u32[]{:S(2)}, u32[]{:S(2)}) collective-permute-start(f32[256,256]{1,0:T(8,128)S(1)} %get-tuple-element.32), channel_id=1, source_target_pairs={{0,4},{1,5},{2,6},{3,7},{4,0},{5,1},{6,2},{7,3},{8,12},{9,13},{10,... | collective-permute-start | bytes 786440 | tf_op jit(solution)/shard_map/ppermute | solution.py:53
  94.9 6.6 %collective-permute-start.19 = (f32[64,256]{1,0:T(8,128)S(1)}, f32[64,256]{1,0:T(8,128)S(1)}, u32[]{:S(2)}, u32[]{:S(2)}) collective-permute-start(f32[64,256]{1,0:T(8,128)S(1)} %get-tuple-element.34), channel_id=1, source_target_pairs={{0,8},{1,9},{2,10},{3,11},{4,12},{5,13},{6,14},{7,15},{8,0},{9,1},... | collective-permute-start | bytes 196616 | tf_op jit(solution)/shard_map/ppermute | solution.py:53
  96.3 8.6 %collective-permute-start.20 = (f32[64,256]{1,0:T(8,128)S(1)}, f32[64,256]{1,0:T(8,128)S(1)}, u32[]{:S(2)}, u32[]{:S(2)}) collective-permute-start(f32[64,256]{1,0:T(8,128)S(1)} %get-tuple-element.35), channel_id=1, source_target_pairs={{0,16},{1,17},{2,18},{3,19},{4,20},{5,21},{6,22},{7,23},{8,24},{9,... | collective-permute-start | bytes 196616 | tf_op jit(solution)/shard_map/ppermute | solution.py:53
  98.1 8.7 %collective-permute-start.21 = (f32[64,256]{1,0:T(8,128)S(1)}, f32[64,256]{1,0:T(8,128)S(1)}, u32[]{:S(2)}, u32[]{:S(2)}) collective-permute-start(f32[64,256]{1,0:T(8,128)S(1)} %get-tuple-element.36), channel_id=1, source_target_pairs={{0,24},{1,25},{2,26},{3,27},{4,28},{5,29},{6,30},{7,31},{8,16},{9,... | collective-permute-start | bytes 196616 | tf_op jit(solution)/shard_map/ppermute | solution.py:53

commit v5 on v4

--- a/solution.py
+++ b/solution.py
@@ -265,23 +265,29 @@
         for ref in (x1, x2, x3):
             total += ref[rows, :].astype(jnp.float32)
         out, k = (send if mask & 1 else keep), mask // 2
-        out[k * SHARD : (k + 1) * SHARD] = total
+        out[k * SHARD : (k + 1) * SHARD] = total.astype(out.dtype)
 
 
 def sum_z1_kernel(keep, got, own, z2, z4, z6):
     for k, out in enumerate((own, z2, z4, z6)):
         rows = slice(k * SHARD, (k + 1) * SHARD)
-        out[...] = keep[rows] + got[rows]
+        out[...] = (keep[rows] + got[rows].astype(jnp.float32)).astype(out.dtype)
 
 
 def sum_z_kernel(own, z2, z4, z6, out):
-    out[...] = own[...] + z2[...] + z4[...] + z6[...]
+    total = own[...]
+    for ref in (z2, z4, z6):
+        total += ref[...].astype(jnp.float32)
+    out[...] = total
 
 
 def small(body, out_rows, *arrays):
     return pl.pallas_call(
         body,
-        out_shape=tuple(jax.ShapeDtypeStruct((r, MEMBERS), jnp.float32) for r in out_rows),
+        out_shape=tuple(
+            jax.ShapeDtypeStruct((rows, MEMBERS), jnp.bfloat16 if n else jnp.float32)
+            for n, rows in enumerate(out_rows)
+        ),
         in_specs=[VMEM] * len(arrays),
         out_specs=(VMEM,) * len(out_rows),
         compiler_params=pltpu.CompilerParams(vmem_limit_bytes=6 << 20),
@@ -330,25 +336,51 @@
     )(*parts)
 
 
-def load_kernel(obs, places, out):
+def load_kernel(
+    state_in, state_pos, obs_in, obs_pos, state, obs, state_places, obs_places, sems
+):
+    copies = [
+        pltpu.make_async_copy(state_pos, state_places, sems.at[0]),
+        pltpu.make_async_copy(state_in.at[0], state.at[:SHARD], sems.at[1]),
+        pltpu.make_async_copy(obs_pos, obs_places, sems.at[2]),
+        pltpu.make_async_copy(obs_in.at[0, 0], obs.at[0, :OBS_ROWS], sems.at[3]),
+        pltpu.make_async_copy(obs_in.at[1, 0], obs.at[1, :OBS_ROWS], sems.at[4]),
+    ]
+    for copy in copies:
+        copy.start()
+    copies[0].wait()
+    held = state_places[...].astype(jnp.float32)
+    row = jnp.concatenate([held, jnp.zeros((1, MEMBERS - SHARD), jnp.float32)], axis=1)
+    rows = jnp.concatenate([row, jnp.zeros((PAD - 1, MEMBERS), jnp.float32)], axis=0)
+    state[SHARD:] = rows.astype(jnp.bfloat16)
+    copies[2].wait()
     for t in range(BATCHES):
-        out[t, :OBS_ROWS] = obs[t]
-        held = places[t : t + 1].astype(jnp.float32)
+        held = obs_places[t : t + 1].astype(jnp.float32)
         rows = [held[:, r * EDGE : (r + 1) * EDGE] for r in range(SPAN)]
         rows.append(jnp.zeros((PAD - SPAN, EDGE), jnp.float32))
-        out[t, OBS_ROWS:, :EDGE] = jnp.concatenate(rows, axis=0).astype(jnp.bfloat16)
-        out[t, OBS_ROWS:, EDGE:] = jnp.zeros((PAD, MEMBERS - EDGE), jnp.bfloat16)
-
-
-def load(obs, places):
+        obs[t, OBS_ROWS:, :EDGE] = jnp.concatenate(rows, axis=0).astype(jnp.bfloat16)
+        obs[t, OBS_ROWS:, EDGE:] = jnp.zeros((PAD, MEMBERS - EDGE), jnp.bfloat16)
+    for k in (1, 3, 4):
+        copies[k].wait()
+
+
+def load(state, state_pos, obs, obs_pos):
     return pl.pallas_call(
         load_kernel,
-        out_shape=jax.ShapeDtypeStruct((BATCHES, OBS_ROWS + PAD, MEMBERS), jnp.bfloat16),
-        in_specs=[VMEM, VMEM],
-        out_specs=VMEM,
+        out_shape=(
+            jax.ShapeDtypeStruct((SHARD + PAD, MEMBERS), jnp.bfloat16),
+            jax.ShapeDtypeStruct((BATCHES, OBS_ROWS + PAD, MEMBERS), jnp.bfloat16),
+        ),
+        in_specs=[pl.BlockSpec(memory_space=pltpu.HBM)] * 4,
+        out_specs=(VMEM, VMEM),
+        scratch_shapes=[
+            pltpu.VMEM((1, SHARD), jnp.bfloat16),
+            pltpu.VMEM((BATCHES, SPAN * EDGE), jnp.bfloat16),
+            pltpu.SemaphoreType.DMA((5,)),
+        ],
         compiler_params=pltpu.CompilerParams(vmem_limit_bytes=8 << 20),
         name="load",
-    )(obs, places)
+    )(state, state_pos, obs, obs_pos)
 
 
 def relay_kernel(batch, obs, weights, out):
@@ -368,9 +400,7 @@
 
 
 def local(ens_state, state_pos, obs_ens, obs_pos, innov_weight, block_rows):
-    state = jnp.concatenate(
-        [ens_state[0], jnp.pad(state_pos[None, :], ((0, PAD - 1), (0, MEMBERS - SHARD)))], axis=0
-    )
+    state, obs = load(ens_state, state_pos[None], obs_ens, obs_pos)
     mine = flip(state)
     parts = [mine]
     for mask in (4, 2, 6):
@@ -385,7 +415,6 @@
     weight = innov_weight[:, 0]
     weight_left = along_rows(weight, 1)
     weight_right = along_rows(weight, ROWS - 1)
-    obs = load(obs_ens[:, 0], obs_pos)
     obs_left = along_rows_flip(obs, 1)
     obs_right = along_rows_flip(obs, ROWS - 1)
     obs_own = flip(obs)

time: 108 us -> 102 us (0.944)
  the two profiles are of different devices: /device:TPU:38 before, /device:TPU:1 now
where the time goes in v5:
time: 102 us; the launch traced here: 101 us
  waiting for transfers between devices  49.5 us (49%)
  starting transfers between devices  35.1 us (34%)
  Pallas kernels  14.2 us (14%)
  local copies, waits for them, and re-layouts  1.82 us (2%)
    ppermute x6, waiting for transfers between devices, swap_x(): return lax.ppermute(value, 'obs', pairs)  16.9 us
    ppermute x4, waiting for transfers between devices, along_rows(): lax.ppermute(value, 'rows', [(s, (s + step) % ROWS) for s in range(ROWS)])  11.7 us
    ppermute x6, starting transfers between devices, swap_x(): return lax.ppermute(value, 'obs', pairs)  8.7 us
    pallas_call x2, Pallas kernels, near(): pl.pallas_call(functools.partial(near_kernel, late), out_shape=(jax.Shape...  8.39 us
    ppermute x2, waiting for transfers between devices, along_rows_flip(): return lax.ppermute(value, ('rows', 'half'), pairs)  8.25 us
    ppermute x3, starting transfers between devices, swap_z_flip(): return lax.ppermute(value, ('half', 'obs'), pairs)  7.58 us
    ppermute x5, starting transfers between devices, swap_z(): return lax.ppermute(value, 'obs', pairs)  7.39 us
    ppermute x5, waiting for transfers between devices, swap_z(): return lax.ppermute(value, 'obs', pairs)  7.1 us
  transfers between devices with their start and end apart: 22, of which 13 were waited for; matrix products, arithmetic and copies ran while one was open for 0% of the time, Pallas kernels for 11%

profile of v5, /device:TPU:1, one launch (start us, length us, event | category | flops | bytes accessed | tf_op | source)
XLA Modules:
  0.0 100.8 jit_solution(13893948296374853713)
XLA Ops:
  0.0 2.1 %collective-permute-start.8 = (bf16[2,512,256]{2,1,0:T(8,128)(2,1)}, bf16[2,512,256]{2,1,0:T(8,128)(2,1)S(1)}, u32[]{:S(2)}, u32[]{:S(2)}) collective-permute-start(bf16[2,512,256]{2,1,0:T(8,128)(2,1)} %bitcast.6), channel_id=1, source_target_pairs={{0,64},{64,128},{128,192},{192,0},{1,65},{65,129},{129,193},{193,1... | collective-permute-start | bytes 1572872 | tf_op jit(solution)/shard_map/ppermute | solution.py:39
  2.1 1.0 %copy-done = bf16[2,1,512,256]{3,2,1,0:T(8,128)(2,1)S(1)} copy-done((bf16[2,1,512,256]{3,2,1,0:T(8,128)(2,1)S(1)}, bf16[2,1,512,256]{3,2,1,0:T(8,128)(2,1)}, u32[]{:S(2)}) %copy-start) | copy-done | bytes 524312
  3.2 0.8 copy-done.2
  3.9 0.1 load.1
  4.1 1.8 %collective-permute-start = (bf16[80,256]{1,0:T(8,128)(2,1)S(1)}, bf16[80,256]{1,0:T(8,128)(2,1)S(1)}, u32[]{:S(2)}, u32[]{:S(2)}) collective-permute-start(bf16[80,256]{1,0:T(8,128)(2,1)S(1)} %get-tuple-element.23), channel_id=1, source_target_pairs={{0,32},{32,0},{1,33},{33,1},{2,34},{34,2},{3,35},{35,3},{4,36},{36... | collective-permute-start | bytes 122888 | tf_op jit(solution)/shard_map/ppermute | solution.py:35
  5.9 6.1 %collective-permute-start.1 = (bf16[80,256]{1,0:T(8,128)(2,1)S(1)}, bf16[80,256]{1,0:T(8,128)(2,1)S(1)}, u32[]{:S(2)}, u32[]{:S(2)}) collective-permute-start(bf16[80,256]{1,0:T(8,128)(2,1)S(1)} %get-tuple-element.23), channel_id=1, source_target_pairs={{0,48},{1,49},{2,50},{3,51},{4,52},{5,53},{6,54},{7,55},{8,56},{9,... | collective-permute-start | bytes 122888 | tf_op jit(solution)/shard_map/ppermute | solution.py:63
  12.0 1.5 %collective-permute-start.2 = (bf16[80,256]{1,0:T(8,128)(2,1)S(1)}, bf16[80,256]{1,0:T(8,128)(2,1)S(1)}, u32[]{:S(2)}, u32[]{:S(2)}) collective-permute-start(bf16[80,256]{1,0:T(8,128)(2,1)S(1)} %get-tuple-element.23), channel_id=1, source_target_pairs={{0,40},{1,41},{2,42},{3,43},{4,44},{5,45},{6,46},{7,47},{8,32},{9,... | collective-permute-start | bytes 122888 | tf_op jit(solution)/shard_map/ppermute | solution.py:63
  13.5 0.0 collective-permute-start.3
  13.5 0.0 collective-permute-done.refs_0_
  13.5 0.4 collective-permute-done.1.refs_1_
  13.9 3.5 %collective-permute-done.2.refs_2_ = bf16[80,256]{1,0:T(8,128)(2,1)S(1)} collective-permute-done((bf16[80,256]{1,0:T(8,128)(2,1)S(1)}, bf16[80,256]{1,0:T(8,128)(2,1)S(1)}, u32[]{:S(2)}, u32[]{:S(2)}) %collective-permute-start.2) | collective-permute-done | bytes 40992 | tf_op jit(solution)/shard_map/ppermute | solution.py:63
  17.4 1.6 %collective-permute-done.3.refs_3_ = bf16[80,256]{1,0:T(8,128)(2,1)S(1)} collective-permute-done((bf16[80,256]{1,0:T(8,128)(2,1)S(1)}, bf16[80,256]{1,0:T(8,128)(2,1)S(1)}, u32[]{:S(2)}, u32[]{:S(2)}) %collective-permute-start.3) | collective-permute-done | bytes 40992 | tf_op jit(solution)/shard_map/ppermute | solution.py:63
  19.0 1.6 %collective-permute-start.4 = (bf16[320,256]{1,0:T(8,128)(2,1)S(1)}, bf16[320,256]{1,0:T(8,128)(2,1)S(1)}, u32[]{:S(2)}, u32[]{:S(2)}) collective-permute-start(bf16[320,256]{1,0:T(8,128)(2,1)S(1)} %join.1.a), channel_id=1, source_target_pairs={{0,4},{1,5},{2,6},{3,7},{4,0},{5,1},{6,2},{7,3},{8,12},{9,13},{10,... | collective-permute-start | bytes 491528 | tf_op jit(solution)/shard_map/ppermute | solution.py:53
  20.6 0.8 collective-permute-start.7
  21.4 2.1 %collective-permute-start.9 = (bf16[2,528,256]{2,1,0:T(8,128)(2,1)S(1)}, bf16[2,528,256]{2,1,0:T(8,128)(2,1)S(1)}, u32[]{:S(2)}, u32[]{:S(2)}) collective-permute-start(bf16[2,528,256]{2,1,0:T(8,128)(2,1)S(1)} %get-tuple-element.24), channel_id=1, source_target_pairs={{0,224},{32,192},{64,32},{96,0},{128,96},{160,64},{192,160},{224,1... | collective-permute-start | bytes 1622024 | tf_op jit(solution)/shard_map/ppermute | solution.py:48
  23.6 0.6 collective-permute-start.10
  24.2 0.6 collective-permute-done.4.b
  24.8 1.0 collective-permute-start.6
  25.8 1.3 %collective-permute-start.5 = (bf16[528,256]{1,0:T(8,128)(2,1)S(1)}, bf16[528,256]{1,0:T(8,128)(2,1)S(1)}, u32[]{:S(2)}, u32[]{:S(2)}) collective-permute-start(bf16[528,256]{1,0:T(8,128)(2,1)S(1)} %pack.1.p0), channel_id=1, source_target_pairs={{0,1},{1,0},{2,3},{3,2},{4,5},{5,4},{6,7},{7,6},{8,9},{9,8},{10,11... | collective-permute-start | bytes 811016 | tf_op jit(solution)/shard_map/ppermute | solution.py:68
  27.1 8.2 %collective-permute-done.7.ol.obs = bf16[2,528,256]{2,1,0:T(8,128)(2,1)S(1)} collective-permute-done((bf16[2,528,256]{2,1,0:T(8,128)(2,1)S(1)}, bf16[2,528,256]{2,1,0:T(8,128)(2,1)S(1)}, u32[]{:S(2)}, u32[]{:S(2)}) %collective-permute-start.7) | collective-permute-done | bytes 540704 | tf_op jit(solution)/shard_map/ppermute | solution.py:48
  35.4 0.0 copy-start.1
  35.4 0.5 collective-permute-start.11
  35.9 11.7 %collective-permute-done.10.wr.weights = bf16[2,512,256]{2,1,0:T(8,128)(2,1)S(1)} collective-permute-done((bf16[2,512,256]{2,1,0:T(8,128)(2,1)S(1)}, bf16[2,512,256]{2,1,0:T(8,128)(2,1)S(1)}, u32[]{:S(2)}, u32[]{:S(2)}) %collective-permute-start.10) | collective-permute-done | bytes 524320 | tf_op jit(solution)/shard_map/ppermute | solution.py:39
  47.5 0.0 collective-permute-done.9.orr.obs
  47.6 2.5 %collective-permute-start.12 = (bf16[1040,256]{1,0:T(8,128)(2,1)S(1)}, bf16[1040,256]{1,0:T(8,128)(2,1)S(1)}, u32[]{:S(2)}, u32[]{:S(2)}) collective-permute-start(bf16[1040,256]{1,0:T(8,128)(2,1)S(1)} %relay.3), channel_id=1, source_target_pairs={{0,192},{64,0},{128,64},{192,128},{1,193},{65,1},{129,65},{193,129... | collective-permute-start | bytes 1597448 | tf_op jit(solution)/shard_map/ppermute | solution.py:39
  50.1 2.7 %collective-permute-start.14 = (bf16[528,256]{1,0:T(8,128)(2,1)S(1)}, bf16[528,256]{1,0:T(8,128)(2,1)S(1)}, u32[]{:S(2)}, u32[]{:S(2)}) collective-permute-start(bf16[528,256]{1,0:T(8,128)(2,1)S(1)} %pack.1.p0), channel_id=1, source_target_pairs={{0,2},{1,3},{2,0},{3,1},{4,6},{5,7},{6,4},{7,5},{8,10},{9,11},{10,... | collective-permute-start | bytes 811016 | tf_op jit(solution)/shard_map/ppermute | solution.py:68
  52.8 0.9 collective-permute-start.15
  53.7 0.3 masks.1
  54.0 4.2 %near_early.1 = (bf16[16,64,256]{2,1,0:T(8,128)(2,1)S(1)}, f32[16,64,128]{2,1,0:T(8,128)S(1)}, f32[8,128,256]{2,1,0:T(8,128)S(1)}) custom-call(f32[128,512]{1,0:T(8,128)S(1)} %masks.1, bf16[528,256]{1,0:T(8,128)(2,1)S(1)} %pack.1.p0, bf16[528,256]{1,0:T(8,128)(2,1)S(1)} %collective-permute-done.5.p1, bf16[2,528,256]{2,1,0:T(8,128)(2,1)S(1)} %collective-permute-done.6.oo, ...), custom_call_target="tpu_custom_call" | custom-call | flops 2000000000 | bytes 4000000 | tf_op jit(solution)/shard_map/near_early/pallas_call | solution.py:206
  58.2 0.8 collective-permute-done.14.p0
  59.0 6.8 %collective-permute-done.15.p1 = bf16[528,256]{1,0:T(8,128)(2,1)S(1)} collective-permute-done((bf16[528,256]{1,0:T(8,128)(2,1)S(1)}, bf16[528,256]{1,0:T(8,128)(2,1)S(1)}, u32[]{:S(2)}, u32[]{:S(2)}) %collective-permute-start.15) | collective-permute-done | bytes 270368 | tf_op jit(solution)/shard_map/ppermute | solution.py:68
  65.8 4.2 %near_late.1 = (bf16[16,64,256]{2,1,0:T(8,128)(2,1)S(1)}, f32[16,64,128]{2,1,0:T(8,128)S(1)}, f32[8,128,256]{2,1,0:T(8,128)S(1)}) custom-call(f32[128,512]{1,0:T(8,128)S(1)} %masks.1, bf16[528,256]{1,0:T(8,128)(2,1)S(1)} %collective-permute-done.14.p0, bf16[528,256]{1,0:T(8,128)(2,1)S(1)} %collective-permute-done.15.p1, ...), custom_call_target="tpu_custom_call" | custom-call | flops 2000000000 | bytes 4000000 | tf_op jit(solution)/shard_map/near_late/pallas_call | solution.py:206
  70.0 2.2 %far_late.1 = (bf16[512,256]{1,0:T(8,128)(2,1)S(1)}, bf16[512,256]{1,0:T(8,128)(2,1)S(1)}) custom-call(f32[128,512]{1,0:T(8,128)S(1)} %masks.1, bf16[16,64,256]{2,1,0:T(8,128)(2,1)S(1)} %get-tuple-element.30.state, f32[16,64,128]{2,1,0:T(8,128)S(1)} %get-tuple-element.31.spot, f32[8,128,256]{2,1,0:T(8,128)S(1)} %get-tuple-element.32.near_acc, ...), custom_call_target="tpu_custom_call" | custom-call | flops 500000000 | bytes 4000000 | tf_op jit(solution)/shard_map/far_late/pallas_call | solution.py:243
  72.2 1.1 %collective-permute-start.16 = (bf16[512,256]{1,0:T(8,128)(2,1)S(1)}, bf16[512,256]{1,0:T(8,128)(2,1)S(1)}, u32[]{:S(2)}, u32[]{:S(2)}) collective-permute-start(bf16[512,256]{1,0:T(8,128)(2,1)S(1)} %get-tuple-element.33), channel_id=1, source_target_pairs={{0,2},{1,3},{2,0},{3,1},{4,6},{5,7},{6,4},{7,5},{8,10},{9,11},{10,... | collective-permute-start | bytes 786440 | tf_op jit(solution)/shard_map/ppermute | solution.py:68
  73.3 2.6 %collective-permute-start.17 = (bf16[512,256]{1,0:T(8,128)(2,1)S(1)}, bf16[512,256]{1,0:T(8,128)(2,1)S(1)}, u32[]{:S(2)}, u32[]{:S(2)}) collective-permute-start(bf16[512,256]{1,0:T(8,128)(2,1)S(1)} %get-tuple-element.34), channel_id=1, source_target_pairs={{0,3},{1,2},{2,1},{3,0},{4,7},{5,6},{6,5},{7,4},{8,11},{9,10},{10,... | collective-permute-start | bytes 786440 | tf_op jit(solution)/shard_map/ppermute | solution.py:68
  75.9 2.2 %far_early.1 = (f32[512,256]{1,0:T(8,128)S(1)}, bf16[512,256]{1,0:T(8,128)(2,1)S(1)}) custom-call(f32[128,512]{1,0:T(8,128)S(1)} %masks.1, bf16[16,64,256]{2,1,0:T(8,128)(2,1)S(1)} %get-tuple-element.25.state, f32[16,64,128]{2,1,0:T(8,128)S(1)} %get-tuple-element.26.spot, f32[8,128,256]{2,1,0:T(8,128)S(1)} %get-tuple-element.27.near_acc, ...), custom_call_target="tpu_custom_call" | custom-call | flops 500000000 | bytes 4000000 | tf_op jit(solution)/shard_map/far_early/pallas_call | solution.py:243
  78.2 0.1 collective-permute-start.13
  78.3 3.0 %collective-permute-done.16.x2 = bf16[512,256]{1,0:T(8,128)(2,1)S(1)} collective-permute-done((bf16[512,256]{1,0:T(8,128)(2,1)S(1)}, bf16[512,256]{1,0:T(8,128)(2,1)S(1)}, u32[]{:S(2)}, u32[]{:S(2)}) %collective-permute-start.16) | collective-permute-done | bytes 262176 | tf_op jit(solution)/shard_map/ppermute | solution.py:68
  81.2 6.4 %collective-permute-done.17.x3 = bf16[512,256]{1,0:T(8,128)(2,1)S(1)} collective-permute-done((bf16[512,256]{1,0:T(8,128)(2,1)S(1)}, bf16[512,256]{1,0:T(8,128)(2,1)S(1)}, u32[]{:S(2)}, u32[]{:S(2)}) %collective-permute-start.17) | collective-permute-done | bytes 262176 | tf_op jit(solution)/shard_map/ppermute | solution.py:68
  87.7 0.1 shard_map.64
  87.8 0.1 collective-permute-start.18
  87.9 4.4 %collective-permute-done.18.got = bf16[256,256]{1,0:T(8,128)(2,1)S(1)} collective-permute-done((bf16[256,256]{1,0:T(8,128)(2,1)S(1)}, bf16[256,256]{1,0:T(8,128)(2,1)S(1)}, u32[]{:S(2)}, u32[]{:S(2)}) %collective-permute-start.18) | collective-permute-done | bytes 131104 | tf_op jit(solution)/shard_map/ppermute | solution.py:53
  92.3 0.6 collective-permute-start.19
  92.9 1.8 %collective-permute-start.20 = (bf16[64,256]{1,0:T(8,128)(2,1)S(1)}, bf16[64,256]{1,0:T(8,128)(2,1)S(1)}, u32[]{:S(2)}, u32[]{:S(2)}) collective-permute-start(bf16[64,256]{1,0:T(8,128)(2,1)S(1)} %get-tuple-element.39), channel_id=1, source_target_pairs={{0,16},{1,17},{2,18},{3,19},{4,20},{5,21},{6,22},{7,23},{8,24},{9,... | collective-permute-start | bytes 98312 | tf_op jit(solution)/shard_map/ppermute | solution.py:53
  94.7 3.4 %collective-permute-start.21 = (bf16[64,256]{1,0:T(8,128)(2,1)S(1)}, bf16[64,256]{1,0:T(8,128)(2,1)S(1)}, u32[]{:S(2)}, u32[]{:S(2)}) collective-permute-start(bf16[64,256]{1,0:T(8,128)(2,1)S(1)} %get-tuple-element.40), channel_id=1, source_target_pairs={{0,24},{1,25},{2,26},{3,27},{4,28},{5,29},{6,30},{7,31},{8,16},{9,... | collective-permute-start | bytes 98312 | tf_op jit(solution)/shard_map/ppermute | solution.py:53
  98.1 1.6 %collective-permute-done.20.z4 = bf16[64,256]{1,0:T(8,128)(2,1)S(1)} collective-permute-done((bf16[64,256]{1,0:T(8,128)(2,1)S(1)}, bf16[64,256]{1,0:T(8,128)(2,1)S(1)}, u32[]{:S(2)}, u32[]{:S(2)}) %collective-permute-start.20) | collective-permute-done | bytes 32800 | tf_op jit(solution)/shard_map/ppermute | solution.py:53
  99.7 0.5 collective-permute-done.21.z6
  100.2 0.6 shard_map.66
  (21 shorter events, 0.2 us)
Async XLA Ops:
  0.0 2.1 %copy-start.3 = (bf16[2,512]{1,0:T(2,128)(2,1)S(1)}, bf16[2,512]{1,0:T(2,128)(2,1)}, u32[]{:S(2)}) copy-start(bf16[2,512]{1,0:T(2,128)(2,1)} %obs_pos.1) | copy-start | bytes 6148
  0.0 2.1 %copy-start.4 = (bf16[64]{0:T(256)(128)(2,1)S(1)}, bf16[64]{0:T(256)(128)(2,1)}, u32[]{:S(2)}) copy-start(bf16[64]{0:T(256)(128)(2,1)} %param.7) | copy-start | bytes 388
  0.0 25.8 %collective-permute-start.8 = (bf16[2,512,256]{2,1,0:T(8,128)(2,1)}, bf16[2,512,256]{2,1,0:T(8,128)(2,1)S(1)}, u32[]{:S(2)}, u32[]{:S(2)}) collective-permute-start(bf16[2,512,256]{2,1,0:T(8,128)(2,1)} %bitcast.6), channel_id=1, source_target_pairs={{0,64},{64,128},{128,192},{192,0},{1,65},{65,129},{129,193},{193,1... | collective-permute-start | bytes 1572872 | tf_op jit(solution)/shard_map/ppermute | solution.py:39
  2.1 1.0 %copy-start = (bf16[2,1,512,256]{3,2,1,0:T(8,128)(2,1)S(1)}, bf16[2,1,512,256]{3,2,1,0:T(8,128)(2,1)}, u32[]{:S(2)}) copy-start(bf16[2,1,512,256]{3,2,1,0:T(8,128)(2,1)} %obs_in.1) | copy-start | bytes 1572868
  3.2 0.8 copy-start.2
  3.9 19.6 %copy-start.5 = (bf16[2,1,512,256]{3,2,1,0:T(8,128)(2,1)S(1)}, bf16[2,1,512,256]{3,2,1,0:T(8,128)(2,1)}, u32[]{:S(2)}) copy-start(bf16[2,1,512,256]{3,2,1,0:T(8,128)(2,1)} %param.10) | copy-start | bytes 1572868
  4.1 9.4 %collective-permute-start = (bf16[80,256]{1,0:T(8,128)(2,1)S(1)}, bf16[80,256]{1,0:T(8,128)(2,1)S(1)}, u32[]{:S(2)}, u32[]{:S(2)}) collective-permute-start(bf16[80,256]{1,0:T(8,128)(2,1)S(1)} %get-tuple-element.23), channel_id=1, source_target_pairs={{0,32},{32,0},{1,33},{33,1},{2,34},{34,2},{3,35},{35,3},{4,36},{36... | collective-permute-start | bytes 122888 | tf_op jit(solution)/shard_map/ppermute | solution.py:35
  5.9 8.0 %collective-permute-start.1 = (bf16[80,256]{1,0:T(8,128)(2,1)S(1)}, bf16[80,256]{1,0:T(8,128)(2,1)S(1)}, u32[]{:S(2)}, u32[]{:S(2)}) collective-permute-start(bf16[80,256]{1,0:T(8,128)(2,1)S(1)} %get-tuple-element.23), channel_id=1, source_target_pairs={{0,48},{1,49},{2,50},{3,51},{4,52},{5,53},{6,54},{7,55},{8,56},{9,... | collective-permute-start | bytes 122888 | tf_op jit(solution)/shard_map/ppermute | solution.py:63
  12.0 5.4 %collective-permute-start.2 = (bf16[80,256]{1,0:T(8,128)(2,1)S(1)}, bf16[80,256]{1,0:T(8,128)(2,1)S(1)}, u32[]{:S(2)}, u32[]{:S(2)}) collective-permute-start(bf16[80,256]{1,0:T(8,128)(2,1)S(1)} %get-tuple-element.23), channel_id=1, source_target_pairs={{0,40},{1,41},{2,42},{3,43},{4,44},{5,45},{6,46},{7,47},{8,32},{9,... | collective-permute-start | bytes 122888 | tf_op jit(solution)/shard_map/ppermute | solution.py:63
  13.5 5.5 %collective-permute-start.3 = (bf16[80,256]{1,0:T(8,128)(2,1)S(1)}, bf16[80,256]{1,0:T(8,128)(2,1)S(1)}, u32[]{:S(2)}, u32[]{:S(2)}) collective-permute-start(bf16[80,256]{1,0:T(8,128)(2,1)S(1)} %get-tuple-element.23), channel_id=1, source_target_pairs={{0,56},{1,57},{2,58},{3,59},{4,60},{5,61},{6,62},{7,63},{8,48},{9,... | collective-permute-start | bytes 122888 | tf_op jit(solution)/shard_map/ppermute | solution.py:63
  19.0 5.7 %collective-permute-start.4 = (bf16[320,256]{1,0:T(8,128)(2,1)S(1)}, bf16[320,256]{1,0:T(8,128)(2,1)S(1)}, u32[]{:S(2)}, u32[]{:S(2)}) collective-permute-start(bf16[320,256]{1,0:T(8,128)(2,1)S(1)} %join.1.a), channel_id=1, source_target_pairs={{0,4},{1,5},{2,6},{3,7},{4,0},{5,1},{6,2},{7,3},{8,12},{9,13},{10,... | collective-permute-start | bytes 491528 | tf_op jit(solution)/shard_map/ppermute | solution.py:53
  20.6 14.7 %collective-permute-start.7 = (bf16[2,528,256]{2,1,0:T(8,128)(2,1)S(1)}, bf16[2,528,256]{2,1,0:T(8,128)(2,1)S(1)}, u32[]{:S(2)}, u32[]{:S(2)}) collective-permute-start(bf16[2,528,256]{2,1,0:T(8,128)(2,1)S(1)} %get-tuple-element.24), channel_id=1, source_target_pairs={{0,96},{32,64},{64,160},{96,128},{128,224},{160,192},{192,32},{224... | collective-permute-start | bytes 1622024 | tf_op jit(solution)/shard_map/ppermute | solution.py:48
  21.4 26.1 %collective-permute-start.9 = (bf16[2,528,256]{2,1,0:T(8,128)(2,1)S(1)}, bf16[2,528,256]{2,1,0:T(8,128)(2,1)S(1)}, u32[]{:S(2)}, u32[]{:S(2)}) collective-permute-start(bf16[2,528,256]{2,1,0:T(8,128)(2,1)S(1)} %get-tuple-element.24), channel_id=1, source_target_pairs={{0,224},{32,192},{64,32},{96,0},{128,96},{160,64},{192,160},{224,1... | collective-permute-start | bytes 1622024 | tf_op jit(solution)/shard_map/ppermute | solution.py:48
  23.6 24.0 %collective-permute-start.10 = (bf16[2,512,256]{2,1,0:T(8,128)(2,1)S(1)}, bf16[2,512,256]{2,1,0:T(8,128)(2,1)S(1)}, u32[]{:S(2)}, u32[]{:S(2)}) collective-permute-start(bf16[2,512,256]{2,1,0:T(8,128)(2,1)S(1)} %bitcast.7), channel_id=1, source_target_pairs={{0,192},{64,0},{128,64},{192,128},{1,193},{65,1},{129,65},{193,129... | collective-permute-start | bytes 1572872 | tf_op jit(solution)/shard_map/ppermute | solution.py:39
  24.8 29.2 %collective-permute-start.6 = (bf16[2,528,256]{2,1,0:T(8,128)(2,1)S(1)}, bf16[2,528,256]{2,1,0:T(8,128)(2,1)S(1)}, u32[]{:S(2)}, u32[]{:S(2)}) collective-permute-start(bf16[2,528,256]{2,1,0:T(8,128)(2,1)S(1)} %get-tuple-element.24), channel_id=1, source_target_pairs={{0,32},{32,0},{1,33},{33,1},{2,34},{34,2},{3,35},{35,3},{4,36},{36... | collective-permute-start | bytes 1622024 | tf_op jit(solution)/shard_map/ppermute | solution.py:35
  25.8 27.0 %collective-permute-start.5 = (bf16[528,256]{1,0:T(8,128)(2,1)S(1)}, bf16[528,256]{1,0:T(8,128)(2,1)S(1)}, u32[]{:S(2)}, u32[]{:S(2)}) collective-permute-start(bf16[528,256]{1,0:T(8,128)(2,1)S(1)} %pack.1.p0), channel_id=1, source_target_pairs={{0,1},{1,0},{2,3},{3,2},{4,5},{5,4},{6,7},{7,6},{8,9},{9,8},{10,11... | collective-permute-start | bytes 811016 | tf_op jit(solution)/shard_map/ppermute | solution.py:68
  35.4 18.3 %copy-start.1 = (s32[2,512,16]{1,2,0:T(8,128)S(1)}, s32[2,512,16]{1,2,0:T(8,128)}, u32[]{:S(2)}) copy-start(s32[2,512,16]{1,2,0:T(8,128)} %param.11) | copy-start | bytes 196612
  35.4 34.6 %collective-permute-start.11 = (bf16[1040,256]{1,0:T(8,128)(2,1)S(1)}, bf16[1040,256]{1,0:T(8,128)(2,1)S(1)}, u32[]{:S(2)}, u32[]{:S(2)}) collective-permute-start(bf16[1040,256]{1,0:T(8,128)(2,1)S(1)} %relay.2), channel_id=1, source_target_pairs={{0,64},{64,128},{128,192},{192,0},{1,65},{65,129},{129,193},{193,1... | collective-permute-start | bytes 1597448 | tf_op jit(solution)/shard_map/ppermute | solution.py:39
  47.6 22.4 %collective-permute-start.12 = (bf16[1040,256]{1,0:T(8,128)(2,1)S(1)}, bf16[1040,256]{1,0:T(8,128)(2,1)S(1)}, u32[]{:S(2)}, u32[]{:S(2)}) collective-permute-start(bf16[1040,256]{1,0:T(8,128)(2,1)S(1)} %relay.3), channel_id=1, source_target_pairs={{0,192},{64,0},{128,64},{192,128},{1,193},{65,1},{129,65},{193,129... | collective-permute-start | bytes 1597448 | tf_op jit(solution)/shard_map/ppermute | solution.py:39
  50.1 8.9 %collective-permute-start.14 = (bf16[528,256]{1,0:T(8,128)(2,1)S(1)}, bf16[528,256]{1,0:T(8,128)(2,1)S(1)}, u32[]{:S(2)}, u32[]{:S(2)}) collective-permute-start(bf16[528,256]{1,0:T(8,128)(2,1)S(1)} %pack.1.p0), channel_id=1, source_target_pairs={{0,2},{1,3},{2,0},{3,1},{4,6},{5,7},{6,4},{7,5},{8,10},{9,11},{10,... | collective-permute-start | bytes 811016 | tf_op jit(solution)/shard_map/ppermute | solution.py:68
  52.8 13.0 %collective-permute-start.15 = (bf16[528,256]{1,0:T(8,128)(2,1)S(1)}, bf16[528,256]{1,0:T(8,128)(2,1)S(1)}, u32[]{:S(2)}, u32[]{:S(2)}) collective-permute-start(bf16[528,256]{1,0:T(8,128)(2,1)S(1)} %pack.1.p0), channel_id=1, source_target_pairs={{0,3},{1,2},{2,1},{3,0},{4,7},{5,6},{6,5},{7,4},{8,11},{9,10},{10,... | collective-permute-start | bytes 811016 | tf_op jit(solution)/shard_map/ppermute | solution.py:68
  72.2 9.0 %collective-permute-start.16 = (bf16[512,256]{1,0:T(8,128)(2,1)S(1)}, bf16[512,256]{1,0:T(8,128)(2,1)S(1)}, u32[]{:S(2)}, u32[]{:S(2)}) collective-permute-start(bf16[512,256]{1,0:T(8,128)(2,1)S(1)} %get-tuple-element.33), channel_id=1, source_target_pairs={{0,2},{1,3},{2,0},{3,1},{4,6},{5,7},{6,4},{7,5},{8,10},{9,11},{10,... | collective-permute-start | bytes 786440 | tf_op jit(solution)/shard_map/ppermute | solution.py:68
  73.3 14.3 %collective-permute-start.17 = (bf16[512,256]{1,0:T(8,128)(2,1)S(1)}, bf16[512,256]{1,0:T(8,128)(2,1)S(1)}, u32[]{:S(2)}, u32[]{:S(2)}) collective-permute-start(bf16[512,256]{1,0:T(8,128)(2,1)S(1)} %get-tuple-element.34), channel_id=1, source_target_pairs={{0,3},{1,2},{2,1},{3,0},{4,7},{5,6},{6,5},{7,4},{8,11},{9,10},{10,... | collective-permute-start | bytes 786440 | tf_op jit(solution)/shard_map/ppermute | solution.py:68
  78.2 9.5 %collective-permute-start.13 = (bf16[512,256]{1,0:T(8,128)(2,1)S(1)}, bf16[512,256]{1,0:T(8,128)(2,1)S(1)}, u32[]{:S(2)}, u32[]{:S(2)}) collective-permute-start(bf16[512,256]{1,0:T(8,128)(2,1)S(1)} %get-tuple-element.29), channel_id=1, source_target_pairs={{0,1},{1,0},{2,3},{3,2},{4,5},{5,4},{6,7},{7,6},{8,9},{9,8},{10,11... | collective-permute-start | bytes 786440 | tf_op jit(solution)/shard_map/ppermute | solution.py:68
  87.8 4.5 %collective-permute-start.18 = (bf16[256,256]{1,0:T(8,128)(2,1)S(1)}, bf16[256,256]{1,0:T(8,128)(2,1)S(1)}, u32[]{:S(2)}, u32[]{:S(2)}) collective-permute-start(bf16[256,256]{1,0:T(8,128)(2,1)S(1)} %get-tuple-element.36), channel_id=1, source_target_pairs={{0,4},{1,5},{2,6},{3,7},{4,0},{5,1},{6,2},{7,3},{8,12},{9,13},{10,... | collective-permute-start | bytes 393224 | tf_op jit(solution)/shard_map/ppermute | solution.py:53
  92.3 5.7 %collective-permute-start.19 = (bf16[64,256]{1,0:T(8,128)(2,1)S(1)}, bf16[64,256]{1,0:T(8,128)(2,1)S(1)}, u32[]{:S(2)}, u32[]{:S(2)}) collective-permute-start(bf16[64,256]{1,0:T(8,128)(2,1)S(1)} %get-tuple-element.38), channel_id=1, source_target_pairs={{0,8},{1,9},{2,10},{3,11},{4,12},{5,13},{6,14},{7,15},{8,0},{9,1},... | collective-permute-start | bytes 98312 | tf_op jit(solution)/shard_map/ppermute | solution.py:53
  92.9 6.8 %collective-permute-start.20 = (bf16[64,256]{1,0:T(8,128)(2,1)S(1)}, bf16[64,256]{1,0:T(8,128)(2,1)S(1)}, u32[]{:S(2)}, u32[]{:S(2)}) collective-permute-start(bf16[64,256]{1,0:T(8,128)(2,1)S(1)} %get-tuple-element.39), channel_id=1, source_target_pairs={{0,16},{1,17},{2,18},{3,19},{4,20},{5,21},{6,22},{7,23},{8,24},{9,... | collective-permute-start | bytes 98312 | tf_op jit(solution)/shard_map/ppermute | solution.py:53
  94.7 5.5 %collective-permute-start.21 = (bf16[64,256]{1,0:T(8,128)(2,1)S(1)}, bf16[64,256]{1,0:T(8,128)(2,1)S(1)}, u32[]{:S(2)}, u32[]{:S(2)}) collective-permute-start(bf16[64,256]{1,0:T(8,128)(2,1)S(1)} %get-tuple-element.40), channel_id=1, source_target_pairs={{0,24},{1,25},{2,26},{3,27},{4,28},{5,29},{6,30},{7,31},{8,16},{9,... | collective-permute-start | bytes 98312 | tf_op jit(solution)/shard_map/ppermute | solution.py:53

commit v6 on v5

--- a/solution.py
+++ b/solution.py
@@ -20,7 +20,7 @@
 NAMED = 16
 OBS_ROWS = SPAN * EDGE
 PAD = 16
-Z_ORDER = (0, 4, 2, 6, 1, 5, 3, 7)
+Z_ORDER = (0, 1, 4, 5, 2, 3, 6, 7)
 
 TURNS = (0, ROWS - 1, 1, 2)
 SPAN_KEYS = BATCHES * RANGE_BLOCKS
@@ -257,28 +257,28 @@
     )(masks, state, spot, acc, *arrays)
 
 
-def sum_x_kernel(own, x1, x2, x3, keep, send):
+def sum_x_kernel(own, x1, x2, x3, keep, z2, z4, z6):
     my_z = lax.shift_right_logical(lax.axis_index("obs"), 2)
     for mask in range(NZ):
         rows = pl.ds(pl.multiple_of(jnp.bitwise_xor(my_z, mask) * SHARD, SHARD), SHARD)
         total = own[rows, :]
         for ref in (x1, x2, x3):
             total += ref[rows, :].astype(jnp.float32)
-        out, k = (send if mask & 1 else keep), mask // 2
+        out, k = (keep, z2, z4, z6)[mask // 2], mask & 1
         out[k * SHARD : (k + 1) * SHARD] = total.astype(out.dtype)
 
 
-def sum_z1_kernel(keep, got, own, z2, z4, z6):
-    for k, out in enumerate((own, z2, z4, z6)):
+def sum_z_kernel(keep, z2, z4, z6, own, send):
+    for k, out in enumerate((own, send)):
         rows = slice(k * SHARD, (k + 1) * SHARD)
-        out[...] = (keep[rows] + got[rows].astype(jnp.float32)).astype(out.dtype)
-
-
-def sum_z_kernel(own, z2, z4, z6, out):
-    total = own[...]
-    for ref in (z2, z4, z6):
-        total += ref[...].astype(jnp.float32)
-    out[...] = total
+        total = keep[rows]
+        for ref in (z2, z4, z6):
+            total += ref[rows].astype(jnp.float32)
+        out[...] = total.astype(out.dtype)
+
+
+def sum_pair_kernel(own, other, out):
+    out[...] = own[...] + other[...].astype(jnp.float32)
 
 
 def small(body, out_rows, *arrays):
@@ -294,45 +294,29 @@
     )(*arrays)
 
 
-def pack_kernel(a, b, out):
-    held = SHARD + PAD
+def pack_kernel(*refs):
+    out = refs[-1]
+    held = (refs[0].shape[0] - PAD) // SHARD
     places = []
-    for p in range(NZ):
-        ref, q = (a, p) if p < NZ // 2 else (b, p - NZ // 2)
-        out[p * SHARD : (p + 1) * SHARD] = ref[q * held : q * held + SHARD]
-        places.append(ref[q * held + SHARD : (q + 1) * held].astype(jnp.float32)[:1])
-    places.append(jnp.zeros((PAD - NZ, MEMBERS), jnp.float32))
-    out[NZ * SHARD :] = jnp.concatenate(places, axis=0).astype(jnp.bfloat16)
-
-
-def pack(a, b):
+    for q, ref in enumerate(refs[:-1]):
+        for i in range(held):
+            p = q * held + i
+            out[p * SHARD : (p + 1) * SHARD] = ref[i * SHARD : (i + 1) * SHARD]
+        places.append(ref[held * SHARD :].astype(jnp.float32)[:held])
+    count = held * (len(refs) - 1)
+    places.append(jnp.zeros((PAD - count, MEMBERS), jnp.float32))
+    out[count * SHARD :] = jnp.concatenate(places, axis=0).astype(jnp.bfloat16)
+
+
+def pack(*parts):
+    count = len(parts) * (parts[0].shape[0] - PAD) // SHARD
     return pl.pallas_call(
         pack_kernel,
-        out_shape=jax.ShapeDtypeStruct((NZ * SHARD + PAD, MEMBERS), jnp.bfloat16),
-        in_specs=[VMEM, VMEM],
+        out_shape=jax.ShapeDtypeStruct((count * SHARD + PAD, MEMBERS), jnp.bfloat16),
+        in_specs=[VMEM] * len(parts),
         out_specs=VMEM,
         compiler_params=pltpu.CompilerParams(vmem_limit_bytes=4 << 20),
         name="pack",
-    )(a, b)
-
-
-def join_kernel(*refs):
-    out = refs[-1]
-    start = 0
-    for ref in refs[:-1]:
-        out[start : start + ref.shape[0]] = ref[...]
-        start += ref.shape[0]
-
-
-def join(*parts):
-    rows = sum(part.shape[0] for part in parts)
-    return pl.pallas_call(
-        join_kernel,
-        out_shape=jax.ShapeDtypeStruct((rows, MEMBERS), jnp.bfloat16),
-        in_specs=[VMEM] * len(parts),
-        out_specs=VMEM,
-        compiler_params=pltpu.CompilerParams(vmem_limit_bytes=4 << 20),
-        name="join",
     )(*parts)
 
 
@@ -402,12 +386,12 @@
 def local(ens_state, state_pos, obs_ens, obs_pos, innov_weight, block_rows):
     state, obs = load(ens_state, state_pos[None], obs_ens, obs_pos)
     mine = flip(state)
-    parts = [mine]
+    other = swap_z_flip(state, 1)
+    state = pack(mine, other)
+    parts = [state]
     for mask in (4, 2, 6):
-        parts.append(swap_z_flip(state, mask))
-    state = join(*parts)
-    other = swap_z(state, 1)
-    state = pack(state, other)
+        parts.append(swap_z(state, mask))
+    state = pack(*parts)
     pieces = [state]
     for k in range(1, NX):
         pieces.append(swap_x(state, k))
@@ -433,12 +417,12 @@
     own, part1 = far(0, masks, *early, (far0, far1))
     part1 = swap_x(part1, 1)
     parts = [part1, part2, part3]
-    keep, send = small(sum_x_kernel, (4 * SHARD, 4 * SHARD), own, *parts)
-    got = swap_z(send, 1)
-    own, *parts = small(sum_z1_kernel, (SHARD,) * 4, keep, got)
+    keep, *parts = small(sum_x_kernel, (2 * SHARD,) * 4, own, *parts)
     for k, mask in ((1, 4), (0, 2), (2, 6)):
         parts[k] = swap_z(parts[k], mask)
-    (total,) = small(sum_z_kernel, (SHARD,), own, *parts)
+    own, other = small(sum_z_kernel, (SHARD, SHARD), keep, *parts)
+    other = swap_z(other, 1)
+    (total,) = small(sum_pair_kernel, (SHARD,), own, other)
     return total[None]
 
 

time: 102 us -> 98.9 us (0.970)
  waiting for transfers between devices: 49.5 us -> 42.1 us
  starting transfers between devices: 35.1 us -> 40.3 us
    ppermute x5 -> x7, starting transfers between devices: 7.39 us -> 18.4 us  [swap_z(): return lax.ppermute(value, 'obs', pairs)]
    ppermute x2, waiting for transfers between devices: 8.25 us -> 0.01 us  [along_rows_flip(): return lax.ppermute(value, ('rows', 'half'), pairs)]
    ppermute x3 -> x1, starting transfers between devices: 7.58 us -> 0.82 us  [swap_z_flip(): return lax.ppermute(value, ('half', 'obs'), pairs)]
    ppermute x5 -> x7, waiting for transfers between devices: 7.1 us -> 13.5 us  [swap_z(): return lax.ppermute(value, 'obs', pairs)]
    ppermute x4, waiting for transfers between devices: 11.7 us -> 8.71 us  [along_rows(): lax.ppermute(value, 'rows', [(s, (s + step) % ROWS) for s in range(ROWS)])]
    ppermute x3 -> x1, waiting for transfers between devices: 5.53 us -> 2.85 us  [swap_z_flip(): return lax.ppermute(value, ('half', 'obs'), pairs)]
where the time goes in v6:
time: 98.9 us; the launch traced here: 98.5 us
  waiting for transfers between devices  42.1 us (43%)
  starting transfers between devices  40.3 us (41%)
  Pallas kernels  14.2 us (14%)
  local copies, waits for them, and re-layouts  1.82 us (2%)
    ppermute x7, starting transfers between devices, swap_z(): return lax.ppermute(value, 'obs', pairs)  18.4 us
    ppermute x6, waiting for transfers between devices, swap_x(): return lax.ppermute(value, 'obs', pairs)  16.9 us
    ppermute x7, waiting for transfers between devices, swap_z(): return lax.ppermute(value, 'obs', pairs)  13.5 us
    ppermute x4, waiting for transfers between devices, along_rows(): lax.ppermute(value, 'rows', [(s, (s + step) % ROWS) for s in range(ROWS)])  8.71 us
    ppermute x6, starting transfers between devices, swap_x(): return lax.ppermute(value, 'obs', pairs)  8.7 us
    pallas_call x2, Pallas kernels, near(): pl.pallas_call(functools.partial(near_kernel, late), out_shape=(jax.Shape...  8.39 us
    ppermute x4, starting transfers between devices, along_rows(): lax.ppermute(value, 'rows', [(s, (s + step) % ROWS) for s in range(ROWS)])  5.57 us
    pallas_call x2, Pallas kernels, far(): pl.pallas_call(functools.partial(far_kernel, late), out_shape=(jax.ShapeD...  4.47 us
  transfers between devices with their start and end apart: 22, of which 13 were waited for; matrix products, arithmetic and copies ran while one was open for 0% of the time, Pallas kernels for 11%

profile of v6, /device:TPU:1, one launch (start us, length us, event | category | flops | bytes accessed | tf_op | source)
XLA Modules:
  0.0 98.5 jit_solution(10003735677563514256)
XLA Ops:
  0.0 2.1 %collective-permute-start.8 = (bf16[2,512,256]{2,1,0:T(8,128)(2,1)}, bf16[2,512,256]{2,1,0:T(8,128)(2,1)S(1)}, u32[]{:S(2)}, u32[]{:S(2)}) collective-permute-start(bf16[2,512,256]{2,1,0:T(8,128)(2,1)} %bitcast.6), channel_id=1, source_target_pairs={{0,64},{64,128},{128,192},{192,0},{1,65},{65,129},{129,193},{193,1... | collective-permute-start | bytes 1572872 | tf_op jit(solution)/shard_map/ppermute | solution.py:39
  2.1 1.0 %copy-done = bf16[2,1,512,256]{3,2,1,0:T(8,128)(2,1)S(1)} copy-done((bf16[2,1,512,256]{3,2,1,0:T(8,128)(2,1)S(1)}, bf16[2,1,512,256]{3,2,1,0:T(8,128)(2,1)}, u32[]{:S(2)}) %copy-start) | copy-done | bytes 524312
  3.2 0.8 copy-done.2
  3.9 0.1 load.1
  4.1 1.8 %collective-permute-start = (bf16[80,256]{1,0:T(8,128)(2,1)S(1)}, bf16[80,256]{1,0:T(8,128)(2,1)S(1)}, u32[]{:S(2)}, u32[]{:S(2)}) collective-permute-start(bf16[80,256]{1,0:T(8,128)(2,1)S(1)} %get-tuple-element.23), channel_id=1, source_target_pairs={{0,32},{32,0},{1,33},{33,1},{2,34},{34,2},{3,35},{35,3},{4,36},{36... | collective-permute-start | bytes 122888 | tf_op jit(solution)/shard_map/ppermute | solution.py:35
  5.9 0.8 collective-permute-start.1
  6.7 0.1 collective-permute-done.refs_0_
  6.8 2.9 %collective-permute-done.1.refs_1_ = bf16[80,256]{1,0:T(8,128)(2,1)S(1)} collective-permute-done((bf16[80,256]{1,0:T(8,128)(2,1)S(1)}, bf16[80,256]{1,0:T(8,128)(2,1)S(1)}, u32[]{:S(2)}, u32[]{:S(2)}) %collective-permute-start.1) | collective-permute-done | bytes 40992 | tf_op jit(solution)/shard_map/ppermute | solution.py:63
  9.6 6.2 %collective-permute-start.2 = (bf16[144,256]{1,0:T(8,128)(2,1)S(1)}, bf16[144,256]{1,0:T(8,128)(2,1)S(1)}, u32[]{:S(2)}, u32[]{:S(2)}) collective-permute-start(bf16[144,256]{1,0:T(8,128)(2,1)S(1)} %pack.2.refs_0_), channel_id=1, source_target_pairs={{0,16},{1,17},{2,18},{3,19},{4,20},{5,21},{6,22},{7,23},{8,24},{9,... | collective-permute-start | bytes 221192 | tf_op jit(solution)/shard_map/ppermute | solution.py:53
  15.8 1.3 %collective-permute-start.7 = (bf16[2,528,256]{2,1,0:T(8,128)(2,1)S(1)}, bf16[2,528,256]{2,1,0:T(8,128)(2,1)S(1)}, u32[]{:S(2)}, u32[]{:S(2)}) collective-permute-start(bf16[2,528,256]{2,1,0:T(8,128)(2,1)S(1)} %get-tuple-element.24), channel_id=1, source_target_pairs={{0,96},{32,64},{64,160},{96,128},{128,224},{160,192},{192,32},{224... | collective-permute-start | bytes 1622024 | tf_op jit(solution)/shard_map/ppermute | solution.py:48
  17.1 1.7 %collective-permute-start.9 = (bf16[2,528,256]{2,1,0:T(8,128)(2,1)S(1)}, bf16[2,528,256]{2,1,0:T(8,128)(2,1)S(1)}, u32[]{:S(2)}, u32[]{:S(2)}) collective-permute-start(bf16[2,528,256]{2,1,0:T(8,128)(2,1)S(1)} %get-tuple-element.24), channel_id=1, source_target_pairs={{0,224},{32,192},{64,32},{96,0},{128,96},{160,64},{192,160},{224,1... | collective-permute-start | bytes 1622024 | tf_op jit(solution)/shard_map/ppermute | solution.py:48
  18.8 1.2 %collective-permute-start.3 = (bf16[144,256]{1,0:T(8,128)(2,1)S(1)}, bf16[144,256]{1,0:T(8,128)(2,1)S(1)}, u32[]{:S(2)}, u32[]{:S(2)}) collective-permute-start(bf16[144,256]{1,0:T(8,128)(2,1)S(1)} %pack.2.refs_0_), channel_id=1, source_target_pairs={{0,8},{1,9},{2,10},{3,11},{4,12},{5,13},{6,14},{7,15},{8,0},{9,1},... | collective-permute-start | bytes 221192 | tf_op jit(solution)/shard_map/ppermute | solution.py:53
  20.0 0.0 collective-permute-done.2.refs_1_
  20.0 0.6 collective-permute-start.10
  20.6 4.4 %collective-permute-done.3.refs_2_ = bf16[144,256]{1,0:T(8,128)(2,1)S(1)} collective-permute-done((bf16[144,256]{1,0:T(8,128)(2,1)S(1)}, bf16[144,256]{1,0:T(8,128)(2,1)S(1)}, u32[]{:S(2)}, u32[]{:S(2)}) %collective-permute-start.3) | collective-permute-done | bytes 73760 | tf_op jit(solution)/shard_map/ppermute | solution.py:53
  25.0 1.2 %collective-permute-start.4 = (bf16[144,256]{1,0:T(8,128)(2,1)S(1)}, bf16[144,256]{1,0:T(8,128)(2,1)S(1)}, u32[]{:S(2)}, u32[]{:S(2)}) collective-permute-start(bf16[144,256]{1,0:T(8,128)(2,1)S(1)} %pack.2.refs_0_), channel_id=1, source_target_pairs={{0,24},{1,25},{2,26},{3,27},{4,28},{5,29},{6,30},{7,31},{8,16},{9,... | collective-permute-start | bytes 221192 | tf_op jit(solution)/shard_map/ppermute | solution.py:53
  26.2 4.2 %collective-permute-done.4.refs_3_ = bf16[144,256]{1,0:T(8,128)(2,1)S(1)} collective-permute-done((bf16[144,256]{1,0:T(8,128)(2,1)S(1)}, bf16[144,256]{1,0:T(8,128)(2,1)S(1)}, u32[]{:S(2)}, u32[]{:S(2)}) %collective-permute-start.4) | collective-permute-done | bytes 73760 | tf_op jit(solution)/shard_map/ppermute | solution.py:53
  30.4 2.0 %collective-permute-start.6 = (bf16[2,528,256]{2,1,0:T(8,128)(2,1)S(1)}, bf16[2,528,256]{2,1,0:T(8,128)(2,1)S(1)}, u32[]{:S(2)}, u32[]{:S(2)}) collective-permute-start(bf16[2,528,256]{2,1,0:T(8,128)(2,1)S(1)} %get-tuple-element.24), channel_id=1, source_target_pairs={{0,32},{32,0},{1,33},{33,1},{2,34},{34,2},{3,35},{35,3},{4,36},{36... | collective-permute-start | bytes 1622024 | tf_op jit(solution)/shard_map/ppermute | solution.py:35
  32.5 1.3 %collective-permute-start.5 = (bf16[528,256]{1,0:T(8,128)(2,1)S(1)}, bf16[528,256]{1,0:T(8,128)(2,1)S(1)}, u32[]{:S(2)}, u32[]{:S(2)}) collective-permute-start(bf16[528,256]{1,0:T(8,128)(2,1)S(1)} %pack.3.p0), channel_id=1, source_target_pairs={{0,1},{1,0},{2,3},{3,2},{4,5},{5,4},{6,7},{7,6},{8,9},{9,8},{10,11... | collective-permute-start | bytes 811016 | tf_op jit(solution)/shard_map/ppermute | solution.py:68
  33.8 0.0 collective-permute-done.7.ol.obs
  33.8 0.0 copy-start.1
  33.8 0.2 collective-permute-start.11
  34.0 8.7 %collective-permute-done.10.wr.weights = bf16[2,512,256]{2,1,0:T(8,128)(2,1)S(1)} collective-permute-done((bf16[2,512,256]{2,1,0:T(8,128)(2,1)S(1)}, bf16[2,512,256]{2,1,0:T(8,128)(2,1)S(1)}, u32[]{:S(2)}, u32[]{:S(2)}) %collective-permute-start.10) | collective-permute-done | bytes 524320 | tf_op jit(solution)/shard_map/ppermute | solution.py:39
  42.7 2.7 %collective-permute-start.12 = (bf16[1040,256]{1,0:T(8,128)(2,1)S(1)}, bf16[1040,256]{1,0:T(8,128)(2,1)S(1)}, u32[]{:S(2)}, u32[]{:S(2)}) collective-permute-start(bf16[1040,256]{1,0:T(8,128)(2,1)S(1)} %relay.3), channel_id=1, source_target_pairs={{0,192},{64,0},{128,64},{192,128},{1,193},{65,1},{129,65},{193,129... | collective-permute-start | bytes 1597448 | tf_op jit(solution)/shard_map/ppermute | solution.py:39
  45.4 2.7 %collective-permute-start.14 = (bf16[528,256]{1,0:T(8,128)(2,1)S(1)}, bf16[528,256]{1,0:T(8,128)(2,1)S(1)}, u32[]{:S(2)}, u32[]{:S(2)}) collective-permute-start(bf16[528,256]{1,0:T(8,128)(2,1)S(1)} %pack.3.p0), channel_id=1, source_target_pairs={{0,2},{1,3},{2,0},{3,1},{4,6},{5,7},{6,4},{7,5},{8,10},{9,11},{10,... | collective-permute-start | bytes 811016 | tf_op jit(solution)/shard_map/ppermute | solution.py:68
  48.1 0.9 collective-permute-start.15
  49.0 0.3 masks.1
  49.3 4.2 %near_early.1 = (bf16[16,64,256]{2,1,0:T(8,128)(2,1)S(1)}, f32[16,64,128]{2,1,0:T(8,128)S(1)}, f32[8,128,256]{2,1,0:T(8,128)S(1)}) custom-call(f32[128,512]{1,0:T(8,128)S(1)} %masks.1, bf16[528,256]{1,0:T(8,128)(2,1)S(1)} %pack.3.p0, bf16[528,256]{1,0:T(8,128)(2,1)S(1)} %collective-permute-done.5.p1, bf16[2,528,256]{2,1,0:T(8,128)(2,1)S(1)} %collective-permute-done.6.oo, ...), custom_call_target="tpu_custom_call" | custom-call | flops 2000000000 | bytes 4000000 | tf_op jit(solution)/shard_map/near_early/pallas_call | solution.py:206
  53.5 0.5 collective-permute-done.14.p0
  54.0 7.1 %collective-permute-done.15.p1 = bf16[528,256]{1,0:T(8,128)(2,1)S(1)} collective-permute-done((bf16[528,256]{1,0:T(8,128)(2,1)S(1)}, bf16[528,256]{1,0:T(8,128)(2,1)S(1)}, u32[]{:S(2)}, u32[]{:S(2)}) %collective-permute-start.15) | collective-permute-done | bytes 270368 | tf_op jit(solution)/shard_map/ppermute | solution.py:68
  61.1 4.2 %near_late.1 = (bf16[16,64,256]{2,1,0:T(8,128)(2,1)S(1)}, f32[16,64,128]{2,1,0:T(8,128)S(1)}, f32[8,128,256]{2,1,0:T(8,128)S(1)}) custom-call(f32[128,512]{1,0:T(8,128)S(1)} %masks.1, bf16[528,256]{1,0:T(8,128)(2,1)S(1)} %collective-permute-done.14.p0, bf16[528,256]{1,0:T(8,128)(2,1)S(1)} %collective-permute-done.15.p1, ...), custom_call_target="tpu_custom_call" | custom-call | flops 2000000000 | bytes 4000000 | tf_op jit(solution)/shard_map/near_late/pallas_call | solution.py:206
  65.3 2.2 %far_late.1 = (bf16[512,256]{1,0:T(8,128)(2,1)S(1)}, bf16[512,256]{1,0:T(8,128)(2,1)S(1)}) custom-call(f32[128,512]{1,0:T(8,128)S(1)} %masks.1, bf16[16,64,256]{2,1,0:T(8,128)(2,1)S(1)} %get-tuple-element.30.state, f32[16,64,128]{2,1,0:T(8,128)S(1)} %get-tuple-element.31.spot, f32[8,128,256]{2,1,0:T(8,128)S(1)} %get-tuple-element.32.near_acc, ...), custom_call_target="tpu_custom_call" | custom-call | flops 500000000 | bytes 4000000 | tf_op jit(solution)/shard_map/far_late/pallas_call | solution.py:243
  67.5 1.1 %collective-permute-start.16 = (bf16[512,256]{1,0:T(8,128)(2,1)S(1)}, bf16[512,256]{1,0:T(8,128)(2,1)S(1)}, u32[]{:S(2)}, u32[]{:S(2)}) collective-permute-start(bf16[512,256]{1,0:T(8,128)(2,1)S(1)} %get-tuple-element.33), channel_id=1, source_target_pairs={{0,2},{1,3},{2,0},{3,1},{4,6},{5,7},{6,4},{7,5},{8,10},{9,11},{10,... | collective-permute-start | bytes 786440 | tf_op jit(solution)/shard_map/ppermute | solution.py:68
  68.6 2.6 %collective-permute-start.17 = (bf16[512,256]{1,0:T(8,128)(2,1)S(1)}, bf16[512,256]{1,0:T(8,128)(2,1)S(1)}, u32[]{:S(2)}, u32[]{:S(2)}) collective-permute-start(bf16[512,256]{1,0:T(8,128)(2,1)S(1)} %get-tuple-element.34), channel_id=1, source_target_pairs={{0,3},{1,2},{2,1},{3,0},{4,7},{5,6},{6,5},{7,4},{8,11},{9,10},{10,... | collective-permute-start | bytes 786440 | tf_op jit(solution)/shard_map/ppermute | solution.py:68
  71.2 2.2 %far_early.1 = (f32[512,256]{1,0:T(8,128)S(1)}, bf16[512,256]{1,0:T(8,128)(2,1)S(1)}) custom-call(f32[128,512]{1,0:T(8,128)S(1)} %masks.1, bf16[16,64,256]{2,1,0:T(8,128)(2,1)S(1)} %get-tuple-element.25.state, f32[16,64,128]{2,1,0:T(8,128)S(1)} %get-tuple-element.26.spot, f32[8,128,256]{2,1,0:T(8,128)S(1)} %get-tuple-element.27.near_acc, ...), custom_call_target="tpu_custom_call" | custom-call | flops 500000000 | bytes 4000000 | tf_op jit(solution)/shard_map/far_early/pallas_call | solution.py:243
  73.5 0.1 collective-permute-start.13
  73.6 3.0 %collective-permute-done.16.x2 = bf16[512,256]{1,0:T(8,128)(2,1)S(1)} collective-permute-done((bf16[512,256]{1,0:T(8,128)(2,1)S(1)}, bf16[512,256]{1,0:T(8,128)(2,1)S(1)}, u32[]{:S(2)}, u32[]{:S(2)}) %collective-permute-start.16) | collective-permute-done | bytes 262176 | tf_op jit(solution)/shard_map/ppermute | solution.py:68
  76.5 6.4 %collective-permute-done.17.x3 = bf16[512,256]{1,0:T(8,128)(2,1)S(1)} collective-permute-done((bf16[512,256]{1,0:T(8,128)(2,1)S(1)}, bf16[512,256]{1,0:T(8,128)(2,1)S(1)}, u32[]{:S(2)}, u32[]{:S(2)}) %collective-permute-start.17) | collective-permute-done | bytes 262176 | tf_op jit(solution)/shard_map/ppermute | solution.py:68
  83.0 0.1 shard_map.64
  83.1 1.3 %collective-permute-start.18 = (bf16[128,256]{1,0:T(8,128)(2,1)S(1)}, bf16[128,256]{1,0:T(8,128)(2,1)S(1)}, u32[]{:S(2)}, u32[]{:S(2)}) collective-permute-start(bf16[128,256]{1,0:T(8,128)(2,1)S(1)} %get-tuple-element.36), channel_id=1, source_target_pairs={{0,8},{1,9},{2,10},{3,11},{4,12},{5,13},{6,14},{7,15},{8,0},{9,1},... | collective-permute-start | bytes 196616 | tf_op jit(solution)/shard_map/ppermute | solution.py:53
  84.4 0.1 collective-permute-start.19
  84.5 4.3 %collective-permute-start.20 = (bf16[128,256]{1,0:T(8,128)(2,1)S(1)}, bf16[128,256]{1,0:T(8,128)(2,1)S(1)}, u32[]{:S(2)}, u32[]{:S(2)}) collective-permute-start(bf16[128,256]{1,0:T(8,128)(2,1)S(1)} %get-tuple-element.38), channel_id=1, source_target_pairs={{0,24},{1,25},{2,26},{3,27},{4,28},{5,29},{6,30},{7,31},{8,16},{9,... | collective-permute-start | bytes 196616 | tf_op jit(solution)/shard_map/ppermute | solution.py:53
  88.8 1.6 %collective-permute-done.18.z2 = bf16[128,256]{1,0:T(8,128)(2,1)S(1)} collective-permute-done((bf16[128,256]{1,0:T(8,128)(2,1)S(1)}, bf16[128,256]{1,0:T(8,128)(2,1)S(1)}, u32[]{:S(2)}, u32[]{:S(2)}) %collective-permute-start.18) | collective-permute-done | bytes 65568 | tf_op jit(solution)/shard_map/ppermute | solution.py:53
  90.4 1.6 %collective-permute-done.19.z4 = bf16[128,256]{1,0:T(8,128)(2,1)S(1)} collective-permute-done((bf16[128,256]{1,0:T(8,128)(2,1)S(1)}, bf16[128,256]{1,0:T(8,128)(2,1)S(1)}, u32[]{:S(2)}, u32[]{:S(2)}) %collective-permute-start.19) | collective-permute-done | bytes 65568 | tf_op jit(solution)/shard_map/ppermute | solution.py:53
  92.1 0.3 collective-permute-done.20.z6
  92.5 4.1 %collective-permute-start.21 = (bf16[64,256]{1,0:T(8,128)(2,1)S(1)}, bf16[64,256]{1,0:T(8,128)(2,1)S(1)}, u32[]{:S(2)}, u32[]{:S(2)}) collective-permute-start(bf16[64,256]{1,0:T(8,128)(2,1)S(1)} %get-tuple-element.40), channel_id=1, source_target_pairs={{0,4},{1,5},{2,6},{3,7},{4,0},{5,1},{6,2},{7,3},{8,12},{9,13},{10,... | collective-permute-start | bytes 98312 | tf_op jit(solution)/shard_map/ppermute | solution.py:53
  96.6 1.3 %collective-permute-done.21.other = bf16[64,256]{1,0:T(8,128)(2,1)S(1)} collective-permute-done((bf16[64,256]{1,0:T(8,128)(2,1)S(1)}, bf16[64,256]{1,0:T(8,128)(2,1)S(1)}, u32[]{:S(2)}, u32[]{:S(2)}) %collective-permute-start.21) | collective-permute-done | bytes 32800 | tf_op jit(solution)/shard_map/ppermute | solution.py:53
  97.9 0.6 shard_map.66
  (21 shorter events, 0.2 us)
Async XLA Ops:
  0.0 2.1 %copy-start.3 = (bf16[2,512]{1,0:T(2,128)(2,1)S(1)}, bf16[2,512]{1,0:T(2,128)(2,1)}, u32[]{:S(2)}) copy-start(bf16[2,512]{1,0:T(2,128)(2,1)} %obs_pos.1) | copy-start | bytes 6148
  0.0 2.1 %copy-start.4 = (bf16[64]{0:T(256)(128)(2,1)S(1)}, bf16[64]{0:T(256)(128)(2,1)}, u32[]{:S(2)}) copy-start(bf16[64]{0:T(256)(128)(2,1)} %param.7) | copy-start | bytes 388
  0.0 32.4 %collective-permute-start.8 = (bf16[2,512,256]{2,1,0:T(8,128)(2,1)}, bf16[2,512,256]{2,1,0:T(8,128)(2,1)S(1)}, u32[]{:S(2)}, u32[]{:S(2)}) collective-permute-start(bf16[2,512,256]{2,1,0:T(8,128)(2,1)} %bitcast.6), channel_id=1, source_target_pairs={{0,64},{64,128},{128,192},{192,0},{1,65},{65,129},{129,193},{193,1... | collective-permute-start | bytes 1572872 | tf_op jit(solution)/shard_map/ppermute | solution.py:39
  2.1 1.0 %copy-start = (bf16[2,1,512,256]{3,2,1,0:T(8,128)(2,1)S(1)}, bf16[2,1,512,256]{3,2,1,0:T(8,128)(2,1)}, u32[]{:S(2)}) copy-start(bf16[2,1,512,256]{3,2,1,0:T(8,128)(2,1)} %obs_in.1) | copy-start | bytes 1572868
  3.2 0.8 copy-start.2
  3.9 16.1 %copy-start.5 = (bf16[2,1,512,256]{3,2,1,0:T(8,128)(2,1)S(1)}, bf16[2,1,512,256]{3,2,1,0:T(8,128)(2,1)}, u32[]{:S(2)}) copy-start(bf16[2,1,512,256]{3,2,1,0:T(8,128)(2,1)} %param.10) | copy-start | bytes 1572868
  4.1 2.7 %collective-permute-start = (bf16[80,256]{1,0:T(8,128)(2,1)S(1)}, bf16[80,256]{1,0:T(8,128)(2,1)S(1)}, u32[]{:S(2)}, u32[]{:S(2)}) collective-permute-start(bf16[80,256]{1,0:T(8,128)(2,1)S(1)} %get-tuple-element.23), channel_id=1, source_target_pairs={{0,32},{32,0},{1,33},{33,1},{2,34},{34,2},{3,35},{35,3},{4,36},{36... | collective-permute-start | bytes 122888 | tf_op jit(solution)/shard_map/ppermute | solution.py:35
  5.9 3.7 %collective-permute-start.1 = (bf16[80,256]{1,0:T(8,128)(2,1)S(1)}, bf16[80,256]{1,0:T(8,128)(2,1)S(1)}, u32[]{:S(2)}, u32[]{:S(2)}) collective-permute-start(bf16[80,256]{1,0:T(8,128)(2,1)S(1)} %get-tuple-element.23), channel_id=1, source_target_pairs={{0,36},{1,37},{2,38},{3,39},{4,32},{5,33},{6,34},{7,35},{8,44},{9,... | collective-permute-start | bytes 122888 | tf_op jit(solution)/shard_map/ppermute | solution.py:63
  9.6 10.3 %collective-permute-start.2 = (bf16[144,256]{1,0:T(8,128)(2,1)S(1)}, bf16[144,256]{1,0:T(8,128)(2,1)S(1)}, u32[]{:S(2)}, u32[]{:S(2)}) collective-permute-start(bf16[144,256]{1,0:T(8,128)(2,1)S(1)} %pack.2.refs_0_), channel_id=1, source_target_pairs={{0,16},{1,17},{2,18},{3,19},{4,20},{5,21},{6,22},{7,23},{8,24},{9,... | collective-permute-start | bytes 221192 | tf_op jit(solution)/shard_map/ppermute | solution.py:53
  15.8 17.9 %collective-permute-start.7 = (bf16[2,528,256]{2,1,0:T(8,128)(2,1)S(1)}, bf16[2,528,256]{2,1,0:T(8,128)(2,1)S(1)}, u32[]{:S(2)}, u32[]{:S(2)}) collective-permute-start(bf16[2,528,256]{2,1,0:T(8,128)(2,1)S(1)} %get-tuple-element.24), channel_id=1, source_target_pairs={{0,96},{32,64},{64,160},{96,128},{128,224},{160,192},{192,32},{224... | collective-permute-start | bytes 1622024 | tf_op jit(solution)/shard_map/ppermute | solution.py:48
  17.1 25.6 %collective-permute-start.9 = (bf16[2,528,256]{2,1,0:T(8,128)(2,1)S(1)}, bf16[2,528,256]{2,1,0:T(8,128)(2,1)S(1)}, u32[]{:S(2)}, u32[]{:S(2)}) collective-permute-start(bf16[2,528,256]{2,1,0:T(8,128)(2,1)S(1)} %get-tuple-element.24), channel_id=1, source_target_pairs={{0,224},{32,192},{64,32},{96,0},{128,96},{160,64},{192,160},{224,1... | collective-permute-start | bytes 1622024 | tf_op jit(solution)/shard_map/ppermute | solution.py:48
  18.8 6.2 %collective-permute-start.3 = (bf16[144,256]{1,0:T(8,128)(2,1)S(1)}, bf16[144,256]{1,0:T(8,128)(2,1)S(1)}, u32[]{:S(2)}, u32[]{:S(2)}) collective-permute-start(bf16[144,256]{1,0:T(8,128)(2,1)S(1)} %pack.2.refs_0_), channel_id=1, source_target_pairs={{0,8},{1,9},{2,10},{3,11},{4,12},{5,13},{6,14},{7,15},{8,0},{9,1},... | collective-permute-start | bytes 221192 | tf_op jit(solution)/shard_map/ppermute | solution.py:53
  20.0 22.7 %collective-permute-start.10 = (bf16[2,512,256]{2,1,0:T(8,128)(2,1)S(1)}, bf16[2,512,256]{2,1,0:T(8,128)(2,1)S(1)}, u32[]{:S(2)}, u32[]{:S(2)}) collective-permute-start(bf16[2,512,256]{2,1,0:T(8,128)(2,1)S(1)} %bitcast.7), channel_id=1, source_target_pairs={{0,192},{64,0},{128,64},{192,128},{1,193},{65,1},{129,65},{193,129... | collective-permute-start | bytes 1572872 | tf_op jit(solution)/shard_map/ppermute | solution.py:39
  25.0 5.4 %collective-permute-start.4 = (bf16[144,256]{1,0:T(8,128)(2,1)S(1)}, bf16[144,256]{1,0:T(8,128)(2,1)S(1)}, u32[]{:S(2)}, u32[]{:S(2)}) collective-permute-start(bf16[144,256]{1,0:T(8,128)(2,1)S(1)} %pack.2.refs_0_), channel_id=1, source_target_pairs={{0,24},{1,25},{2,26},{3,27},{4,28},{5,29},{6,30},{7,31},{8,16},{9,... | collective-permute-start | bytes 221192 | tf_op jit(solution)/shard_map/ppermute | solution.py:53
  30.4 18.9 %collective-permute-start.6 = (bf16[2,528,256]{2,1,0:T(8,128)(2,1)S(1)}, bf16[2,528,256]{2,1,0:T(8,128)(2,1)S(1)}, u32[]{:S(2)}, u32[]{:S(2)}) collective-permute-start(bf16[2,528,256]{2,1,0:T(8,128)(2,1)S(1)} %get-tuple-element.24), channel_id=1, source_target_pairs={{0,32},{32,0},{1,33},{33,1},{2,34},{34,2},{3,35},{35,3},{4,36},{36... | collective-permute-start | bytes 1622024 | tf_op jit(solution)/shard_map/ppermute | solution.py:35
  32.5 15.7 %collective-permute-start.5 = (bf16[528,256]{1,0:T(8,128)(2,1)S(1)}, bf16[528,256]{1,0:T(8,128)(2,1)S(1)}, u32[]{:S(2)}, u32[]{:S(2)}) collective-permute-start(bf16[528,256]{1,0:T(8,128)(2,1)S(1)} %pack.3.p0), channel_id=1, source_target_pairs={{0,1},{1,0},{2,3},{3,2},{4,5},{5,4},{6,7},{7,6},{8,9},{9,8},{10,11... | collective-permute-start | bytes 811016 | tf_op jit(solution)/shard_map/ppermute | solution.py:68
  33.8 15.2 %copy-start.1 = (s32[2,512,16]{1,2,0:T(8,128)S(1)}, s32[2,512,16]{1,2,0:T(8,128)}, u32[]{:S(2)}) copy-start(s32[2,512,16]{1,2,0:T(8,128)} %param.11) | copy-start | bytes 196612
  33.8 31.5 %collective-permute-start.11 = (bf16[1040,256]{1,0:T(8,128)(2,1)S(1)}, bf16[1040,256]{1,0:T(8,128)(2,1)S(1)}, u32[]{:S(2)}, u32[]{:S(2)}) collective-permute-start(bf16[1040,256]{1,0:T(8,128)(2,1)S(1)} %relay.2), channel_id=1, source_target_pairs={{0,64},{64,128},{128,192},{192,0},{1,65},{65,129},{129,193},{193,1... | collective-permute-start | bytes 1597448 | tf_op jit(solution)/shard_map/ppermute | solution.py:39
  42.7 22.6 %collective-permute-start.12 = (bf16[1040,256]{1,0:T(8,128)(2,1)S(1)}, bf16[1040,256]{1,0:T(8,128)(2,1)S(1)}, u32[]{:S(2)}, u32[]{:S(2)}) collective-permute-start(bf16[1040,256]{1,0:T(8,128)(2,1)S(1)} %relay.3), channel_id=1, source_target_pairs={{0,192},{64,0},{128,64},{192,128},{1,193},{65,1},{129,65},{193,129... | collective-permute-start | bytes 1597448 | tf_op jit(solution)/shard_map/ppermute | solution.py:39
  45.4 8.6 %collective-permute-start.14 = (bf16[528,256]{1,0:T(8,128)(2,1)S(1)}, bf16[528,256]{1,0:T(8,128)(2,1)S(1)}, u32[]{:S(2)}, u32[]{:S(2)}) collective-permute-start(bf16[528,256]{1,0:T(8,128)(2,1)S(1)} %pack.3.p0), channel_id=1, source_target_pairs={{0,2},{1,3},{2,0},{3,1},{4,6},{5,7},{6,4},{7,5},{8,10},{9,11},{10,... | collective-permute-start | bytes 811016 | tf_op jit(solution)/shard_map/ppermute | solution.py:68
  48.1 13.0 %collective-permute-start.15 = (bf16[528,256]{1,0:T(8,128)(2,1)S(1)}, bf16[528,256]{1,0:T(8,128)(2,1)S(1)}, u32[]{:S(2)}, u32[]{:S(2)}) collective-permute-start(bf16[528,256]{1,0:T(8,128)(2,1)S(1)} %pack.3.p0), channel_id=1, source_target_pairs={{0,3},{1,2},{2,1},{3,0},{4,7},{5,6},{6,5},{7,4},{8,11},{9,10},{10,... | collective-permute-start | bytes 811016 | tf_op jit(solution)/shard_map/ppermute | solution.py:68
  67.5 9.0 %collective-permute-start.16 = (bf16[512,256]{1,0:T(8,128)(2,1)S(1)}, bf16[512,256]{1,0:T(8,128)(2,1)S(1)}, u32[]{:S(2)}, u32[]{:S(2)}) collective-permute-start(bf16[512,256]{1,0:T(8,128)(2,1)S(1)} %get-tuple-element.33), channel_id=1, source_target_pairs={{0,2},{1,3},{2,0},{3,1},{4,6},{5,7},{6,4},{7,5},{8,10},{9,11},{10,... | collective-permute-start | bytes 786440 | tf_op jit(solution)/shard_map/ppermute | solution.py:68
  68.6 14.3 %collective-permute-start.17 = (bf16[512,256]{1,0:T(8,128)(2,1)S(1)}, bf16[512,256]{1,0:T(8,128)(2,1)S(1)}, u32[]{:S(2)}, u32[]{:S(2)}) collective-permute-start(bf16[512,256]{1,0:T(8,128)(2,1)S(1)} %get-tuple-element.34), channel_id=1, source_target_pairs={{0,3},{1,2},{2,1},{3,0},{4,7},{5,6},{6,5},{7,4},{8,11},{9,10},{10,... | collective-permute-start | bytes 786440 | tf_op jit(solution)/shard_map/ppermute | solution.py:68
  73.5 9.5 %collective-permute-start.13 = (bf16[512,256]{1,0:T(8,128)(2,1)S(1)}, bf16[512,256]{1,0:T(8,128)(2,1)S(1)}, u32[]{:S(2)}, u32[]{:S(2)}) collective-permute-start(bf16[512,256]{1,0:T(8,128)(2,1)S(1)} %get-tuple-element.29), channel_id=1, source_target_pairs={{0,1},{1,0},{2,3},{3,2},{4,5},{5,4},{6,7},{7,6},{8,9},{9,8},{10,11... | collective-permute-start | bytes 786440 | tf_op jit(solution)/shard_map/ppermute | solution.py:68
  83.1 7.4 %collective-permute-start.18 = (bf16[128,256]{1,0:T(8,128)(2,1)S(1)}, bf16[128,256]{1,0:T(8,128)(2,1)S(1)}, u32[]{:S(2)}, u32[]{:S(2)}) collective-permute-start(bf16[128,256]{1,0:T(8,128)(2,1)S(1)} %get-tuple-element.36), channel_id=1, source_target_pairs={{0,8},{1,9},{2,10},{3,11},{4,12},{5,13},{6,14},{7,15},{8,0},{9,1},... | collective-permute-start | bytes 196616 | tf_op jit(solution)/shard_map/ppermute | solution.py:53
  84.4 7.7 %collective-permute-start.19 = (bf16[128,256]{1,0:T(8,128)(2,1)S(1)}, bf16[128,256]{1,0:T(8,128)(2,1)S(1)}, u32[]{:S(2)}, u32[]{:S(2)}) collective-permute-start(bf16[128,256]{1,0:T(8,128)(2,1)S(1)} %get-tuple-element.37), channel_id=1, source_target_pairs={{0,16},{1,17},{2,18},{3,19},{4,20},{5,21},{6,22},{7,23},{8,24},{9,... | collective-permute-start | bytes 196616 | tf_op jit(solution)/shard_map/ppermute | solution.py:53
  84.5 7.9 %collective-permute-start.20 = (bf16[128,256]{1,0:T(8,128)(2,1)S(1)}, bf16[128,256]{1,0:T(8,128)(2,1)S(1)}, u32[]{:S(2)}, u32[]{:S(2)}) collective-permute-start(bf16[128,256]{1,0:T(8,128)(2,1)S(1)} %get-tuple-element.38), channel_id=1, source_target_pairs={{0,24},{1,25},{2,26},{3,27},{4,28},{5,29},{6,30},{7,31},{8,16},{9,... | collective-permute-start | bytes 196616 | tf_op jit(solution)/shard_map/ppermute | solution.py:53
  92.5 5.4 %collective-permute-start.21 = (bf16[64,256]{1,0:T(8,128)(2,1)S(1)}, bf16[64,256]{1,0:T(8,128)(2,1)S(1)}, u32[]{:S(2)}, u32[]{:S(2)}) collective-permute-start(bf16[64,256]{1,0:T(8,128)(2,1)S(1)} %get-tuple-element.40), channel_id=1, source_target_pairs={{0,4},{1,5},{2,6},{3,7},{4,0},{5,1},{6,2},{7,3},{8,12},{9,13},{10,... | collective-permute-start | bytes 98312 | tf_op jit(solution)/shard_map/ppermute | solution.py:53
